TPU v7x, 32 devices: a whole 2x2x4 slice. The times are simulated.
32 devices in a mesh: seq: 8 (over y, x, core), chan: 4 (over z).
Axes of the slice: x: 2, y: 2, z: 4, core: 2. Of those that a mesh axis runs over, the one named last changes fastest.
Arguments:
- hidden: bfloat16 [4096, 4096], P('seq', 'chan'), may hold values from -6 to 6
- norm_gain: float32 [2048], replicated, may hold values from 0.25 to 1.75
- w_values: bfloat16 [2048, 4096], P(None, 'chan'), may hold values from -0.125 to 0.125
- w_gates: bfloat16 [2048, 4096], P(None, 'chan'), may hold values from -0.125 to 0.125
- w_control: bfloat16 [2048, 320], replicated, may hold values from -0.046875 to 0.046875
- dt_bias: float32 [64], replicated, may hold values from -1 to 1
- decay_total: float32 [64], replicated, may hold values from 0 to 137
- skip_gain: float32 [64], replicated, may hold values from 0.5 to 2
- gate_gain: float32 [4096], P('chan'), may hold values from 0.25 to 1.75
- w_out: bfloat16 [4096, 2048], P('chan'), may hold values from -0.125 to 0.125
- doc_starts: int32 [4], replicated, may hold values from 0 to 3328, as said below
Outputs:
- layer_out: bfloat16 [4096, 4096], P('seq', 'chan')
Inputs may be any that keep to these rules, and one draw needn't show every extreme that they name: doc_starts[0] is 0 and the offsets rise strictly; document k runs from doc_starts[k] up to the next offset or the window's end.
All inputs are finite; a program needn't handle non-finite values.
Results may differ from a plain program's by a relative error of at most 0.013.
Values may be sent and summed in bfloat16 or wider, within the bound.
No kernel may reach another device: no remote copies, remote signals or barrier semaphores. Data moves between devices by JAX's collectives and lax.ppermute only.
A program may use at most 128 MiB of HBM per device.

v0:
```python
import functools

import jax
import jax.numpy as jnp
from jax import lax
from jax.experimental import pallas as pl
from jax.experimental.pallas import tpu as pltpu
from jax.sharding import PartitionSpec as P

HEAD_DIM = 64
STATE = 128
CHUNK = 128
LANES = 128
REV = 256
KEEP_ROWS = 16

norm_eps = 1e-05
highest = lax.Precision.HIGHEST
f32 = jnp.float32
bf16 = jnp.bfloat16


def mm(a, b):
    return jnp.dot(a, b, preferred_element_type=f32)


def mm_nt(a, b):
    return lax.dot_general(a, b, (((1,), (1,)), ((), ())), preferred_element_type=f32)


def mm_tn(a, b):
    return lax.dot_general(a, b, (((0,), (0,)), ((), ())), preferred_element_type=f32)


def iota(shape, dim):
    return lax.broadcasted_iota(jnp.int32, shape, dim)


def exchange_matrix(mirror):
    row, col = iota((REV, REV), 0), iota((REV, REV), 1)
    return (row == jnp.where(mirror == 1, REV - 1 - col, col)).astype(f32).astype(bf16)


def segment_of(position, starts_ref):
    total = jnp.zeros_like(position)
    for k in range(starts_ref.shape[0]):
        total = total + (position >= starts_ref[k]).astype(jnp.int32)
    return total


def expander(width):
    row, col = iota((2 * LANES, width), 0), iota((2 * LANES, width), 1)
    return ((row % LANES) == (col // HEAD_DIM)).astype(f32).astype(bf16)


def expand(w, spread):
    high = w.astype(bf16)
    low = (w - high.astype(f32)).astype(bf16)
    return mm(jnp.concatenate([high, low], axis=1), spread)


def full(shape):
    return pl.BlockSpec(shape, lambda *_: (0,) * len(shape))


SMEM = pl.BlockSpec(memory_space=pltpu.SMEM)


def norm_project_kernel(pieces, mirror_ref, *refs):
    xs = refs[:pieces]
    gain_ref, wv_ref, wc_ref, normed_ref, values_ref, control_ref, scr = refs[pieces:]
    half = normed_ref.shape[1]
    blocks = half // REV

    @pl.when(pl.program_id(0) == 0)
    def _():
        mirror = mirror_ref[0]
        swap = exchange_matrix(mirror)
        squares = jnp.zeros((normed_ref.shape[0], 1), f32)
        at = 0
        for x_ref in xs:
            for q in range(x_ref.shape[1] // REV):
                xb = x_ref[:, q * REV : (q + 1) * REV]
                wide = xb.astype(f32)
                squares = squares + jnp.sum(wide * wide, axis=1, keepdims=True)
                scr[jnp.where(mirror == 1, blocks - 1 - at, at)] = mm(xb, swap).astype(bf16)
                at += 1
        scale = lax.rsqrt(squares / half + norm_eps)
        for q in range(blocks):
            cols = slice(q * REV, (q + 1) * REV)
            normed_ref[:, cols] = (scr[q].astype(f32) * scale * gain_ref[:, cols]).astype(bf16)
        control_ref[...] = mm(normed_ref[...], wc_ref[...]).astype(bf16)

    values_ref[...] = mm(normed_ref[...], wv_ref[...]).astype(bf16)


def norm_project(xs, mirror, gain, w_values, w_control):
    tokens = xs[0].shape[0]
    half, cols = w_values.shape
    tile = min(256, cols)
    return pl.pallas_call(
        functools.partial(norm_project_kernel, len(xs)),
        grid=(cols // tile,),
        in_specs=[SMEM]
        + [full(x.shape) for x in xs]
        + [full(gain.shape), pl.BlockSpec((half, tile), lambda j: (0, j)), full(w_control.shape)],
        out_specs=[
            full((tokens, half)),
            pl.BlockSpec((tokens, tile), lambda j: (0, j)),
            full((tokens, w_control.shape[1])),
        ],
        out_shape=[
            jax.ShapeDtypeStruct((tokens, half), bf16),
            jax.ShapeDtypeStruct((tokens, cols), bf16),
            jax.ShapeDtypeStruct((tokens, w_control.shape[1]), bf16),
        ],
        scratch_shapes=[pltpu.VMEM((half // REV, tokens, REV), bf16)],
        name="norm_project",
    )(mirror, *xs, gain, w_values, w_control)


def states_kernel(
    starts_ref, base_ref, control_ref, values_ref, par_ref,
    total_ref, pre_ref, cola_ref, colb_ref, rowf_ref, rowb_ref, reach_ref,
):
    tokens, cols = values_ref.shape
    chunks = tokens // CHUNK
    heads = cols // HEAD_DIM
    base = base_ref[0]
    spread = expander(cols)
    row, col = iota((CHUNK, CHUNK), 0), iota((CHUNK, CHUNK), 1)
    tri = (row >= col).astype(f32)
    seg_at = lambda offset: segment_of(base + jnp.full((1, 1), offset, jnp.int32), starts_ref)
    pieces = []
    for k in range(chunks):
        rows = slice(k * CHUNK, (k + 1) * CHUNK)
        raw = control_ref[rows, 2 * STATE :].astype(f32) + par_ref[0:1, :]
        step = jnp.maximum(raw, 0.0) + jnp.log1p(jnp.exp(-jnp.abs(raw)))
        log_step = jnp.log(step)
        log_rate = -par_ref[1:2, :] * step
        cum = jnp.dot(tri, log_rate, precision=highest, preferred_element_type=f32)
        before = cum - log_rate
        whole = cum[CHUNK - 1 : CHUNK, :]
        cola_ref[rows, :] = cum
        colb_ref[rows, :] = before
        rowf_ref[k] = jnp.transpose(cum - log_step)[:heads]
        rowb_ref[k] = jnp.transpose(before + log_step)[:heads]
        seg = segment_of(base + k * CHUNK + iota((CHUNK, 1), 0), starts_ref)
        first, last = seg_at(k * CHUNK), seg_at((k + 1) * CHUNK - 1)
        prior, after = seg_at(k * CHUNK - 1), seg_at((k + 1) * CHUNK)
        w_f = jnp.where(seg == last, step * jnp.exp(whole - cum), 0.0)
        w_b = jnp.where(seg == first, step * jnp.exp(before), 0.0)
        b_in = control_ref[rows, :STATE]
        wide = values_ref[rows, :].astype(f32)
        add_f = mm_tn(b_in, (wide * expand(w_f, spread)).astype(bf16))
        add_b = mm_tn(b_in, (wide * expand(w_b, spread)).astype(bf16))
        keep = jnp.exp(whole)
        keep_f = jnp.where(prior == last, keep, 0.0)
        keep_b = jnp.where(first == after, keep, 0.0)
        pieces.append((seg, cum, before, whole, add_f, add_b, keep_f, keep_b))
    lift = lambda w: expand(jnp.broadcast_to(w, (8, LANES)), spread)[0:1]
    for d, order in enumerate((range(chunks), range(chunks - 1, -1, -1))):
        state = jnp.zeros((STATE, cols), f32)
        keep_all = jnp.ones((1, LANES), f32)
        shift = jnp.zeros((1, LANES), f32)
        edge = seg_at(-1) if d == 0 else seg_at(tokens)
        for k in order:
            seg, cum, before, whole, add_f, add_b, keep_f, keep_b = pieces[k]
            pre_ref[d, k] = state.astype(bf16)
            add, keep = (add_f, keep_f) if d == 0 else (add_b, keep_b)
            inner = cum if d == 0 else whole - before
            reach_ref[d, k * CHUNK : (k + 1) * CHUNK, :] = jnp.where(
                seg == edge, jnp.exp(inner + shift), 0.0
            )
            state = lift(keep) * state + add
            keep_all = keep_all * keep
            shift = shift + whole
        total_ref[d, :STATE] = state.astype(bf16)
        total_ref[d, STATE:] = jnp.broadcast_to(lift(keep_all), (KEEP_ROWS, cols)).astype(bf16)


def chunk_states(starts, base, control, values, par):
    tokens, cols = values.shape
    chunks, heads = tokens // CHUNK, cols // HEAD_DIM
    shapes = [
        ((2, STATE + KEEP_ROWS, cols), bf16),
        ((2, chunks, STATE, cols), bf16),
        ((tokens, LANES), f32),
        ((tokens, LANES), f32),
        ((chunks, heads, CHUNK), f32),
        ((chunks, heads, CHUNK), f32),
        ((2, tokens, LANES), f32),
    ]
    return pl.pallas_call(
        states_kernel,
        grid=(1,),
        in_specs=[SMEM, SMEM, full(control.shape), full(values.shape), full(par.shape)],
        out_specs=[full(s) for s, _ in shapes],
        out_shape=[jax.ShapeDtypeStruct(s, t) for s, t in shapes],
        name="chunk_states",
    )(starts, base, control, values, par)


def within_kernel(
    starts_ref, base_ref, control_ref, values_ref, skip_ref,
    pre_ref, cola_ref, colb_ref, rowf_ref, rowb_ref, out_ref,
):
    cols = values_ref.shape[1]
    k = pl.program_id(0)
    start = base_ref[0] + k * CHUNK
    spread = expander(cols)
    row, col = iota((CHUNK, CHUNK), 0), iota((CHUNK, CHUNK), 1)
    low_lanes = iota((CHUNK, LANES), 1) < HEAD_DIM
    b_in, c_out = control_ref[:, :STATE], control_ref[:, STATE : 2 * STATE]
    seg_col = segment_of(start + iota((CHUNK, 1), 0), starts_ref)
    seg_row = segment_of(start + iota((1, CHUNK), 1), starts_ref)
    prior = segment_of(jnp.full((1, 1), start - 1, jnp.int32), starts_ref)
    after = segment_of(jnp.full((1, 1), start + CHUNK, jnp.int32), starts_ref)
    same = seg_col == seg_row
    lower = row >= col
    scores = mm_nt(c_out, b_in)
    scores_f = jnp.where(lower & same, scores, 0.0)
    scores_b = jnp.where((row <= col) & same, scores, 0.0)
    cum, before = cola_ref[...], colb_ref[...]
    whole = cum[CHUNK - 1 : CHUNK, :]
    far_f = expand(jnp.where(seg_col == prior, jnp.exp(cum), 0.0), spread)
    far_b = expand(jnp.where(seg_col == after, jnp.exp(whole - before), 0.0), spread)
    carry_f = mm(c_out, pre_ref[0, 0]) * far_f
    carry_b = mm(c_out, pre_ref[1, 0]) * far_b
    per_tile = LANES // HEAD_DIM
    for pair in range(cols // LANES):
        lanes = slice(pair * LANES, (pair + 1) * LANES)
        value = values_ref[:, lanes]
        left_f, left_b = [], []
        for h in range(pair * per_tile, (pair + 1) * per_tile):
            gap = jnp.where(
                lower,
                cum[:, h : h + 1] - rowf_ref[0, h : h + 1, :],
                rowb_ref[0, h : h + 1, :] - before[:, h : h + 1],
            )
            weight = jnp.exp(gap)
            left_f.append((weight * scores_f).astype(bf16))
            left_b.append((weight * scores_b).astype(bf16))
        left = jnp.concatenate(
            [jnp.concatenate(left_f, axis=1), jnp.concatenate(left_b, axis=1)], axis=0
        )
        zero = jnp.zeros_like(value)
        right = jnp.concatenate(
            [jnp.where(low_lanes, value, zero), jnp.where(low_lanes, zero, value)], axis=0
        )
        near = mm(left, right)
        direct = value.astype(f32) * skip_ref[:, lanes]
        out_ref[0, :, lanes] = near[:CHUNK] + carry_f[:, lanes] + direct
        out_ref[1, :, lanes] = near[CHUNK:] + carry_b[:, lanes] + direct


def within(starts, base, control, values, skip_row, pre, cola, colb, rowf, rowb):
    tokens, cols = values.shape
    chunks, heads = tokens // CHUNK, cols // HEAD_DIM
    rows = lambda width: pl.BlockSpec((CHUNK, width), lambda k: (k, 0))
    return pl.pallas_call(
        within_kernel,
        grid=(chunks,),
        in_specs=[
            SMEM, SMEM,
            rows(control.shape[1]), rows(cols), full(skip_row.shape),
            pl.BlockSpec((2, 1, STATE, cols), lambda k: (0, k, 0, 0)),
            rows(LANES), rows(LANES),
            pl.BlockSpec((1, heads, CHUNK), lambda k: (k, 0, 0)),
            pl.BlockSpec((1, heads, CHUNK), lambda k: (k, 0, 0)),
        ],
        out_specs=pl.BlockSpec((2, CHUNK, cols), lambda k: (0, k, 0)),
        out_shape=jax.ShapeDtypeStruct((2, tokens, cols), f32),
        name="within_chunk",
    )(starts, base, control, values, skip_row, pre, cola, colb, rowf, rowb)


def gate_kernel(control_ref, near_ref, into_ref, reach_ref, gates_ref, out_ref, squares_ref):
    cols = gates_ref.shape[1]
    spread = expander(cols)
    c_out = control_ref[:, STATE : 2 * STATE]
    gate = gates_ref[...].astype(f32)
    active = gate * jax.nn.sigmoid(gate)
    lane = iota((CHUNK, LANES), 1)
    squares = jnp.zeros((CHUNK, LANES), f32)
    for d in range(2):
        carry = mm(c_out, into_ref[d]) * expand(reach_ref[d], spread)
        y = (near_ref[d] + carry).astype(bf16).astype(f32)
        v = y * active
        squares = jnp.where(lane == d, jnp.sum(v * v, axis=1, keepdims=True), squares)
        out_ref[d] = v.astype(bf16)
    squares_ref[...] = jnp.transpose(squares)[:8]


def carry_gate(control, near, into, reach, gates):
    tokens, cols = gates.shape
    rows = lambda width: pl.BlockSpec((CHUNK, width), lambda k: (k, 0))
    both = lambda width: pl.BlockSpec((2, CHUNK, width), lambda k: (0, k, 0))
    return pl.pallas_call(
        gate_kernel,
        grid=(tokens // CHUNK,),
        in_specs=[rows(control.shape[1]), both(cols), full(into.shape), both(LANES), rows(cols)],
        out_specs=[both(cols), pl.BlockSpec((8, CHUNK), lambda k: (0, k))],
        out_shape=[
            jax.ShapeDtypeStruct((2, tokens, cols), bf16),
            jax.ShapeDtypeStruct((8, tokens), f32),
        ],
        name="carry_gate",
    )(control, near, into, reach, gates)


def output_kernel(inner, sums, mirror_ref, gated_ref, *refs):
    squares_refs = refs[:sums]
    gain_ref, w_ref, out_ref = refs[sums:]
    squares = squares_refs[0][...]
    for other in squares_refs[1:]:
        squares = squares + other[...]
    scale = lax.rsqrt(squares / inner + norm_eps)
    scale = jnp.transpose(jnp.concatenate([scale, jnp.zeros((CHUNK - 8, CHUNK), f32)], axis=0))
    gain = gain_ref[...]
    combined = (
        gated_ref[0].astype(f32) * scale[:, 0:1] * gain
        + gated_ref[1].astype(f32) * scale[:, 1:2] * gain
    ).astype(bf16)
    product = mm(combined, w_ref[...]).astype(bf16)
    width = product.shape[1]
    blocks = width // REV

    @pl.when(mirror_ref[0] == 0)
    def _():
        out_ref[...] = product

    @pl.when(mirror_ref[0] == 1)
    def _():
        swap = exchange_matrix(jnp.int32(1))
        for q in range(blocks):
            back = blocks - 1 - q
            out_ref[:, back * REV : (back + 1) * REV] = mm(
                product[:, q * REV : (q + 1) * REV], swap
            ).astype(bf16)


def output_project(inner, mirror, gated, squares, gain_row, w_out):
    _, tokens, cols = gated.shape
    width = w_out.shape[1]
    return pl.pallas_call(
        functools.partial(output_kernel, inner, len(squares)),
        grid=(tokens // CHUNK,),
        in_specs=[SMEM, pl.BlockSpec((2, CHUNK, cols), lambda k: (0, k, 0))]
        + [pl.BlockSpec((8, CHUNK), lambda k: (0, k)) for _ in squares]
        + [full(gain_row.shape), full(w_out.shape)],
        out_specs=pl.BlockSpec((CHUNK, width), lambda k: (k, 0)),
        out_shape=jax.ShapeDtypeStruct((tokens, width), bf16),
        name="output_project",
    )(mirror, gated, *squares, gain_row, w_out)


def incoming_states(total):
    count = lax.axis_size("seq")
    place = lax.axis_index("seq")
    group = total
    into = [jnp.zeros(total.shape[1:], f32)] * 2
    into_keep = [jnp.ones((1, total.shape[2]), f32)] * 2
    stride = 1
    while stride < count:
        got = lax.ppermute(group, "seq", [(i, i ^ stride) for i in range(count)]).astype(f32)
        mine = group.astype(f32)
        upper = (place // stride) % 2 == 1
        merged = []
        for d in range(2):
            after_got = upper if d == 0 else jnp.logical_not(upper)
            got_keep, my_keep = got[d, STATE : STATE + 1], mine[d, STATE : STATE + 1]
            into[d] = jnp.where(after_got, into_keep[d] * got[d] + into[d], into[d])
            into_keep[d] = jnp.where(after_got, into_keep[d] * got_keep, into_keep[d])
            late, early = jnp.where(after_got, mine[d], got[d]), jnp.where(after_got, got[d], mine[d])
            late_keep = jnp.where(after_got, my_keep, got_keep)
            states = late_keep * early[:STATE] + late[:STATE]
            merged.append(jnp.concatenate([states, early[STATE:] * late[STATE:]], axis=0))
        group = jnp.stack(merged).astype(bf16)
        stride *= 2
    return jnp.stack([into[0][:STATE], into[1][:STATE]]).astype(bf16)


def chan_parts(part):
    count = lax.axis_size("chan")
    others = [
        lax.ppermute(part, "chan", [(i, (i + k) % count) for i in range(count)])
        for k in range(1, count)
    ]
    return [part] + others


def local(
    hidden, norm_gain, w_values, w_gates, w_control, dt_bias, decay_total, skip_gain, gate_gain,
    w_out, doc_starts,
):
    seq_count, chan_count = lax.axis_size("seq"), lax.axis_size("chan")
    seq_rank, chan_rank = lax.axis_index("seq"), lax.axis_index("chan")
    tokens = hidden.shape[0]
    half = norm_gain.shape[0]
    cols = w_values.shape[1]
    heads = cols // HEAD_DIM
    mine = lambda a, axis: lax.dynamic_slice_in_dim(a, chan_rank * heads, heads, axis)
    lanes = lambda a: jnp.pad(a, ((0, 0), (0, LANES - heads)))
    w_steps = lanes(mine(w_control[:, 2 * STATE :], 1))
    w_small = jnp.concatenate([w_control[:, : 2 * STATE], w_steps], axis=1)
    par = lanes(jnp.stack([mine(dt_bias, 0), mine(decay_total, 0) / (tokens * seq_count)]))
    par = jnp.pad(par, ((0, 6), (0, 0)))
    skip_row = jnp.repeat(mine(skip_gain, 0), HEAD_DIM)[None]
    gain_row, gate_row = norm_gain[None], gate_gain[None]
    base = jnp.reshape(seq_rank * tokens, (1,)).astype(jnp.int32)
    whole = lax.all_gather(hidden, "chan", axis=1, tiled=True)
    parts = []
    for strand in range(2):
        mirror = jnp.full((1,), strand, jnp.int32)
        x = whole[:, strand * half : (strand + 1) * half]
        normed, values, control = norm_project([x], mirror, gain_row, w_values, w_small)
        total, pre, cola, colb, rowf, rowb, reach = chunk_states(
            doc_starts, base, control, values, par
        )
        into = incoming_states(total)
        gates = mm(normed, w_gates).astype(bf16)
        near = within(doc_starts, base, control, values, skip_row, pre, cola, colb, rowf, rowb)
        gated, squares = carry_gate(control, near, into, reach, gates)
        parts.append(
            output_project(
                cols * chan_count, mirror, gated, chan_parts(squares), gate_row, w_out
            )
        )
    partial_value = jnp.concatenate(parts, axis=1)
    return lax.psum_scatter(partial_value, "chan", scatter_dimension=1, tiled=True)


def solution(mesh):
    in_specs = (
        P("seq", "chan"), P(), P(None, "chan"), P(None, "chan"), P(), P(), P(), P(), P("chan"),
        P("chan", None), P(),
    )
    return jax.shard_map(
        local, mesh=mesh, in_specs=in_specs, out_specs=P("seq", "chan"), check_vma=False
    )
```

profile of v0, /device:TPU:0, one launch (start us, length us, event | category | flops | bytes accessed | tf_op | source)
XLA Modules:
  0.0 315.9 jit_solution(1843197836235761916)
XLA Ops:
  6.5 0.7 all-gather.2.cloned.1.call-update
  9.8 1.3 fusion.1.refs_3_
  11.1 81.3 %all-gather.2.cloned.1.call-done = bf16[512,4096]{1,0:T(8,128)(2,1)} async-done(((bf16[512,1024]{1,0:T(8,128)(2,1)}), bf16[512,4096]{1,0:T(8,128)(2,1)}) %all-gather.2.cloned.1.call-update) | async-done | bytes 4194320 | tf_op jit(solution)/shard_map/all_gather | solution.py:412
  92.4 4.8 %fusion.48 = (bf16[512,2048]{1,0:T(8,128)(2,1)}, bf16[512,2048]{1,0:T(8,128)(2,1)}) fusion(bf16[512,4096]{1,0:T(8,128)(2,1)} %all-gather.2.cloned.1.call-done), kind=kLoop, calls=%fused_computation.150 | loop fusion | bytes 8388608 | tf_op jit(solution)/shard_map/slice | solution.py:416
  97.2 9.0 %norm_project.3 = (bf16[512,2048]{1,0:T(8,128)(2,1)}, bf16[512,1024]{1,0:T(8,128)(2,1)}, bf16[512,384]{1,0:T(8,128)(2,1)}) custom-call(s32[1]{0:T(128)} %constant.92.clone.1.mirror_ref, bf16[512,2048]{1,0:T(8,128)(2,1)} %get-tuple-element.54.refs_0_, f32[1,2048]{1,0:T(1,128)} %bitcast.179, bf16[2048,1024]{1,0:T(8,128)(2,1)} %refs_2_.3, ...), custom_call_target="tpu_custom_call" | custom-call | tf_op jit(solution)/shard_map/norm_project/pallas_call | solution.py:101
  106.3 7.0 %chunk_states.3 = (bf16[2,144,1024]{2,1,0:T(8,128)(2,1)}, bf16[2,4,128,1024]{3,2,1,0:T(8,128)(2,1)}, f32[512,128]{1,0:T(8,128)}, f32[512,128]{1,0:T(8,128)}, f32...) custom-call(s32[4]{0:T(128)} %starts_ref.7, s32[1]{0:T(128)} %bitcast.1.base_ref, ...), custom_call_target="tpu_custom_call" | custom-call | tf_op jit(solution)/shard_map/chunk_states/pallas_call | solution.py:194
  113.3 9.1 %norm_project.2 = (bf16[512,2048]{1,0:T(8,128)(2,1)}, bf16[512,1024]{1,0:T(8,128)(2,1)}, bf16[512,384]{1,0:T(8,128)(2,1)}) custom-call(s32[1]{0:T(128)} %constant.76.clone.1.mirror_ref, bf16[512,2048]{1,0:T(8,128)(2,1)} %get-tuple-element.53.refs_0_, f32[1,2048]{1,0:T(1,128)} %bitcast.180, bf16[2048,1024]{1,0:T(8,128)(2,1)} %refs_2_.3, ...), custom_call_target="tpu_custom_call" | custom-call | tf_op jit(solution)/shard_map/norm_project/pallas_call | solution.py:101
  122.4 7.0 %chunk_states.2 = (bf16[2,144,1024]{2,1,0:T(8,128)(2,1)}, bf16[2,4,128,1024]{3,2,1,0:T(8,128)(2,1)}, f32[512,128]{1,0:T(8,128)}, f32[512,128]{1,0:T(8,128)}, f32...) custom-call(s32[4]{0:T(128)} %starts_ref.7, s32[1]{0:T(128)} %bitcast.1.base_ref, ...), custom_call_target="tpu_custom_call" | custom-call | tf_op jit(solution)/shard_map/chunk_states/pallas_call | solution.py:194
  129.9 6.3 %convolution_convert_fusion.1.gates_ref = bf16[512,1024]{1,0:T(8,128)(2,1)} fusion(bf16[512,2048]{1,0:T(8,128)(2,1)} %get-tuple-element.38, bf16[2048,1024]{1,0:T(8,128)(2,1)} %param.14), kind=kOutput, calls=%fused_computation.5 | convolution fusion | flops 2148007936 | bytes 7340032 | tf_op jit(solution)/shard_map/dot_general | solution.py:24
  136.1 3.3 %convolution_convert_fusion.gates_ref = bf16[512,1024]{1,0:T(8,128)(2,1)} fusion(bf16[512,2048]{1,0:T(8,128)(2,1)S(1)} %copy-done.9, bf16[2048,1024]{1,0:T(8,128)(2,1)S(1)} %copy-done.8), kind=kOutput, calls=%fused_computation.4 | convolution fusion | flops 2148007936 | bytes 7340032 | tf_op jit(solution)/shard_map/dot_general | solution.py:24
  139.6 0.9 copy-done.1
  140.7 7.0 %within_chunk.3.near_ref = f32[2,512,1024]{2,1,0:T(8,128)} custom-call(s32[4]{0:T(128)} %starts_ref.7, s32[1]{0:T(128)} %bitcast.1.base_ref, bf16[512,384]{1,0:T(8,128)(2,1)} %get-tuple-element.41.control_ref, bf16[512,1024]{1,0:T(8,128)(2,1)} %get-tuple-element.42.values_ref, f32[1,1024]{1,0:T(1,128)} %broadcast_in_dim_reshape.3.skip_ref, ...), custom_call_target="tpu_custom_call" | custom-call | tf_op jit(solution)/shard_map/within_chunk/pallas_call | solution.py:261
  147.7 6.9 %within_chunk.2.near_ref = f32[2,512,1024]{2,1,0:T(8,128)} custom-call(s32[4]{0:T(128)} %starts_ref.7, s32[1]{0:T(128)} %bitcast.1.base_ref, bf16[512,384]{1,0:T(8,128)(2,1)} %get-tuple-element.29.control_ref, bf16[512,1024]{1,0:T(8,128)(2,1)} %get-tuple-element.30.values_ref, f32[1,1024]{1,0:T(1,128)} %broadcast_in_dim_reshape.3.skip_ref, ...), custom_call_target="tpu_custom_call" | custom-call | tf_op jit(solution)/shard_map/within_chunk/pallas_call | solution.py:261
  154.6 1.2 convert_element_type.54
  156.3 1.2 convert_element_type.48
  158.3 1.5 collective-permute-start.7
  160.8 13.7 %collective-permute-done.7 = bf16[2,144,1024]{2,1,0:T(8,128)(2,1)S(1)} collective-permute-done((bf16[2,144,1024]{2,1,0:T(8,128)(2,1)S(1)}, bf16[2,144,1024]{2,1,0:T(8,128)(2,1)S(1)}, u32[]{:S(2)}, u32[]{:S(2)}) %collective-permute-start.7) | collective-permute-done | bytes 589856 | tf_op jit(solution)/shard_map/ppermute | solution.py:366
  175.4 1.5 collective-permute-start.8
  176.9 9.3 %collective-permute-done.1 = bf16[2,144,1024]{2,1,0:T(8,128)(2,1)S(1)} collective-permute-done((bf16[2,144,1024]{2,1,0:T(8,128)(2,1)S(1)}, bf16[2,144,1024]{2,1,0:T(8,128)(2,1)S(1)}, u32[]{:S(2)}, u32[]{:S(2)}) %collective-permute-start.1) | collective-permute-done | bytes 589856 | tf_op jit(solution)/shard_map/ppermute | solution.py:366
  187.1 1.5 collective-permute-start.2
  189.5 0.8 pad_maximum_fusion.6.into_ref
  190.4 6.0 %carry_gate.3 = (bf16[2,512,1024]{2,1,0:T(8,128)(2,1)}, f32[8,512]{1,0:T(8,128)}) custom-call(bf16[512,384]{1,0:T(8,128)(2,1)} %get-tuple-element.41.control_ref, f32[2,512,1024]{2,1,0:T(8,128)} %within_chunk.3.near_ref, bf16[2,128,1024]{2,1,0:T(8,128)(2,1)} %pad_maximum_fusion.6.into_ref, f32[2,512,128]{2,1,0:T(8,128)} %get-tuple-element.49.reach_ref, ...), custom_call_target="tpu_custom_call" | custom-call | tf_op jit(solution)/shard_map/carry_gate/pallas_call | solution.py:299
  196.4 0.8 collective-permute-start.11
  197.4 2.0 collective-permute-start.9
  199.4 2.2 collective-permute-done.2
  202.2 0.8 pad_maximum_fusion.5.into_ref
  203.0 6.0 %carry_gate.2 = (bf16[2,512,1024]{2,1,0:T(8,128)(2,1)}, f32[8,512]{1,0:T(8,128)}) custom-call(bf16[512,384]{1,0:T(8,128)(2,1)} %get-tuple-element.29.control_ref, f32[2,512,1024]{2,1,0:T(8,128)} %within_chunk.2.near_ref, bf16[2,128,1024]{2,1,0:T(8,128)(2,1)} %pad_maximum_fusion.5.into_ref, f32[2,512,128]{2,1,0:T(8,128)} %get-tuple-element.37.reach_ref, ...), custom_call_target="tpu_custom_call" | custom-call | tf_op jit(solution)/shard_map/carry_gate/pallas_call | solution.py:299
  210.0 2.0 collective-permute-start.3
  212.0 8.3 %output_project.3 = bf16[512,2048]{1,0:T(8,128)(2,1)} custom-call(s32[1]{0:T(128)} %constant.92.clone.1.mirror_ref, bf16[2,512,1024]{2,1,0:T(8,128)(2,1)} %get-tuple-element.51.gated_ref, f32[8,512]{1,0:T(8,128)} %get-tuple-element.52.refs_0_, f32[8,512]{1,0:T(8,128)} %collective-permute-done.9.refs_1_, f32[8,512]{1,0:T(8,128)} %collective-permute-done.10.refs_2_, ...), custom_call_target="tpu_custom_call" | custom-call | tf_op jit(solution)/shard_map/output_project/pallas_call | solution.py:346
  221.0 7.6 %output_project.2 = bf16[512,2048]{1,0:T(8,128)(2,1)} custom-call(s32[1]{0:T(128)} %constant.76.clone.1.mirror_ref, bf16[2,512,1024]{2,1,0:T(8,128)(2,1)} %get-tuple-element.39.gated_ref, f32[8,512]{1,0:T(8,128)} %get-tuple-element.40.refs_0_, f32[8,512]{1,0:T(8,128)} %copy-done.5, f32[8,512]{1,0:T(8,128)} %copy-done.4, f32[8,512]{1,0:T(8,128)} %copy-done.3, ...), custom_call_target="tpu_custom_call" | custom-call | tf_op jit(solution)/shard_map/output_project/pallas_call | solution.py:346
  228.6 4.0 %pad_maximum_fusion = bf16[512,4096]{1,0:T(8,128)(2,1)} fusion(bf16[512,2048]{1,0:T(8,128)(2,1)S(1)} %copy-done, bf16[512,2048]{1,0:T(8,128)(2,1)} %output_project.2), kind=kLoop, calls=%fused_computation | loop fusion | flops 8388608 | bytes 8388608 | tf_op jit(solution)/shard_map/concatenate | solution.py:430
  232.6 76.5 %reduce-scatter.2.cloned.1.call-done = bf16[512,1024]{1,0:T(8,128)(2,1)} async-done(((bf16[512,4096]{1,0:T(8,128)(2,1)}), bf16[512,1024]{1,0:T(8,128)(2,1)}) %reduce-scatter.2.cloned.1.call-update) | async-done | bytes 1048592 | tf_op jit(solution)/shard_map/reduce_scatter | solution.py:431
  (108 shorter events, 10.1 us)
Async XLA Ops:
  6.5 1.7 slice-start
  6.5 2.0 slice-start.1
  6.5 0.9 copy-start.10
  6.5 85.9 %all-gather.2.cloned.1.call-start = ((), (), s32[]{:S(2)}) async-start(), calls=%async_computation.1 | async-start | bytes 5242880 | tf_op jit(solution)/shard_map/all_gather | solution.py:412
  7.3 301.8 %reduce-scatter.2.cloned.1.call-start = ((), (), s32[]{:S(2)}) async-start(), calls=%async_computation.2 | async-start | bytes 5242880 | tf_op jit(solution)/shard_map/reduce_scatter | solution.py:431
  7.4 1.7 copy-start.6
  7.4 1.7 copy-start.7
  113.2 41.3 %collective-permute-start.6 = (bf16[2,144,1024]{2,1,0:T(8,128)(2,1)}, bf16[2,144,1024]{2,1,0:T(8,128)(2,1)}, u32[]{:S(2)}, u32[]{:S(2)}) collective-permute-start(bf16[2,144,1024]{2,1,0:T(8,128)(2,1)} %get-tuple-element.48), channel_id=1, source_target_pairs={{0,4},{4,0},{8,12},{12,8},{16,20},{20,16},{24,28},{28,24},{1,5},{5... | collective-permute-start | bytes 1769480 | tf_op jit(solution)/shard_map/ppermute | solution.py:366
  129.4 26.9 %collective-permute-start = (bf16[2,144,1024]{2,1,0:T(8,128)(2,1)}, bf16[2,144,1024]{2,1,0:T(8,128)(2,1)}, u32[]{:S(2)}, u32[]{:S(2)}) collective-permute-start(bf16[2,144,1024]{2,1,0:T(8,128)(2,1)} %get-tuple-element.36), channel_id=1, source_target_pairs={{0,4},{4,0},{8,12},{12,8},{16,20},{20,16},{24,28},{28,24},{1,5},{5... | collective-permute-start | bytes 1769480 | tf_op jit(solution)/shard_map/ppermute | solution.py:366
  129.9 6.3 %copy-start.8 = (bf16[2048,1024]{1,0:T(8,128)(2,1)S(1)}, bf16[2048,1024]{1,0:T(8,128)(2,1)}, u32[]{:S(2)}) copy-start(bf16[2048,1024]{1,0:T(8,128)(2,1)} %param.14) | copy-start | bytes 12582916
  129.9 6.3 %copy-start.9 = (bf16[512,2048]{1,0:T(8,128)(2,1)S(1)}, bf16[512,2048]{1,0:T(8,128)(2,1)}, u32[]{:S(2)}) copy-start(bf16[512,2048]{1,0:T(8,128)(2,1)} %get-tuple-element.50) | copy-start | bytes 6291460
  136.1 3.3 %copy-start.2 = (bf16[2,144,1024]{2,1,0:T(8,128)(2,1)S(1)}, bf16[2,144,1024]{2,1,0:T(8,128)(2,1)}, u32[]{:S(2)}) copy-start(bf16[2,144,1024]{2,1,0:T(8,128)(2,1)} %get-tuple-element.48) | copy-start | bytes 1769476
  139.5 1.1 copy-start.1
  158.3 16.3 %collective-permute-start.7 = (bf16[2,144,1024]{2,1,0:T(8,128)(2,1)S(1)}, bf16[2,144,1024]{2,1,0:T(8,128)(2,1)S(1)}, u32[]{:S(2)}, u32[]{:S(2)}) collective-permute-start(bf16[2,144,1024]{2,1,0:T(8,128)(2,1)S(1)} %get-tuple-element.114), channel_id=1, source_target_pairs={{0,8},{4,12},{8,0},{12,4},{16,24},{20,28},{24,16},{28,20},{1,9},{5... | collective-permute-start | bytes 1769480 | tf_op jit(solution)/shard_map/ppermute | solution.py:366
  160.2 26.1 %collective-permute-start.1 = (bf16[2,144,1024]{2,1,0:T(8,128)(2,1)S(1)}, bf16[2,144,1024]{2,1,0:T(8,128)(2,1)S(1)}, u32[]{:S(2)}, u32[]{:S(2)}) collective-permute-start(bf16[2,144,1024]{2,1,0:T(8,128)(2,1)S(1)} %get-tuple-element.110), channel_id=1, source_target_pairs={{0,8},{4,12},{8,0},{12,4},{16,24},{20,28},{24,16},{28,20},{1,9},{5... | collective-permute-start | bytes 1769480 | tf_op jit(solution)/shard_map/ppermute | solution.py:366
  175.4 13.5 %collective-permute-start.8 = (bf16[2,144,1024]{2,1,0:T(8,128)(2,1)S(1)}, bf16[2,144,1024]{2,1,0:T(8,128)(2,1)S(1)}, u32[]{:S(2)}, u32[]{:S(2)}) collective-permute-start(bf16[2,144,1024]{2,1,0:T(8,128)(2,1)S(1)} %pad_maximum_fusion.4), channel_id=1, source_target_pairs={{0,16},{4,20},{8,24},{12,28},{16,0},{20,4},{24,8},{28,12},{1,17},{... | collective-permute-start | bytes 1769480 | tf_op jit(solution)/shard_map/ppermute | solution.py:366
  187.1 14.5 %collective-permute-start.2 = (bf16[2,144,1024]{2,1,0:T(8,128)(2,1)S(1)}, bf16[2,144,1024]{2,1,0:T(8,128)(2,1)S(1)}, u32[]{:S(2)}, u32[]{:S(2)}) collective-permute-start(bf16[2,144,1024]{2,1,0:T(8,128)(2,1)S(1)} %pad_maximum_fusion.2), channel_id=1, source_target_pairs={{0,16},{4,20},{8,24},{12,28},{16,0},{20,4},{24,8},{28,12},{1,17},{... | collective-permute-start | bytes 1769480 | tf_op jit(solution)/shard_map/ppermute | solution.py:366
  196.4 13.6 %collective-permute-start.11 = (f32[8,512]{1,0:T(8,128)}, f32[8,512]{1,0:T(8,128)}, u32[]{:S(2)}, u32[]{:S(2)}) collective-permute-start(f32[8,512]{1,0:T(8,128)} %get-tuple-element.52.refs_0_), channel_id=1, source_target_pairs={{0,3},{1,0},{2,1},{3,2},{4,7},{5,4},{6,5},{7,6},{8,11},{9,8},{10,9... | collective-permute-start | bytes 49160 | tf_op jit(solution)/shard_map/ppermute | solution.py:387
  197.2 14.8 %collective-permute-start.10 = (f32[8,512]{1,0:T(8,128)}, f32[8,512]{1,0:T(8,128)}, u32[]{:S(2)}, u32[]{:S(2)}) collective-permute-start(f32[8,512]{1,0:T(8,128)} %get-tuple-element.52.refs_0_), channel_id=1, source_target_pairs={{0,2},{1,3},{2,0},{3,1},{4,6},{5,7},{6,4},{7,5},{8,10},{9,11},{10,... | collective-permute-start | bytes 49160 | tf_op jit(solution)/shard_map/ppermute | solution.py:387
  197.4 14.6 %collective-permute-start.9 = (f32[8,512]{1,0:T(8,128)}, f32[8,512]{1,0:T(8,128)}, u32[]{:S(2)}, u32[]{:S(2)}) collective-permute-start(f32[8,512]{1,0:T(8,128)} %get-tuple-element.52.refs_0_), channel_id=1, source_target_pairs={{0,1},{1,2},{2,3},{3,0},{4,5},{5,6},{6,7},{7,4},{8,9},{9,10},{10,1... | collective-permute-start | bytes 49160 | tf_op jit(solution)/shard_map/ppermute | solution.py:387
  209.1 11.3 %collective-permute-start.5 = (f32[8,512]{1,0:T(8,128)}, f32[8,512]{1,0:T(8,128)S(1)}, u32[]{:S(2)}, u32[]{:S(2)}) collective-permute-start(f32[8,512]{1,0:T(8,128)} %get-tuple-element.40.refs_0_), channel_id=1, source_target_pairs={{0,3},{1,0},{2,1},{3,2},{4,7},{5,4},{6,5},{7,6},{8,11},{9,8},{10,9... | collective-permute-start | bytes 49160 | tf_op jit(solution)/shard_map/ppermute | solution.py:387
  209.6 10.7 %collective-permute-start.4 = (f32[8,512]{1,0:T(8,128)}, f32[8,512]{1,0:T(8,128)S(1)}, u32[]{:S(2)}, u32[]{:S(2)}) collective-permute-start(f32[8,512]{1,0:T(8,128)} %get-tuple-element.40.refs_0_), channel_id=1, source_target_pairs={{0,2},{1,3},{2,0},{3,1},{4,6},{5,7},{6,4},{7,5},{8,10},{9,11},{10,... | collective-permute-start | bytes 49160 | tf_op jit(solution)/shard_map/ppermute | solution.py:387
  210.0 10.3 %collective-permute-start.3 = (f32[8,512]{1,0:T(8,128)}, f32[8,512]{1,0:T(8,128)S(1)}, u32[]{:S(2)}, u32[]{:S(2)}) collective-permute-start(f32[8,512]{1,0:T(8,128)} %get-tuple-element.40.refs_0_), channel_id=1, source_target_pairs={{0,1},{1,2},{2,3},{3,0},{4,5},{5,6},{6,7},{7,4},{8,9},{9,10},{10,1... | collective-permute-start | bytes 49160 | tf_op jit(solution)/shard_map/ppermute | solution.py:387
  220.3 0.6 copy-start.3
  220.3 0.6 copy-start.4
  220.4 0.6 copy-start.5
  221.0 7.6 %copy-start = (bf16[512,2048]{1,0:T(8,128)(2,1)S(1)}, bf16[512,2048]{1,0:T(8,128)(2,1)}, u32[]{:S(2)}) copy-start(bf16[512,2048]{1,0:T(8,128)(2,1)} %output_project.3) | copy-start | bytes 6291460
Sparse Core Ops, SparseCore 0:
  8.9 83.4 all-gather.1
  232.7 76.3 reduce-scatter.1
where the time goes:
time: 317 us; the launch traced here: 316 us
  waiting for transfers between devices  184 us (58%)
  Pallas kernels  74.1 us (23%)
  between operations  14 us (4%)
  other arithmetic  13.7 us (4%)
  starting transfers between devices  11.6 us (4%)
  matrix products  9.58 us (3%)
  local copies, waits for them, and re-layouts  9.09 us (3%)
    all_gather x1, waiting for transfers between devices, local(): whole = lax.all_gather(hidden, 'chan', axis=1, tiled=True)  81.3 us
    reduce_scatter x1, waiting for transfers between devices, local(): lax.psum_scatter(partial_value, 'chan', scatter_dimension=1, tiled=True)  76.5 us
    ppermute x6, waiting for transfers between devices, incoming_states(): lax.ppermute(group, 'seq', [(i, i ^ stride) for i in range(count)])  25.3 us
    pallas_call x2, Pallas kernels, norm_project(): pl.pallas_call(functools.partial(norm_project_kernel, len(xs)), grid=(col...  18.2 us
    pallas_call x2, Pallas kernels, output_project(): pl.pallas_call(functools.partial(output_kernel, inner, len(squares)), gri...  15.9 us
    pallas_call x2, Pallas kernels, chunk_states(): pl.pallas_call(states_kernel, grid=(1,), in_specs=[SMEM, SMEM, full(contr...  14 us
    pallas_call x2, Pallas kernels, within(): pl.pallas_call(within_kernel, grid=(chunks,), in_specs=[SMEM, SMEM, rows(...  13.9 us
    pallas_call x2, Pallas kernels, carry_gate(): pl.pallas_call(gate_kernel, grid=(tokens // CHUNK,), in_specs=[rows(contr...  12.1 us
  transfers between devices with their start and end apart: 14, of which 5 were waited for; matrix products, arithmetic and copies ran while one was open for 6% of the time, Pallas kernels for 16%

commit v1 on v0

--- a/solution.py
+++ b/solution.py
@@ -7,12 +7,15 @@
 from jax.experimental.pallas import tpu as pltpu
 from jax.sharding import PartitionSpec as P
 
+
 HEAD_DIM = 64
 STATE = 128
 CHUNK = 128
 LANES = 128
 REV = 256
 KEEP_ROWS = 16
+PIECES = 2
+
 
 norm_eps = 1e-05
 highest = lax.Precision.HIGHEST
@@ -66,21 +69,39 @@
 SMEM = pl.BlockSpec(memory_space=pltpu.SMEM)
 
 
-def norm_project_kernel(pieces, mirror_ref, *refs):
-    xs = refs[:pieces]
-    gain_ref, wv_ref, wc_ref, normed_ref, values_ref, control_ref, scr = refs[pieces:]
+def norm_project_kernel(routes, rank_ref, mirror_ref, *refs):
+    slots, pieces = len(routes[0]), len(routes[0][0])
+    xs = refs[: 1 + max(at for by_slot in routes for row in by_slot for at in row)]
+    gain_ref, wa_ref, wb_ref, wc_ref, normed_ref, values_ref, control_ref, scr, held, sems = refs[
+        len(xs) :
+    ]
     half = normed_ref.shape[1]
     blocks = half // REV
+    _, tokens, width = held.shape
+    rows = tokens // pieces
 
     @pl.when(pl.program_id(0) == 0)
     def _():
-        mirror = mirror_ref[0]
+        rank, mirror = rank_ref[0], mirror_ref[0]
+        target = lambda j, p: held.at[j, pl.ds(p * rows, rows), :]
+        for r, by_slot in enumerate(routes):
+
+            @pl.when(rank == r)
+            def _():
+                for j in range(slots):
+                    for p in range(pieces):
+                        pltpu.make_async_copy(
+                            xs[by_slot[j][p]], target(j, p), sems.at[j, p]
+                        ).start()
+
         swap = exchange_matrix(mirror)
-        squares = jnp.zeros((normed_ref.shape[0], 1), f32)
+        squares = jnp.zeros((tokens, 1), f32)
         at = 0
-        for x_ref in xs:
-            for q in range(x_ref.shape[1] // REV):
-                xb = x_ref[:, q * REV : (q + 1) * REV]
+        for j in range(slots):
+            for p in range(pieces):
+                pltpu.make_async_copy(xs[0], target(j, p), sems.at[j, p]).wait()
+            for q in range(width // REV):
+                xb = held[j, :, q * REV : (q + 1) * REV]
                 wide = xb.astype(f32)
                 squares = squares + jnp.sum(wide * wide, axis=1, keepdims=True)
                 scr[jnp.where(mirror == 1, blocks - 1 - at, at)] = mm(xb, swap).astype(bf16)
@@ -91,19 +112,57 @@
             normed_ref[:, cols] = (scr[q].astype(f32) * scale * gain_ref[:, cols]).astype(bf16)
         control_ref[...] = mm(normed_ref[...], wc_ref[...]).astype(bf16)
 
-    values_ref[...] = mm(normed_ref[...], wv_ref[...]).astype(bf16)
-
-
-def norm_project(xs, mirror, gain, w_values, w_control):
-    tokens = xs[0].shape[0]
-    half, cols = w_values.shape
+    two_weights(normed_ref, wa_ref, wb_ref, values_ref)
+
+
+def two_weights(x_ref, wa_ref, wb_ref, out_ref):
+    first = pl.program_id(0) < pl.num_programs(0) // 2
+
+    @pl.when(first)
+    def _():
+        out_ref[...] = mm(x_ref[...], wa_ref[...]).astype(bf16)
+
+    @pl.when(jnp.logical_not(first))
+    def _():
+        out_ref[...] = mm(x_ref[...], wb_ref[...]).astype(bf16)
+
+
+def weight_specs(half, tile, steps):
+    return [
+        pl.BlockSpec((half, tile), lambda j: (0, jnp.minimum(j, steps - 1))),
+        pl.BlockSpec((half, tile), lambda j: (0, jnp.maximum(j - steps, 0))),
+    ]
+
+
+def project(x, weights):
+    tokens, half = x.shape
+    cols = weights[0].shape[1]
     tile = min(256, cols)
-    return pl.pallas_call(
-        functools.partial(norm_project_kernel, len(xs)),
-        grid=(cols // tile,),
-        in_specs=[SMEM]
-        + [full(x.shape) for x in xs]
-        + [full(gain.shape), pl.BlockSpec((half, tile), lambda j: (0, j)), full(w_control.shape)],
+    steps = cols // tile
+    return pl.pallas_call(
+        two_weights,
+        grid=(2 * steps,),
+        in_specs=[full(x.shape)] + weight_specs(half, tile, steps),
+        out_specs=pl.BlockSpec((tokens, tile), lambda j: (0, j)),
+        out_shape=jax.ShapeDtypeStruct((tokens, 2 * cols), bf16),
+        name="project",
+    )(x, *weights)
+
+
+def norm_project(routes, xs, rank, mirror, gain, weights, w_control):
+    slots, pieces = len(routes[0]), len(routes[0][0])
+    tokens = xs[0].shape[0] * pieces
+    half, cols = weights[0].shape
+    tile = min(256, cols)
+    steps = cols // tile
+    return pl.pallas_call(
+        functools.partial(norm_project_kernel, routes),
+        grid=(2 * steps,),
+        in_specs=[SMEM, SMEM]
+        + [pl.BlockSpec(memory_space=pl.ANY) for x in xs]
+        + [full(gain.shape)]
+        + weight_specs(half, tile, steps)
+        + [full(w_control.shape)],
         out_specs=[
             full((tokens, half)),
             pl.BlockSpec((tokens, tile), lambda j: (0, j)),
@@ -111,12 +170,16 @@
         ],
         out_shape=[
             jax.ShapeDtypeStruct((tokens, half), bf16),
-            jax.ShapeDtypeStruct((tokens, cols), bf16),
+            jax.ShapeDtypeStruct((tokens, 2 * cols), bf16),
             jax.ShapeDtypeStruct((tokens, w_control.shape[1]), bf16),
         ],
-        scratch_shapes=[pltpu.VMEM((half // REV, tokens, REV), bf16)],
+        scratch_shapes=[
+            pltpu.VMEM((half // REV, tokens, REV), bf16),
+            pltpu.VMEM((slots, tokens, half // slots), bf16),
+            pltpu.SemaphoreType.DMA((slots, pieces)),
+        ],
         name="norm_project",
-    )(mirror, *xs, gain, w_values, w_control)
+    )(rank, mirror, *xs, gain, *weights, w_control)
 
 
 def states_kernel(
@@ -311,7 +374,7 @@
 
 def output_kernel(inner, sums, mirror_ref, gated_ref, *refs):
     squares_refs = refs[:sums]
-    gain_ref, w_ref, out_ref = refs[sums:]
+    gain_ref, wa_ref, wb_ref, out_ref = refs[sums:]
     squares = squares_refs[0][...]
     for other in squares_refs[1:]:
         squares = squares + other[...]
@@ -322,72 +385,129 @@
         gated_ref[0].astype(f32) * scale[:, 0:1] * gain
         + gated_ref[1].astype(f32) * scale[:, 1:2] * gain
     ).astype(bf16)
-    product = mm(combined, w_ref[...]).astype(bf16)
-    width = product.shape[1]
-    blocks = width // REV
+    cols = wa_ref.shape[0]
+    product = mm(combined[:, :cols], wa_ref[...]) + mm(combined[:, cols:], wb_ref[...])
+    product = product.astype(bf16)
+    slots, _, width = out_ref.shape
+    blocks, per_slot = slots * width // REV, width // REV
 
     @pl.when(mirror_ref[0] == 0)
     def _():
-        out_ref[...] = product
+        for j in range(slots):
+            out_ref[j] = product[:, j * width : (j + 1) * width]
 
     @pl.when(mirror_ref[0] == 1)
     def _():
         swap = exchange_matrix(jnp.int32(1))
         for q in range(blocks):
-            back = blocks - 1 - q
-            out_ref[:, back * REV : (back + 1) * REV] = mm(
+            j, at = divmod(blocks - 1 - q, per_slot)
+            out_ref[j, :, at * REV : (at + 1) * REV] = mm(
                 product[:, q * REV : (q + 1) * REV], swap
             ).astype(bf16)
 
 
-def output_project(inner, mirror, gated, squares, gain_row, w_out):
+def output_project(inner, mirror, gated, squares, gain_row, weights, slots, piece, pieces):
     _, tokens, cols = gated.shape
-    width = w_out.shape[1]
+    width = weights[0].shape[1] // slots
+    steps = tokens // CHUNK // pieces
+    at = lambda k: k + piece * steps
     return pl.pallas_call(
         functools.partial(output_kernel, inner, len(squares)),
-        grid=(tokens // CHUNK,),
-        in_specs=[SMEM, pl.BlockSpec((2, CHUNK, cols), lambda k: (0, k, 0))]
-        + [pl.BlockSpec((8, CHUNK), lambda k: (0, k)) for _ in squares]
-        + [full(gain_row.shape), full(w_out.shape)],
-        out_specs=pl.BlockSpec((CHUNK, width), lambda k: (k, 0)),
-        out_shape=jax.ShapeDtypeStruct((tokens, width), bf16),
+        grid=(steps,),
+        in_specs=[SMEM, pl.BlockSpec((2, CHUNK, cols), lambda k: (0, at(k), 0))]
+        + [pl.BlockSpec((8, CHUNK), lambda k: (0, at(k))) for _ in squares]
+        + [full(gain_row.shape)]
+        + [full(w.shape) for w in weights],
+        out_specs=pl.BlockSpec((slots, CHUNK, width), lambda k: (0, k, 0)),
+        out_shape=jax.ShapeDtypeStruct((slots, tokens // pieces, width), bf16),
         name="output_project",
-    )(mirror, gated, *squares, gain_row, w_out)
+    )(mirror, gated, *squares, gain_row, *weights)
 
 
 def incoming_states(total):
     count = lax.axis_size("seq")
-    place = lax.axis_index("seq")
-    group = total
-    into = [jnp.zeros(total.shape[1:], f32)] * 2
-    into_keep = [jnp.ones((1, total.shape[2]), f32)] * 2
-    stride = 1
-    while stride < count:
-        got = lax.ppermute(group, "seq", [(i, i ^ stride) for i in range(count)]).astype(f32)
-        mine = group.astype(f32)
-        upper = (place // stride) % 2 == 1
-        merged = []
-        for d in range(2):
-            after_got = upper if d == 0 else jnp.logical_not(upper)
-            got_keep, my_keep = got[d, STATE : STATE + 1], mine[d, STATE : STATE + 1]
-            into[d] = jnp.where(after_got, into_keep[d] * got[d] + into[d], into[d])
-            into_keep[d] = jnp.where(after_got, into_keep[d] * got_keep, into_keep[d])
-            late, early = jnp.where(after_got, mine[d], got[d]), jnp.where(after_got, got[d], mine[d])
-            late_keep = jnp.where(after_got, my_keep, got_keep)
-            states = late_keep * early[:STATE] + late[:STATE]
-            merged.append(jnp.concatenate([states, early[STATE:] * late[STATE:]], axis=0))
-        group = jnp.stack(merged).astype(bf16)
-        stride *= 2
-    return jnp.stack([into[0][:STATE], into[1][:STATE]]).astype(bf16)
+    late = lax.axis_index("seq") % 2 == 1
+    state = lambda m: m[:STATE].astype(f32)
+    keep = lambda m: m[STATE : STATE + 1].astype(f32)
+    swap = [(i, i ^ 1) for i in range(count)]
+    mine = jnp.where(late, total[0], total[1])
+    near = lax.ppermute(jnp.where(late, total[1], total[0]), "seq", swap)
+    pair = jnp.concatenate(
+        [
+            keep(mine) * state(near) + state(mine),
+            jnp.broadcast_to(keep(mine) * keep(near), (KEEP_ROWS, total.shape[2])),
+        ],
+        axis=0,
+    ).astype(bf16)
+    into, decay = 0.0, 1.0
+    for k in range(1, count // 2):
+        hop = [(i, i + 2 * k) for i in range(1, count, 2) if i + 2 * k < count]
+        hop += [(i, i - 2 * k) for i in range(0, count, 2) if i - 2 * k >= 0]
+        got = lax.ppermute(pair, "seq", hop)
+        into = into + decay * state(got)
+        decay = decay * keep(got)
+    across = lax.ppermute(into.astype(bf16), "seq", swap)
+    through = (keep(near) * into + state(near)).astype(bf16)
+    return jnp.stack([jnp.where(late, through, across), jnp.where(late, across, through)])
 
 
 def chan_parts(part):
     count = lax.axis_size("chan")
-    others = [
-        lax.ppermute(part, "chan", [(i, (i + k) % count) for i in range(count)])
-        for k in range(1, count)
+    return [part] + [
+        lax.ppermute(part, "chan", [(i, (i + 2 * k) % count) for i in range(count)])
+        for k in range(1, count // 2)
     ]
-    return [part] + others
+
+
+def settled(x):
+    def kernel(x_ref, out_ref):
+        out_ref[...] = x_ref[...]
+
+    return pl.pallas_call(
+        kernel, out_shape=jax.ShapeDtypeStruct(x.shape, x.dtype), name="settled"
+    )(x)
+
+
+def shard_of(rank, turn, count):
+    slots = count // 2
+    return rank % 2 * slots + (rank // 2 + turn) % slots
+
+
+def turns(count, back):
+    for turn in range(count // 2):
+        pairs = [(shard_of(r, turn, count), r) for r in range(count)]
+        yield turn, [(b, a) if back else (a, b) for a, b in pairs if a != b]
+
+
+def gather_strand(hidden, count):
+    slots = count // 2
+    xs = [hidden] + [lax.ppermute(hidden, "chan", pairs) for _, pairs in turns(count, False)]
+    routes = []
+    for rank in range(count):
+        by_slot = [None] * slots
+        for turn in range(slots):
+            shard = shard_of(rank, turn, count)
+            by_slot[shard % slots] = [0 if shard == rank else 1 + turn]
+        routes.append(by_slot)
+    return routes, xs
+
+
+def reduce_strand(partial, count, rank):
+    slots = count // 2
+    total = 0.0
+    for turn, pairs in turns(count, True):
+        mine = lax.dynamic_index_in_dim(partial, (rank // 2 + turn) % slots, 0, False)
+        got = lax.ppermute(mine, "chan", pairs)
+        kept = shard_of(rank, turn, count) == rank
+        total = total + jnp.where(kept, mine, got).astype(f32)
+    return total.astype(bf16)
+
+
+def partner_weights(w, count):
+    rows = w.shape[0] // lax.axis_size("seq")
+    part = lax.dynamic_slice_in_dim(w, lax.axis_index("seq") * rows, rows, 0)
+    part = lax.ppermute(part, "chan", [(i, i ^ 1) for i in range(count)])
+    return lax.all_gather(part, "seq", axis=0, tiled=True)
 
 
 def local(
@@ -397,38 +517,51 @@
     seq_count, chan_count = lax.axis_size("seq"), lax.axis_size("chan")
     seq_rank, chan_rank = lax.axis_index("seq"), lax.axis_index("chan")
     tokens = hidden.shape[0]
-    half = norm_gain.shape[0]
     cols = w_values.shape[1]
     heads = cols // HEAD_DIM
-    mine = lambda a, axis: lax.dynamic_slice_in_dim(a, chan_rank * heads, heads, axis)
-    lanes = lambda a: jnp.pad(a, ((0, 0), (0, LANES - heads)))
-    w_steps = lanes(mine(w_control[:, 2 * STATE :], 1))
-    w_small = jnp.concatenate([w_control[:, : 2 * STATE], w_steps], axis=1)
+    slots = chan_count // 2
+
+    def mine(a, axis):
+        return jnp.concatenate(
+            [
+                lax.dynamic_slice_in_dim(a, rank * heads, heads, axis)
+                for rank in (chan_rank, chan_rank ^ 1)
+            ],
+            axis,
+        )
+
+    lanes = lambda a: jnp.pad(a, ((0, 0), (0, LANES - 2 * heads)))
+    routes, xs = gather_strand(hidden, chan_count)
+    values_w = (w_values, partner_weights(w_values, chan_count))
+    gates_w = (w_gates, partner_weights(w_gates, chan_count))
+    out_w = (w_out, partner_weights(w_out, chan_count))
+    swap = [(i, i ^ 1) for i in range(chan_count)]
+    gate_row = jnp.concatenate([gate_gain, lax.ppermute(gate_gain, "chan", swap)])[None]
+    w_small = jnp.concatenate(
+        [w_control[:, : 2 * STATE], lanes(mine(w_control[:, 2 * STATE :], 1))], axis=1
+    )
     par = lanes(jnp.stack([mine(dt_bias, 0), mine(decay_total, 0) / (tokens * seq_count)]))
     par = jnp.pad(par, ((0, 6), (0, 0)))
+    par = settled(par)
     skip_row = jnp.repeat(mine(skip_gain, 0), HEAD_DIM)[None]
-    gain_row, gate_row = norm_gain[None], gate_gain[None]
-    base = jnp.reshape(seq_rank * tokens, (1,)).astype(jnp.int32)
-    whole = lax.all_gather(hidden, "chan", axis=1, tiled=True)
-    parts = []
-    for strand in range(2):
-        mirror = jnp.full((1,), strand, jnp.int32)
-        x = whole[:, strand * half : (strand + 1) * half]
-        normed, values, control = norm_project([x], mirror, gain_row, w_values, w_small)
-        total, pre, cola, colb, rowf, rowb, reach = chunk_states(
-            doc_starts, base, control, values, par
+    scalar = lambda v: jnp.reshape(v, (1,)).astype(jnp.int32)
+    base, mirror = scalar(seq_rank * tokens), scalar(chan_rank % 2)
+    normed, values, control = norm_project(
+        routes, xs, scalar(chan_rank), mirror, norm_gain[None], values_w, w_small
+    )
+    total, pre, cola, colb, rowf, rowb, reach = chunk_states(doc_starts, base, control, values, par)
+    into = incoming_states(total)
+    gates = project(normed, gates_w)
+    near = within(doc_starts, base, control, values, skip_row, pre, cola, colb, rowf, rowb)
+    gated, squares = carry_gate(control, near, into, reach, gates)
+    sums = chan_parts(squares)
+    result = []
+    for p in range(PIECES):
+        out = output_project(
+            cols * chan_count, mirror, gated, sums, gate_row, out_w, slots, p, PIECES
         )
-        into = incoming_states(total)
-        gates = mm(normed, w_gates).astype(bf16)
-        near = within(doc_starts, base, control, values, skip_row, pre, cola, colb, rowf, rowb)
-        gated, squares = carry_gate(control, near, into, reach, gates)
-        parts.append(
-            output_project(
-                cols * chan_count, mirror, gated, chan_parts(squares), gate_row, w_out
-            )
-        )
-    partial_value = jnp.concatenate(parts, axis=1)
-    return lax.psum_scatter(partial_value, "chan", scatter_dimension=1, tiled=True)
+        result.append(reduce_strand(out, chan_count, chan_rank))
+    return jnp.concatenate(result, axis=0)
 
 
 def solution(mesh):

time: 317 us -> 264 us (0.83)
  waiting for transfers between devices: 184 us -> 109 us
  starting transfers between devices: 11.6 us -> 49.2 us
  matrix products: 9.58 us -> 0 us
  other arithmetic: 13.7 us -> 8.46 us
    ppermute x12 -> x16, waiting for transfers between devices: 25.3 us -> 109 us  [the longest x3 34.1 us: partner_weights(): part = lax.ppermute(part, 'chan', [(i, i ^ 1) for i in range(count)])]
    all_gather x1 -> x3, waiting for transfers between devices: 81.3 us -> 0.01 us  [partner_weights(): return lax.all_gather(part, 'seq', axis=0, tiled=True)]
    reduce_scatter x1 -> x0, waiting for transfers between devices: 76.5 us -> none  [local(): lax.psum_scatter(partial_value, 'chan', scatter_dimension=1, tiled=True)]
    ppermute x12 -> x16, starting transfers between devices: 11.6 us -> 49.1 us  [the longest x1 26.1 us: local(): lax.ppermute(gate_gain, 'chan', swap)]
    dot_general x2 -> x0, matrix products: 9.58 us -> none  [mm(): return jnp.dot(a, b, preferred_element_type=f32)]
    pallas_call x2 -> x3, Pallas kernels: 18.2 us -> 27.1 us  [the longest x1 15.1 us: norm_project(): pl.pallas_call(functools.partial(norm_project_kernel, routes), grid=(2 *...]
    slice x9 -> x4, local copies, waits for them, and re-layouts: 4.84 us -> 0.01 us  [the longest x2 0.01 us: local(): w_control[:, 2 * STATE:]]
    pallas_call x2 -> x1, Pallas kernels: 14 us -> 9.67 us  [chunk_states(): pl.pallas_call(states_kernel, grid=(1,), in_specs=[SMEM, SMEM, full(contr...]
  transfers between devices with their start and end apart: 14 -> 19, of which waited for: 5 -> 10; matrix products, arithmetic and copies ran while one was open for 6% -> 4% of each run, Pallas kernels for 16% -> 24%
where the time goes in v1:
time: 264 us; the launch traced here: 263 us
  waiting for transfers between devices  109 us (41%)
  Pallas kernels  71.7 us (27%)
  starting transfers between devices  49.2 us (19%)
  between operations  13.4 us (5%)
  local copies, waits for them, and re-layouts  11.2 us (4%)
  other arithmetic  8.46 us (3%)
    ppermute x3, waiting for transfers between devices, partner_weights(): part = lax.ppermute(part, 'chan', [(i, i ^ 1) for i in range(count)])  34.1 us
    ppermute x4, waiting for transfers between devices, reduce_strand(): got = lax.ppermute(mine, 'chan', pairs)  32.8 us
    ppermute x1, starting transfers between devices, local(): lax.ppermute(gate_gain, 'chan', swap)  26.1 us
    ppermute x3, waiting for transfers between devices, incoming_states(): got = lax.ppermute(pair, 'seq', hop)  20.2 us
    ppermute x2, waiting for transfers between devices, gather_strand(): lax.ppermute(hidden, 'chan', pairs)  16.5 us
    pallas_call x2, Pallas kernels, output_project(): pl.pallas_call(functools.partial(output_kernel, inner, len(squares)), gri...  15.1 us
    pallas_call x1, Pallas kernels, norm_project(): pl.pallas_call(functools.partial(norm_project_kernel, routes), grid=(2 *...  15.1 us
    pallas_call x1, Pallas kernels, project(): pl.pallas_call(two_weights, grid=(2 * steps,), in_specs=[full(x.shape)] +...  10.8 us
  transfers between devices with their start and end apart: 19, of which 10 were waited for; matrix products, arithmetic and copies ran while one was open for 4% of the time, Pallas kernels for 24%

profile of v1, /device:TPU:0, one launch (start us, length us, event | category | flops | bytes accessed | tf_op | source)
XLA Modules:
  0.0 262.9 jit_solution(580277749598184178)
XLA Ops:
  7.6 3.1 %collective-permute-start.2 = (bf16[256,1024]{1,0:T(8,128)(2,1)S(1)}, bf16[256,1024]{1,0:T(8,128)(2,1)S(1)}, u32[]{:S(2)}, u32[]{:S(2)}) collective-permute-start(bf16[256,1024]{1,0:T(8,128)(2,1)S(1)} %constant_dynamic-slice_fusion.4), channel_id=1, source_target_pairs={{0,1},{1,0},{2,3},{3,2},{4,5},{5,4},{6,7},{7,6},{8,9},{9,8},{10,11... | collective-permute-start | bytes 1572872 | tf_op jit(solution)/shard_map/ppermute | solution.py:509
  10.7 11.9 %collective-permute-done.2 = bf16[256,1024]{1,0:T(8,128)(2,1)S(1)} collective-permute-done((bf16[256,1024]{1,0:T(8,128)(2,1)S(1)}, bf16[256,1024]{1,0:T(8,128)(2,1)S(1)}, u32[]{:S(2)}, u32[]{:S(2)}) %collective-permute-start.2) | collective-permute-done | bytes 524320 | tf_op jit(solution)/shard_map/ppermute | solution.py:509
  24.6 1.8 collective-permute-start.8
  26.4 11.3 %collective-permute-done.8 = bf16[256,1024]{1,0:T(8,128)(2,1)S(1)} collective-permute-done((bf16[256,1024]{1,0:T(8,128)(2,1)S(1)}, bf16[256,1024]{1,0:T(8,128)(2,1)S(1)}, u32[]{:S(2)}, u32[]{:S(2)}) %collective-permute-start.8) | collective-permute-done | bytes 524320 | tf_op jit(solution)/shard_map/ppermute | solution.py:509
  39.8 1.5 collective-permute-start.11
  41.3 10.9 %collective-permute-done.11 = bf16[128,2048]{1,0:T(8,128)(2,1)S(1)} collective-permute-done((bf16[128,2048]{1,0:T(8,128)(2,1)S(1)}, bf16[128,2048]{1,0:T(8,128)(2,1)S(1)}, u32[]{:S(2)}, u32[]{:S(2)}) %collective-permute-start.11) | collective-permute-done | bytes 524320 | tf_op jit(solution)/shard_map/ppermute | solution.py:509
  53.1 1.7 collective-permute-start
  54.7 2.9 %collective-permute-start.1 = (bf16[512,1024]{1,0:T(8,128)(2,1)}, bf16[512,1024]{1,0:T(8,128)(2,1)}, u32[]{:S(2)}, u32[]{:S(2)}) collective-permute-start(bf16[512,1024]{1,0:T(8,128)(2,1)} %refs_0_.1), channel_id=1, source_target_pairs={{1,0},{3,1},{0,2},{2,3},{5,4},{7,5},{4,6},{6,7},{9,8},{11,9},{8,10... | collective-permute-start | bytes 3145736 | tf_op jit(solution)/shard_map/ppermute | solution.py:484
  60.8 1.3 fusion.1.refs_6_
  62.1 16.5 %collective-permute-done.1.refs_2_ = bf16[512,1024]{1,0:T(8,128)(2,1)} collective-permute-done((bf16[512,1024]{1,0:T(8,128)(2,1)}, bf16[512,1024]{1,0:T(8,128)(2,1)}, u32[]{:S(2)}, u32[]{:S(2)}) %collective-permute-start.1) | collective-permute-done | bytes 1048608 | tf_op jit(solution)/shard_map/ppermute | solution.py:484
  78.6 15.1 %norm_project.1 = (bf16[512,2048]{1,0:T(8,128)(2,1)}, bf16[512,2048]{1,0:T(8,128)(2,1)}, bf16[512,384]{1,0:T(8,128)(2,1)}) custom-call(s32[1]{0:T(128)} %bitcast.1.rank_ref, s32[1]{0:T(128)} %bitcast.mirror_ref, bf16[512,1024]{1,0:T(8,128)(2,1)} %refs_0_.1, bf16[512,1024]{1,0:T(8,128)(2,1)} %collective-permute-done.refs_1_, ...), custom_call_target="tpu_custom_call" | custom-call | tf_op jit(solution)/shard_map/norm_project/pallas_call | solution.py:158
  93.8 9.7 %chunk_states.1 = (bf16[2,144,2048]{2,1,0:T(8,128)(2,1)}, bf16[2,4,128,2048]{3,2,1,0:T(8,128)(2,1)}, f32[512,128]{1,0:T(8,128)}, f32[512,128]{1,0:T(8,128)}, f32...) custom-call(s32[4]{0:T(128)} %starts_ref.3, s32[1]{0:T(128)} %bitcast.3.base_ref, ...), custom_call_target="tpu_custom_call" | custom-call | tf_op jit(solution)/shard_map/chunk_states/pallas_call | solution.py:257
  103.4 1.3 broadcast_select_fusion
  104.8 2.0 collective-permute-done.3
  107.1 1.3 collective-permute-start.4
  108.4 1.3 collective-permute-start.5
  109.7 1.5 collective-permute-start.6
  111.2 19.2 %collective-permute-done.4 = bf16[144,2048]{1,0:T(8,128)(2,1)S(1)} collective-permute-done((bf16[144,2048]{1,0:T(8,128)(2,1)S(1)}, bf16[144,2048]{1,0:T(8,128)(2,1)S(1)}, u32[]{:S(2)}, u32[]{:S(2)}) %collective-permute-start.4) | collective-permute-done | bytes 589856 | tf_op jit(solution)/shard_map/ppermute | solution.py:446
  131.8 26.1 %collective-permute-start.10 = (f32[1024]{0:T(1024)S(1)}, f32[1024]{0:T(1024)S(1)}, u32[]{:S(2)}, u32[]{:S(2)}) collective-permute-start(f32[1024]{0:T(1024)S(1)} %copy-done.4), channel_id=1, source_target_pairs={{0,1},{1,0},{2,3},{3,2},{4,5},{5,4},{6,7},{7,6},{8,9},{9,8},{10,11... | collective-permute-start | bytes 12296 | tf_op jit(solution)/shard_map/ppermute | solution.py:539
  158.7 10.5 %within_chunk.1.near_ref = f32[2,512,2048]{2,1,0:T(8,128)} custom-call(s32[4]{0:T(128)} %starts_ref.3, s32[1]{0:T(128)} %bitcast.3.base_ref, bf16[512,384]{1,0:T(8,128)(2,1)} %get-tuple-element.17.control_ref, bf16[512,2048]{1,0:T(8,128)(2,1)} %get-tuple-element.18.values_ref, f32[1,2048]{1,0:T(1,128)} %broadcast_in_dim_reshape.3.skip_ref, ...), custom_call_target="tpu_custom_call" | custom-call | tf_op jit(solution)/shard_map/within_chunk/pallas_call | solution.py:324
  169.2 10.8 %project.1.gates_ref = bf16[512,2048]{1,0:T(8,128)(2,1)} custom-call(bf16[512,2048]{1,0:T(8,128)(2,1)} %get-tuple-element.26.x_ref, bf16[2048,1024]{1,0:T(8,128)(2,1)} %wa_ref.1, bf16[2048,1024]{1,0:T(8,128)(2,1)} %all-gather.6.cloned.1.call-done.wb_ref), custom_call_target="tpu_custom_call" | custom-call | tf_op jit(solution)/shard_map/project/pallas_call | solution.py:142
  181.6 9.2 %carry_gate.1 = (bf16[2,512,2048]{2,1,0:T(8,128)(2,1)}, f32[8,512]{1,0:T(8,128)}) custom-call(bf16[512,384]{1,0:T(8,128)(2,1)} %get-tuple-element.17.control_ref, f32[2,512,2048]{2,1,0:T(8,128)} %within_chunk.1.near_ref, bf16[2,128,2048]{2,1,0:T(8,128)(2,1)} %pad_maximum_fusion.into_ref, f32[2,512,128]{2,1,0:T(8,128)} %get-tuple-element.25.reach_ref, ...), custom_call_target="tpu_custom_call" | custom-call | tf_op jit(solution)/shard_map/carry_gate/pallas_call | solution.py:362
  192.4 3.3 %collective-permute-done.9.refs_1_ = f32[8,512]{1,0:T(8,128)S(1)} collective-permute-done((f32[8,512]{1,0:T(8,128)}, f32[8,512]{1,0:T(8,128)S(1)}, u32[]{:S(2)}, u32[]{:S(2)}) %collective-permute-start.9) | collective-permute-done | bytes 16416 | tf_op jit(solution)/shard_map/ppermute | solution.py:457
  196.3 7.6 %output_project.2 = bf16[2,256,1024]{2,1,0:T(8,128)(2,1)} custom-call(s32[1]{0:T(128)} %bitcast.mirror_ref, bf16[2,512,2048]{2,1,0:T(8,128)(2,1)} %get-tuple-element.27.gated_ref, f32[8,512]{1,0:T(8,128)} %get-tuple-element.28.refs_0_, f32[8,512]{1,0:T(8,128)} %copy-done.3, f32[1,2048]{1,0:T(1,128)} %bitcast.44, bf16[1024,2048]{1,0:T(8,128)(2,1)} %refs_3_.3, ...), custom_call_target="tpu_custom_call" | custom-call | tf_op jit(solution)/shard_map/output_project/pallas_call | solution.py:414
  203.9 1.3 dynamic-slice_bitcast_fusion.3
  205.8 2.8 %collective-permute-start.13 = (bf16[256,1024]{1,0:T(8,128)(2,1)S(1)}, bf16[256,1024]{1,0:T(8,128)(2,1)S(1)}, u32[]{:S(2)}, u32[]{:S(2)}) collective-permute-start(bf16[256,1024]{1,0:T(8,128)(2,1)S(1)} %get-tuple-element.34), channel_id=1, source_target_pairs={{0,1},{1,3},{2,0},{3,2},{4,5},{5,7},{6,4},{7,6},{8,9},{9,11},{10,8... | collective-permute-start | bytes 1572872 | tf_op jit(solution)/shard_map/ppermute | solution.py:500
  208.6 7.6 %output_project.3 = bf16[2,256,1024]{2,1,0:T(8,128)(2,1)} custom-call(s32[1]{0:T(128)} %bitcast.mirror_ref, bf16[2,512,2048]{2,1,0:T(8,128)(2,1)} %get-tuple-element.27.gated_ref, f32[8,512]{1,0:T(8,128)} %get-tuple-element.28.refs_0_, f32[8,512]{1,0:T(8,128)} %copy-done.3, f32[1,2048]{1,0:T(1,128)} %bitcast.45, bf16[1024,2048]{1,0:T(8,128)(2,1)} %refs_3_.3, ...), custom_call_target="tpu_custom_call" | custom-call | tf_op jit(solution)/shard_map/output_project/pallas_call | solution.py:414
  217.5 1.5 collective-permute-start.14
  219.0 1.7 collective-permute-start.15
  220.7 12.3 %collective-permute-done.13 = bf16[256,1024]{1,0:T(8,128)(2,1)S(1)} collective-permute-done((bf16[256,1024]{1,0:T(8,128)(2,1)S(1)}, bf16[256,1024]{1,0:T(8,128)(2,1)S(1)}, u32[]{:S(2)}, u32[]{:S(2)}) %collective-permute-start.13) | collective-permute-done | bytes 524320 | tf_op jit(solution)/shard_map/ppermute | solution.py:500
  233.4 20.5 %collective-permute-done.15 = bf16[256,1024]{1,0:T(8,128)(2,1)} collective-permute-done((bf16[256,1024]{1,0:T(8,128)(2,1)S(1)}, bf16[256,1024]{1,0:T(8,128)(2,1)}, u32[]{:S(2)}, u32[]{:S(2)}) %collective-permute-start.15) | collective-permute-done | bytes 524320 | tf_op jit(solution)/shard_map/ppermute | solution.py:500
  253.9 1.4 add_convert_fusion
  (72 shorter events, 18.5 us)
Async XLA Ops:
  6.5 72.1 %all-gather.4.cloned.1.call-start = ((), (), s32[]{:S(2)}) async-start(), calls=%async_computation | async-start | bytes 4718592 | tf_op jit(solution)/shard_map/all_gather | solution.py:510
  7.6 15.0 %collective-permute-start.2 = (bf16[256,1024]{1,0:T(8,128)(2,1)S(1)}, bf16[256,1024]{1,0:T(8,128)(2,1)S(1)}, u32[]{:S(2)}, u32[]{:S(2)}) collective-permute-start(bf16[256,1024]{1,0:T(8,128)(2,1)S(1)} %constant_dynamic-slice_fusion.4), channel_id=1, source_target_pairs={{0,1},{1,0},{2,3},{3,2},{4,5},{5,4},{6,7},{7,6},{8,9},{9,8},{10,11... | collective-permute-start | bytes 1572872 | tf_op jit(solution)/shard_map/ppermute | solution.py:509
  22.7 0.8 copy-start.2
  23.5 145.7 %all-gather.6.cloned.1.call-start = ((), (), s32[]{:S(2)}) async-start(), calls=%async_computation.1 | async-start | bytes 4718592 | tf_op jit(solution)/shard_map/all_gather | solution.py:510
  24.6 13.2 %collective-permute-start.8 = (bf16[256,1024]{1,0:T(8,128)(2,1)S(1)}, bf16[256,1024]{1,0:T(8,128)(2,1)S(1)}, u32[]{:S(2)}, u32[]{:S(2)}) collective-permute-start(bf16[256,1024]{1,0:T(8,128)(2,1)S(1)} %constant_dynamic-slice_fusion.1), channel_id=1, source_target_pairs={{0,1},{1,0},{2,3},{3,2},{4,5},{5,4},{6,7},{7,6},{8,9},{9,8},{10,11... | collective-permute-start | bytes 1572872 | tf_op jit(solution)/shard_map/ppermute | solution.py:509
  37.8 0.8 copy-start.1
  38.6 153.8 %all-gather.8.cloned.1.call-start = ((), (), s32[]{:S(2)}) async-start(), calls=%async_computation.2 | async-start | bytes 4718592 | tf_op jit(solution)/shard_map/all_gather | solution.py:510
  38.6 19.0 %slice-start = ((bf16[2048,320]{0,1:T(8,128)(2,1)}), bf16[2048,64]{0,1:T(8,128)(2,1)S(1)}, s32[]{:S(2)}) async-start(bf16[2048,320]{0,1:T(8,128)(2,1)} %param.15), calls=%async_computation.3 | async-start | bytes 524288 | tf_op jit(solution)/shard_map/slice | solution.py:541
  39.8 12.4 %collective-permute-start.11 = (bf16[128,2048]{1,0:T(8,128)(2,1)S(1)}, bf16[128,2048]{1,0:T(8,128)(2,1)S(1)}, u32[]{:S(2)}, u32[]{:S(2)}) collective-permute-start(bf16[128,2048]{1,0:T(8,128)(2,1)S(1)} %constant_dynamic-slice_fusion), channel_id=1, source_target_pairs={{0,1},{1,0},{2,3},{3,2},{4,5},{5,4},{6,7},{7,6},{8,9},{9,8},{10,11... | collective-permute-start | bytes 1572872 | tf_op jit(solution)/shard_map/ppermute | solution.py:509
  52.2 0.8 copy-start
  52.2 5.8 %slice-start.1 = ((bf16[2048,320]{0,1:T(8,128)(2,1)}), bf16[2048,256]{0,1:T(8,128)(2,1)S(1)}, s32[]{:S(2)}) async-start(bf16[2048,320]{0,1:T(8,128)(2,1)} %param.15), calls=%async_computation.4 | async-start | bytes 2097152 | tf_op jit(solution)/shard_map/slice | solution.py:541
  53.1 9.1 %collective-permute-start = (bf16[512,1024]{1,0:T(8,128)(2,1)}, bf16[512,1024]{1,0:T(8,128)(2,1)}, u32[]{:S(2)}, u32[]{:S(2)}) collective-permute-start(bf16[512,1024]{1,0:T(8,128)(2,1)} %refs_0_.1), channel_id=1, source_target_pairs={{2,1},{1,2},{6,5},{5,6},{10,9},{9,10},{14,13},{13,14},{18,17},{17,... | collective-permute-start | bytes 3145736 | tf_op jit(solution)/shard_map/ppermute | solution.py:484
  54.7 23.9 %collective-permute-start.1 = (bf16[512,1024]{1,0:T(8,128)(2,1)}, bf16[512,1024]{1,0:T(8,128)(2,1)}, u32[]{:S(2)}, u32[]{:S(2)}) collective-permute-start(bf16[512,1024]{1,0:T(8,128)(2,1)} %refs_0_.1), channel_id=1, source_target_pairs={{1,0},{3,1},{0,2},{2,3},{5,4},{7,5},{4,6},{6,7},{9,8},{11,9},{8,10... | collective-permute-start | bytes 3145736 | tf_op jit(solution)/shard_map/ppermute | solution.py:484
  57.7 0.9 copy-start.5
  57.7 0.9 copy-start.6
  57.7 1.1 copy-start.7
  104.8 2.1 collective-permute-start.3
  107.0 24.7 %copy-start.4 = (f32[1024]{0:T(1024)S(1)}, f32[1024]{0:T(1024)}, u32[]{:S(2)}) copy-start(f32[1024]{0:T(1024)} %param.19) | copy-start | bytes 12292
  107.1 23.3 %collective-permute-start.4 = (bf16[144,2048]{1,0:T(8,128)(2,1)S(1)}, bf16[144,2048]{1,0:T(8,128)(2,1)S(1)}, u32[]{:S(2)}, u32[]{:S(2)}) collective-permute-start(bf16[144,2048]{1,0:T(8,128)(2,1)S(1)} %pad_maximum_fusion.2), channel_id=1, source_target_pairs={{4,12},{12,20},{20,28},{8,0},{16,8},{24,16},{5,13},{13,21},{21,29}... | collective-permute-start | bytes 1769480 | tf_op jit(solution)/shard_map/ppermute | solution.py:446
  108.4 22.0 %collective-permute-start.5 = (bf16[144,2048]{1,0:T(8,128)(2,1)S(1)}, bf16[144,2048]{1,0:T(8,128)(2,1)S(1)}, u32[]{:S(2)}, u32[]{:S(2)}) collective-permute-start(bf16[144,2048]{1,0:T(8,128)(2,1)S(1)} %pad_maximum_fusion.2), channel_id=1, source_target_pairs={{4,20},{12,28},{16,0},{24,8},{5,21},{13,29},{17,1},{25,9},{6,22},{... | collective-permute-start | bytes 1769480 | tf_op jit(solution)/shard_map/ppermute | solution.py:446
  109.7 21.7 %collective-permute-start.6 = (bf16[144,2048]{1,0:T(8,128)(2,1)S(1)}, bf16[144,2048]{1,0:T(8,128)(2,1)S(1)}, u32[]{:S(2)}, u32[]{:S(2)}) collective-permute-start(bf16[144,2048]{1,0:T(8,128)(2,1)S(1)} %pad_maximum_fusion.2), channel_id=1, source_target_pairs={{4,28},{24,0},{5,29},{25,1},{6,30},{26,2},{7,31},{27,3}} | collective-permute-start | bytes 1769480 | tf_op jit(solution)/shard_map/ppermute | solution.py:446
  131.7 48.3 %collective-permute-start.7 = (bf16[128,2048]{1,0:T(8,128)(2,1)S(1)}, bf16[128,2048]{1,0:T(8,128)(2,1)S(1)}, u32[]{:S(2)}, u32[]{:S(2)}) collective-permute-start(bf16[128,2048]{1,0:T(8,128)(2,1)S(1)} %fusion.5), channel_id=1, source_target_pairs={{0,4},{4,0},{8,12},{12,8},{16,20},{20,16},{24,28},{28,24},{1,5},{5... | collective-permute-start | bytes 1572872 | tf_op jit(solution)/shard_map/ppermute | solution.py:449
  131.8 60.0 %collective-permute-start.10 = (f32[1024]{0:T(1024)S(1)}, f32[1024]{0:T(1024)S(1)}, u32[]{:S(2)}, u32[]{:S(2)}) collective-permute-start(f32[1024]{0:T(1024)S(1)} %copy-done.4), channel_id=1, source_target_pairs={{0,1},{1,0},{2,3},{3,2},{4,5},{5,4},{6,7},{7,6},{8,9},{9,8},{10,11... | collective-permute-start | bytes 12296 | tf_op jit(solution)/shard_map/ppermute | solution.py:539
  190.8 4.8 %collective-permute-start.9 = (f32[8,512]{1,0:T(8,128)}, f32[8,512]{1,0:T(8,128)S(1)}, u32[]{:S(2)}, u32[]{:S(2)}) collective-permute-start(f32[8,512]{1,0:T(8,128)} %get-tuple-element.28.refs_0_), channel_id=1, source_target_pairs={{0,2},{1,3},{2,0},{3,1},{4,6},{5,7},{6,4},{7,5},{8,10},{9,11},{10,... | collective-permute-start | bytes 49160 | tf_op jit(solution)/shard_map/ppermute | solution.py:457
  195.7 0.6 copy-start.3
  205.1 15.6 %collective-permute-start.12 = (bf16[256,1024]{1,0:T(8,128)(2,1)S(1)}, bf16[256,1024]{1,0:T(8,128)(2,1)S(1)}, u32[]{:S(2)}, u32[]{:S(2)}) collective-permute-start(bf16[256,1024]{1,0:T(8,128)(2,1)S(1)} %get-tuple-element.33), channel_id=1, source_target_pairs={{1,2},{2,1},{5,6},{6,5},{9,10},{10,9},{13,14},{14,13},{17,18},{18,... | collective-permute-start | bytes 1572872 | tf_op jit(solution)/shard_map/ppermute | solution.py:500
  205.8 27.2 %collective-permute-start.13 = (bf16[256,1024]{1,0:T(8,128)(2,1)S(1)}, bf16[256,1024]{1,0:T(8,128)(2,1)S(1)}, u32[]{:S(2)}, u32[]{:S(2)}) collective-permute-start(bf16[256,1024]{1,0:T(8,128)(2,1)S(1)} %get-tuple-element.34), channel_id=1, source_target_pairs={{0,1},{1,3},{2,0},{3,2},{4,5},{5,7},{6,4},{7,6},{8,9},{9,11},{10,8... | collective-permute-start | bytes 1572872 | tf_op jit(solution)/shard_map/ppermute | solution.py:500
  217.5 16.0 %collective-permute-start.14 = (bf16[256,1024]{1,0:T(8,128)(2,1)S(1)}, bf16[256,1024]{1,0:T(8,128)(2,1)}, u32[]{:S(2)}, u32[]{:S(2)}) collective-permute-start(bf16[256,1024]{1,0:T(8,128)(2,1)S(1)} %get-tuple-element.35), channel_id=1, source_target_pairs={{1,2},{2,1},{5,6},{6,5},{9,10},{10,9},{13,14},{14,13},{17,18},{18,... | collective-permute-start | bytes 1572872 | tf_op jit(solution)/shard_map/ppermute | solution.py:500
  219.0 34.9 %collective-permute-start.15 = (bf16[256,1024]{1,0:T(8,128)(2,1)S(1)}, bf16[256,1024]{1,0:T(8,128)(2,1)}, u32[]{:S(2)}, u32[]{:S(2)}) collective-permute-start(bf16[256,1024]{1,0:T(8,128)(2,1)S(1)} %get-tuple-element.36), channel_id=1, source_target_pairs={{0,1},{1,3},{2,0},{3,2},{4,5},{5,7},{6,4},{7,6},{8,9},{9,11},{10,8... | collective-permute-start | bytes 1572872 | tf_op jit(solution)/shard_map/ppermute | solution.py:500
Sparse Core Ops, SparseCore 0:
  23.6 37.9 all-gather.3
  63.5 36.5 all-gather.5
  102.0 42.2 all-gather.7

commit v2 on v1

--- a/solution.py
+++ b/solution.py
@@ -13,6 +13,7 @@
 CHUNK = 128
 LANES = 128
 REV = 256
+TILE = 512
 KEEP_ROWS = 16
 PIECES = 2
 
@@ -51,15 +52,19 @@
     return total
 
 
-def expander(width):
-    row, col = iota((2 * LANES, width), 0), iota((2 * LANES, width), 1)
+def expander(width, first=0):
+    row, col = iota((2 * LANES, width), 0), first + iota((2 * LANES, width), 1)
     return ((row % LANES) == (col // HEAD_DIM)).astype(f32).astype(bf16)
 
 
-def expand(w, spread):
+def halves(w):
     high = w.astype(bf16)
     low = (w - high.astype(f32)).astype(bf16)
-    return mm(jnp.concatenate([high, low], axis=1), spread)
+    return jnp.concatenate([high, low], axis=1)
+
+
+def expand(w, spread):
+    return mm(halves(w), spread)
 
 
 def full(shape):
@@ -134,18 +139,29 @@
     ]
 
 
-def project(x, weights):
+def gates_kernel(x_ref, wa_ref, wb_ref, out_ref):
+    first = pl.program_id(0) < pl.num_programs(0) // 2
+
+    def activate(w_ref):
+        gate = mm(x_ref[...], w_ref[...]).astype(bf16).astype(f32)
+        out_ref[...] = (gate * jax.nn.sigmoid(gate)).astype(bf16)
+
+    pl.when(first)(lambda: activate(wa_ref))
+    pl.when(jnp.logical_not(first))(lambda: activate(wb_ref))
+
+
+def activated_gates(x, weights):
     tokens, half = x.shape
     cols = weights[0].shape[1]
-    tile = min(256, cols)
+    tile = min(TILE, cols)
     steps = cols // tile
     return pl.pallas_call(
-        two_weights,
+        gates_kernel,
         grid=(2 * steps,),
         in_specs=[full(x.shape)] + weight_specs(half, tile, steps),
         out_specs=pl.BlockSpec((tokens, tile), lambda j: (0, j)),
         out_shape=jax.ShapeDtypeStruct((tokens, 2 * cols), bf16),
-        name="project",
+        name="activated_gates",
     )(x, *weights)
 
 
@@ -153,7 +169,7 @@
     slots, pieces = len(routes[0]), len(routes[0][0])
     tokens = xs[0].shape[0] * pieces
     half, cols = weights[0].shape
-    tile = min(256, cols)
+    tile = min(TILE, cols)
     steps = cols // tile
     return pl.pallas_call(
         functools.partial(norm_project_kernel, routes),
@@ -185,16 +201,53 @@
 def states_kernel(
     starts_ref, base_ref, control_ref, values_ref, par_ref,
     total_ref, pre_ref, cola_ref, colb_ref, rowf_ref, rowb_ref, reach_ref,
+    weights_ref, keeps_ref,
 ):
     tokens, cols = values_ref.shape
     chunks = tokens // CHUNK
-    heads = cols // HEAD_DIM
+    j = pl.program_id(0)
+
+    @pl.when(j == 0)
+    def _():
+        step_terms(
+            starts_ref, base_ref, control_ref, par_ref,
+            cola_ref, colb_ref, rowf_ref, rowb_ref, reach_ref, weights_ref, keeps_ref,
+        )
+
+    tile = 256
+    for at in range(0, cols, tile):
+        lanes = slice(at, at + tile)
+        spread = expander(tile, j * cols + at)
+        lifted = mm(keeps_ref[...], spread)
+        wide = values_ref[:, lanes].astype(f32)
+        for d, order in enumerate((range(chunks), range(chunks - 1, -1, -1))):
+            scaled = (wide * mm(weights_ref[d], spread)).astype(bf16)
+            state = jnp.zeros((STATE, tile), f32)
+            for i, k in enumerate(order):
+                rows = slice(k * CHUNK, (k + 1) * CHUNK)
+                pre_ref[d, k, :, lanes] = state.astype(bf16)
+                line = d * (chunks + 1) + i
+                state = lifted[line : line + 1] * state + mm_tn(
+                    control_ref[rows, :STATE], scaled[rows]
+                )
+            total_ref[d, :STATE, lanes] = state.astype(bf16)
+            line = d * (chunks + 1) + chunks
+            total_ref[d, STATE:, lanes] = jnp.broadcast_to(
+                lifted[line : line + 1], (KEEP_ROWS, tile)
+            ).astype(bf16)
+
+
+def step_terms(
+    starts_ref, base_ref, control_ref, par_ref,
+    cola_ref, colb_ref, rowf_ref, rowb_ref, reach_ref, weights_ref, keeps_ref,
+):
+    tokens = control_ref.shape[0]
+    chunks, heads = rowf_ref.shape[:2]
     base = base_ref[0]
-    spread = expander(cols)
     row, col = iota((CHUNK, CHUNK), 0), iota((CHUNK, CHUNK), 1)
     tri = (row >= col).astype(f32)
     seg_at = lambda offset: segment_of(base + jnp.full((1, 1), offset, jnp.int32), starts_ref)
-    pieces = []
+    small, weights = [], [[], []]
     for k in range(chunks):
         rows = slice(k * CHUNK, (k + 1) * CHUNK)
         raw = control_ref[rows, 2 * STATE :].astype(f32) + par_ref[0:1, :]
@@ -211,35 +264,30 @@
         seg = segment_of(base + k * CHUNK + iota((CHUNK, 1), 0), starts_ref)
         first, last = seg_at(k * CHUNK), seg_at((k + 1) * CHUNK - 1)
         prior, after = seg_at(k * CHUNK - 1), seg_at((k + 1) * CHUNK)
-        w_f = jnp.where(seg == last, step * jnp.exp(whole - cum), 0.0)
-        w_b = jnp.where(seg == first, step * jnp.exp(before), 0.0)
-        b_in = control_ref[rows, :STATE]
-        wide = values_ref[rows, :].astype(f32)
-        add_f = mm_tn(b_in, (wide * expand(w_f, spread)).astype(bf16))
-        add_b = mm_tn(b_in, (wide * expand(w_b, spread)).astype(bf16))
+        weights[0].append(jnp.where(seg == last, step * jnp.exp(whole - cum), 0.0))
+        weights[1].append(jnp.where(seg == first, step * jnp.exp(before), 0.0))
         keep = jnp.exp(whole)
-        keep_f = jnp.where(prior == last, keep, 0.0)
-        keep_b = jnp.where(first == after, keep, 0.0)
-        pieces.append((seg, cum, before, whole, add_f, add_b, keep_f, keep_b))
-    lift = lambda w: expand(jnp.broadcast_to(w, (8, LANES)), spread)[0:1]
-    for d, order in enumerate((range(chunks), range(chunks - 1, -1, -1))):
-        state = jnp.zeros((STATE, cols), f32)
+        keeps = (jnp.where(prior == last, keep, 0.0), jnp.where(first == after, keep, 0.0))
+        small.append((seg, cum, whole - before, whole, keeps))
+    keep_rows = []
+    orders = (range(chunks), range(chunks - 1, -1, -1))
+    for d, order in enumerate(orders):
         keep_all = jnp.ones((1, LANES), f32)
         shift = jnp.zeros((1, LANES), f32)
         edge = seg_at(-1) if d == 0 else seg_at(tokens)
         for k in order:
-            seg, cum, before, whole, add_f, add_b, keep_f, keep_b = pieces[k]
-            pre_ref[d, k] = state.astype(bf16)
-            add, keep = (add_f, keep_f) if d == 0 else (add_b, keep_b)
-            inner = cum if d == 0 else whole - before
+            seg, whole = small[k][0], small[k][3]
             reach_ref[d, k * CHUNK : (k + 1) * CHUNK, :] = jnp.where(
-                seg == edge, jnp.exp(inner + shift), 0.0
+                seg == edge, jnp.exp(small[k][1 + d] + shift), 0.0
             )
-            state = lift(keep) * state + add
-            keep_all = keep_all * keep
+            keep_rows.append(small[k][4][d])
+            keep_all = keep_all * small[k][4][d]
             shift = shift + whole
-        total_ref[d, :STATE] = state.astype(bf16)
-        total_ref[d, STATE:] = jnp.broadcast_to(lift(keep_all), (KEEP_ROWS, cols)).astype(bf16)
+        keep_rows.append(keep_all)
+    padding = keeps_ref.shape[0] - len(keep_rows)
+    keeps_ref[...] = halves(jnp.concatenate(keep_rows + [jnp.zeros((padding, LANES), f32)], axis=0))
+    for d in range(2):
+        weights_ref[d] = halves(jnp.concatenate(weights[d], axis=0))
 
 
 def chunk_states(starts, base, control, values, par):
@@ -254,12 +302,25 @@
         ((chunks, heads, CHUNK), f32),
         ((2, tokens, LANES), f32),
     ]
+    steps = 2 if cols % 512 == 0 else 1
+    width = cols // steps
+    specs = [
+        pl.BlockSpec((2, STATE + KEEP_ROWS, width), lambda j: (0, 0, j)),
+        pl.BlockSpec((2, chunks, STATE, width), lambda j: (0, 0, 0, j)),
+    ] + [full(shape) for shape, _ in shapes[2:]]
     return pl.pallas_call(
         states_kernel,
-        grid=(1,),
-        in_specs=[SMEM, SMEM, full(control.shape), full(values.shape), full(par.shape)],
-        out_specs=[full(s) for s, _ in shapes],
+        grid=(steps,),
+        in_specs=[
+            SMEM, SMEM, full(control.shape), pl.BlockSpec((tokens, width), lambda j: (0, j)),
+            full(par.shape),
+        ],
+        out_specs=specs,
         out_shape=[jax.ShapeDtypeStruct(s, t) for s, t in shapes],
+        scratch_shapes=[
+            pltpu.VMEM((2, tokens, 2 * LANES), bf16),
+            pltpu.VMEM((-(-2 * (chunks + 1) // 16) * 16, 2 * LANES), bf16),
+        ],
         name="chunk_states",
     )(starts, base, control, values, par)
 
@@ -268,10 +329,23 @@
     starts_ref, base_ref, control_ref, values_ref, skip_ref,
     pre_ref, cola_ref, colb_ref, rowf_ref, rowb_ref, out_ref,
 ):
+    per_step = values_ref.shape[0] // CHUNK
+    spread = expander(values_ref.shape[1])
+    for i in range(per_step):
+        rows = pl.ds(i * CHUNK, CHUNK)
+        start = base_ref[0] + (pl.program_id(0) * per_step + i) * CHUNK
+        within_chunk(
+            starts_ref, start, control_ref.at[rows], values_ref.at[rows], skip_ref,
+            pre_ref.at[:, pl.ds(i, 1)], cola_ref.at[rows], colb_ref.at[rows],
+            rowf_ref.at[pl.ds(i, 1)], rowb_ref.at[pl.ds(i, 1)], out_ref.at[:, rows], spread,
+        )
+
+
+def within_chunk(
+    starts_ref, start, control_ref, values_ref, skip_ref,
+    pre_ref, cola_ref, colb_ref, rowf_ref, rowb_ref, out_ref, spread,
+):
     cols = values_ref.shape[1]
-    k = pl.program_id(0)
-    start = base_ref[0] + k * CHUNK
-    spread = expander(cols)
     row, col = iota((CHUNK, CHUNK), 0), iota((CHUNK, CHUNK), 1)
     low_lanes = iota((CHUNK, LANES), 1) < HEAD_DIM
     b_in, c_out = control_ref[:, :STATE], control_ref[:, STATE : 2 * STATE]
@@ -313,115 +387,152 @@
         )
         near = mm(left, right)
         direct = value.astype(f32) * skip_ref[:, lanes]
-        out_ref[0, :, lanes] = near[:CHUNK] + carry_f[:, lanes] + direct
-        out_ref[1, :, lanes] = near[CHUNK:] + carry_b[:, lanes] + direct
+        out_ref[0, :, lanes] = (near[:CHUNK] + carry_f[:, lanes] + direct).astype(bf16)
+        out_ref[1, :, lanes] = (near[CHUNK:] + carry_b[:, lanes] + direct).astype(bf16)
 
 
 def within(starts, base, control, values, skip_row, pre, cola, colb, rowf, rowb):
     tokens, cols = values.shape
     chunks, heads = tokens // CHUNK, cols // HEAD_DIM
-    rows = lambda width: pl.BlockSpec((CHUNK, width), lambda k: (k, 0))
+    n = 1
+    rows = lambda width: pl.BlockSpec((n * CHUNK, width), lambda k: (k, 0))
     return pl.pallas_call(
         within_kernel,
-        grid=(chunks,),
+        grid=(chunks // n,),
         in_specs=[
             SMEM, SMEM,
             rows(control.shape[1]), rows(cols), full(skip_row.shape),
-            pl.BlockSpec((2, 1, STATE, cols), lambda k: (0, k, 0, 0)),
+            pl.BlockSpec((2, n, STATE, cols), lambda k: (0, k, 0, 0)),
             rows(LANES), rows(LANES),
-            pl.BlockSpec((1, heads, CHUNK), lambda k: (k, 0, 0)),
-            pl.BlockSpec((1, heads, CHUNK), lambda k: (k, 0, 0)),
-        ],
-        out_specs=pl.BlockSpec((2, CHUNK, cols), lambda k: (0, k, 0)),
-        out_shape=jax.ShapeDtypeStruct((2, tokens, cols), f32),
+            pl.BlockSpec((n, heads, CHUNK), lambda k: (k, 0, 0)),
+            pl.BlockSpec((n, heads, CHUNK), lambda k: (k, 0, 0)),
+        ],
+        out_specs=pl.BlockSpec((2, n * CHUNK, cols), lambda k: (0, k, 0)),
+        out_shape=jax.ShapeDtypeStruct((2, tokens, cols), bf16),
         name="within_chunk",
     )(starts, base, control, values, skip_row, pre, cola, colb, rowf, rowb)
 
 
-def gate_kernel(control_ref, near_ref, into_ref, reach_ref, gates_ref, out_ref, squares_ref):
-    cols = gates_ref.shape[1]
-    spread = expander(cols)
-    c_out = control_ref[:, STATE : 2 * STATE]
-    gate = gates_ref[...].astype(f32)
-    active = gate * jax.nn.sigmoid(gate)
-    lane = iota((CHUNK, LANES), 1)
-    squares = jnp.zeros((CHUNK, LANES), f32)
+def gate_kernel(control_ref, near_ref, into_ref, reach_ref, active_ref, out_ref, squares_ref, acc):
+    tile = active_ref.shape[1]
+    rows = active_ref.shape[0]
+    j = pl.program_id(0)
+    spread = expander(tile, j * tile)
+    c_out = control_ref[...]
+    active = active_ref[...].astype(f32)
+    lane = iota((rows, LANES), 1)
+    total = jnp.where(j == 0, 0.0, acc[...])
     for d in range(2):
         carry = mm(c_out, into_ref[d]) * expand(reach_ref[d], spread)
-        y = (near_ref[d] + carry).astype(bf16).astype(f32)
-        v = y * active
-        squares = jnp.where(lane == d, jnp.sum(v * v, axis=1, keepdims=True), squares)
+        v = (near_ref[d].astype(f32) + carry) * active
+        total = total + jnp.where(lane == d, jnp.sum(v * v, axis=1, keepdims=True), 0.0)
         out_ref[d] = v.astype(bf16)
-    squares_ref[...] = jnp.transpose(squares)[:8]
-
-
-def carry_gate(control, near, into, reach, gates):
-    tokens, cols = gates.shape
-    rows = lambda width: pl.BlockSpec((CHUNK, width), lambda k: (k, 0))
-    both = lambda width: pl.BlockSpec((2, CHUNK, width), lambda k: (0, k, 0))
+    acc[...] = total
+
+    @pl.when(j == pl.num_programs(0) - 1)
+    def _():
+        squares_ref[...] = jnp.transpose(acc[...])[:8]
+
+
+def carry_gate(control, near, into, reach, active, piece, pieces):
+    tokens, cols = active.shape
+    rows = tokens // pieces
+    tile = min(1024, cols)
     return pl.pallas_call(
         gate_kernel,
-        grid=(tokens // CHUNK,),
-        in_specs=[rows(control.shape[1]), both(cols), full(into.shape), both(LANES), rows(cols)],
-        out_specs=[both(cols), pl.BlockSpec((8, CHUNK), lambda k: (0, k))],
+        grid=(cols // tile,),
+        in_specs=[
+            pl.BlockSpec((rows, STATE), lambda j: (piece, 1)),
+            pl.BlockSpec((2, rows, tile), lambda j: (0, piece, j)),
+            pl.BlockSpec((2, STATE, tile), lambda j: (0, 0, j)),
+            pl.BlockSpec((2, rows, LANES), lambda j: (0, piece, 0)),
+            pl.BlockSpec((rows, tile), lambda j: (piece, j)),
+        ],
+        out_specs=[
+            pl.BlockSpec((2, rows, tile), lambda j: (0, 0, j)),
+            pl.BlockSpec((8, rows), lambda j: (0, 0)),
+        ],
         out_shape=[
-            jax.ShapeDtypeStruct((2, tokens, cols), bf16),
-            jax.ShapeDtypeStruct((8, tokens), f32),
-        ],
+            jax.ShapeDtypeStruct((2, rows, cols), bf16),
+            jax.ShapeDtypeStruct((8, rows), f32),
+        ],
+        scratch_shapes=[pltpu.VMEM((rows, LANES), f32)],
         name="carry_gate",
-    )(control, near, into, reach, gates)
-
-
-def output_kernel(inner, sums, mirror_ref, gated_ref, *refs):
+    )(control, near, into, reach, active)
+
+
+def split_mm(parity, x_ref, first, near_ref, far_ref):
+    rows = near_ref.shape[0]
+    cols = lambda half: pl.ds(pl.multiple_of(first + half * rows, rows), rows)
+    return mm(x_ref[:, cols(parity)], near_ref[...]) + mm(x_ref[:, cols(1 - parity)], far_ref[...])
+
+
+def output_kernel(inner, sums, place_ref, gated_ref, *refs):
     squares_refs = refs[:sums]
-    gain_ref, wa_ref, wb_ref, out_ref = refs[sums:]
-    squares = squares_refs[0][...]
-    for other in squares_refs[1:]:
-        squares = squares + other[...]
-    scale = lax.rsqrt(squares / inner + norm_eps)
-    scale = jnp.transpose(jnp.concatenate([scale, jnp.zeros((CHUNK - 8, CHUNK), f32)], axis=0))
-    gain = gain_ref[...]
-    combined = (
-        gated_ref[0].astype(f32) * scale[:, 0:1] * gain
-        + gated_ref[1].astype(f32) * scale[:, 1:2] * gain
-    ).astype(bf16)
+    gain_ref, wa_ref, near_ref, far_ref, out_ref, combined = refs[sums:]
+    rows, tile = out_ref.shape
+
+    @pl.when(pl.program_id(0) == 0)
+    def _():
+        squares = squares_refs[0][...]
+        for other in squares_refs[1:]:
+            squares = squares + other[...]
+        scale = lax.rsqrt(squares / inner + norm_eps)
+        scale = jnp.concatenate([scale, jnp.zeros((LANES - 8, rows), f32)], axis=0)
+        scale = jnp.transpose(scale)
+        combined[...] = (
+            (
+                gated_ref[0].astype(f32) * scale[:, 0:1]
+                + gated_ref[1].astype(f32) * scale[:, 1:2]
+            )
+            * gain_ref[...]
+        ).astype(bf16)
+
     cols = wa_ref.shape[0]
-    product = mm(combined[:, :cols], wa_ref[...]) + mm(combined[:, cols:], wb_ref[...])
-    product = product.astype(bf16)
-    slots, _, width = out_ref.shape
-    blocks, per_slot = slots * width // REV, width // REV
-
-    @pl.when(mirror_ref[0] == 0)
-    def _():
-        for j in range(slots):
-            out_ref[j] = product[:, j * width : (j + 1) * width]
-
-    @pl.when(mirror_ref[0] == 1)
+    product = mm(combined[:, :cols], wa_ref[...])
+    product = (product + split_mm(place_ref[2], combined, cols, near_ref, far_ref)).astype(bf16)
+
+    @pl.when(place_ref[0] == 0)
+    def _():
+        out_ref[...] = product
+
+    @pl.when(place_ref[0] == 1)
     def _():
         swap = exchange_matrix(jnp.int32(1))
-        for q in range(blocks):
-            j, at = divmod(blocks - 1 - q, per_slot)
-            out_ref[j, :, at * REV : (at + 1) * REV] = mm(
+        for q in range(tile // REV):
+            back = tile - (q + 1) * REV
+            out_ref[:, back : back + REV] = mm(
                 product[:, q * REV : (q + 1) * REV], swap
             ).astype(bf16)
 
 
-def output_project(inner, mirror, gated, squares, gain_row, weights, slots, piece, pieces):
-    _, tokens, cols = gated.shape
-    width = weights[0].shape[1] // slots
-    steps = tokens // CHUNK // pieces
-    at = lambda k: k + piece * steps
+def output_project(inner, place, gated, squares, gain_row, weights, slots):
+    _, rows, cols = gated.shape
+    width = weights[0].shape[1]
+    shard = width // slots
+    tile = min(TILE, shard)
+    steps, per_slot = width // tile, shard // tile
+
+    def column(j, place):
+        at = place[1] * per_slot + j
+        return 0, jnp.where(place[0] == 1, steps - 1 - at, at)
+
+    fixed = lambda shape: pl.BlockSpec(shape, lambda j, place: (0,) * len(shape))
     return pl.pallas_call(
         functools.partial(output_kernel, inner, len(squares)),
-        grid=(steps,),
-        in_specs=[SMEM, pl.BlockSpec((2, CHUNK, cols), lambda k: (0, at(k), 0))]
-        + [pl.BlockSpec((8, CHUNK), lambda k: (0, at(k))) for _ in squares]
-        + [full(gain_row.shape)]
-        + [full(w.shape) for w in weights],
-        out_specs=pl.BlockSpec((slots, CHUNK, width), lambda k: (0, k, 0)),
-        out_shape=jax.ShapeDtypeStruct((slots, tokens // pieces, width), bf16),
+        grid_spec=pltpu.PrefetchScalarGridSpec(
+            num_scalar_prefetch=1,
+            grid=(per_slot,),
+            in_specs=[fixed(gated.shape)]
+            + [fixed(part.shape) for part in squares]
+            + [fixed(gain_row.shape)]
+            + [pl.BlockSpec((w.shape[0], tile), column) for w in weights],
+            out_specs=pl.BlockSpec((rows, tile), lambda j, place: (0, j)),
+            scratch_shapes=[pltpu.VMEM((rows, cols), bf16)],
+        ),
+        out_shape=jax.ShapeDtypeStruct((rows, shard), bf16),
         name="output_project",
-    )(mirror, gated, *squares, gain_row, *weights)
+    )(place, gated, *squares, gain_row, *weights)
 
 
 def incoming_states(total):
@@ -492,22 +603,20 @@
     return routes, xs
 
 
-def reduce_strand(partial, count, rank):
-    slots = count // 2
-    total = 0.0
-    for turn, pairs in turns(count, True):
-        mine = lax.dynamic_index_in_dim(partial, (rank // 2 + turn) % slots, 0, False)
-        got = lax.ppermute(mine, "chan", pairs)
-        kept = shard_of(rank, turn, count) == rank
-        total = total + jnp.where(kept, mine, got).astype(f32)
-    return total.astype(bf16)
-
-
 def partner_weights(w, count):
     rows = w.shape[0] // lax.axis_size("seq")
     part = lax.dynamic_slice_in_dim(w, lax.axis_index("seq") * rows, rows, 0)
     part = lax.ppermute(part, "chan", [(i, i ^ 1) for i in range(count)])
     return lax.all_gather(part, "seq", axis=0, tiled=True)
+
+
+def partner_halves(w, count):
+    seq = lax.axis_size("seq")
+    rows = w.shape[0] // 2
+    part = lax.dynamic_slice_in_dim(w, lax.axis_index("seq") % 2 * rows, rows, 0)
+    near = lax.ppermute(part, "chan", [(i, i ^ 1) for i in range(count)])
+    far = lax.ppermute(near, "seq", [(i, i ^ 1) for i in range(seq)])
+    return near, far
 
 
 def local(
@@ -534,7 +643,7 @@
     routes, xs = gather_strand(hidden, chan_count)
     values_w = (w_values, partner_weights(w_values, chan_count))
     gates_w = (w_gates, partner_weights(w_gates, chan_count))
-    out_w = (w_out, partner_weights(w_out, chan_count))
+    out_w = (w_out, *partner_halves(w_out, chan_count))
     swap = [(i, i ^ 1) for i in range(chan_count)]
     gate_row = jnp.concatenate([gate_gain, lax.ppermute(gate_gain, "chan", swap)])[None]
     w_small = jnp.concatenate(
@@ -551,17 +660,27 @@
     )
     total, pre, cola, colb, rowf, rowb, reach = chunk_states(doc_starts, base, control, values, par)
     into = incoming_states(total)
-    gates = project(normed, gates_w)
-    near = within(doc_starts, base, control, values, skip_row, pre, cola, colb, rowf, rowb)
-    gated, squares = carry_gate(control, near, into, reach, gates)
-    sums = chan_parts(squares)
-    result = []
+    active = activated_gates(normed, gates_w)
+    near = within(
+        doc_starts, base, control, values, skip_row, pre, cola, colb, rowf, rowb
+    )
+    gated, sums = [], []
     for p in range(PIECES):
-        out = output_project(
-            cols * chan_count, mirror, gated, sums, gate_row, out_w, slots, p, PIECES
-        )
-        result.append(reduce_strand(out, chan_count, chan_rank))
-    return jnp.concatenate(result, axis=0)
+        v, squares = carry_gate(control, near, into, reach, active, p, PIECES)
+        gated.append(v)
+        sums.append(chan_parts(squares))
+    total = [0.0] * PIECES
+    for turn, pairs in reversed(list(turns(chan_count, True))):
+        place = [chan_rank % 2, (chan_rank // 2 + turn) % slots, seq_rank % 2]
+        place = jnp.stack(place).astype(jnp.int32)
+        kept = shard_of(chan_rank, turn, chan_count) == chan_rank
+        for p in range(PIECES):
+            part = output_project(
+                cols * chan_count, place, gated[p], sums[p], gate_row, out_w, slots
+            )
+            got = lax.ppermute(part, "chan", pairs)
+            total[p] = total[p] + jnp.where(kept, part, got).astype(f32)
+    return jnp.concatenate(total, axis=0).astype(bf16)
 
 
 def solution(mesh):

time: 264 us -> 281 us (1.064)
  the two profiles are of different devices: /device:TPU:0 before, /device:TPU:16 now
where the time goes in v2:
time: 281 us; the launch traced here: 280 us
  waiting for transfers between devices  142 us (51%)
  Pallas kernels  76.7 us (27%)
  starting transfers between devices  27 us (10%)
  between operations  13.8 us (5%)
  other arithmetic  12.1 us (4%)
  local copies, waits for them, and re-layouts  9.12 us (3%)
    ppermute x1, waiting for transfers between devices, partner_halves(): near = lax.ppermute(part, 'chan', [(i, i ^ 1) for i in range(count)])  44.9 us
    ppermute x2, waiting for transfers between devices, gather_strand(): lax.ppermute(hidden, 'chan', pairs)  40.3 us
    pallas_call x4, Pallas kernels, output_project(): pl.pallas_call(functools.partial(output_kernel, inner, len(squares)), gri...  24.1 us
    ppermute x2, waiting for transfers between devices, partner_weights(): part = lax.ppermute(part, 'chan', [(i, i ^ 1) for i in range(count)])  23.3 us
    ppermute x4, starting transfers between devices, local(): got = lax.ppermute(part, 'chan', pairs)  14.3 us
    pallas_call x1, Pallas kernels, norm_project(): pl.pallas_call(functools.partial(norm_project_kernel, routes), grid=(2 *...  13.7 us
    ppermute x4, waiting for transfers between devices, local(): got = lax.ppermute(part, 'chan', pairs)  12.4 us
    ppermute x3, waiting for transfers between devices, incoming_states(): got = lax.ppermute(pair, 'seq', hop)  11.1 us
  transfers between devices with their start and end apart: 20, of which 10 were waited for; matrix products, arithmetic and copies ran while one was open for 5% of the time, Pallas kernels for 25%

profile of v2, /device:TPU:16, one launch (start us, length us, event | category | flops | bytes accessed | tf_op | source)
XLA Modules:
  0.0 280.4 jit_solution(11235315270017768559)
XLA Ops:
  7.6 1.6 collective-permute-start.2
  9.3 12.1 %collective-permute-done.2 = bf16[256,1024]{1,0:T(8,128)(2,1)S(1)} collective-permute-done((bf16[256,1024]{1,0:T(8,128)(2,1)S(1)}, bf16[256,1024]{1,0:T(8,128)(2,1)S(1)}, u32[]{:S(2)}, u32[]{:S(2)}) %collective-permute-start.2) | collective-permute-done | bytes 524320 | tf_op jit(solution)/shard_map/ppermute | solution.py:609
  23.3 1.6 collective-permute-start.8
  25.0 11.2 %collective-permute-done.8 = bf16[256,1024]{1,0:T(8,128)(2,1)S(1)} collective-permute-done((bf16[256,1024]{1,0:T(8,128)(2,1)S(1)}, bf16[256,1024]{1,0:T(8,128)(2,1)S(1)}, u32[]{:S(2)}, u32[]{:S(2)}) %collective-permute-start.8) | collective-permute-done | bytes 524320 | tf_op jit(solution)/shard_map/ppermute | solution.py:609
  37.1 2.4 collective-permute-start
  43.4 1.3 fusion.1.refs_6_
  44.8 40.3 %collective-permute-done.refs_1_ = bf16[512,1024]{1,0:T(8,128)(2,1)} collective-permute-done((bf16[512,1024]{1,0:T(8,128)(2,1)}, bf16[512,1024]{1,0:T(8,128)(2,1)}, u32[]{:S(2)}, u32[]{:S(2)}) %collective-permute-start) | collective-permute-done | bytes 1048608 | tf_op jit(solution)/shard_map/ppermute | solution.py:595
  85.1 13.7 %norm_project.1 = (bf16[512,2048]{1,0:T(8,128)(2,1)}, bf16[512,2048]{1,0:T(8,128)(2,1)}, bf16[512,384]{1,0:T(8,128)(2,1)}) custom-call(s32[1]{0:T(128)} %bitcast.3.rank_ref, s32[1]{0:T(128)} %bitcast.mirror_ref, bf16[512,1024]{1,0:T(8,128)(2,1)} %refs_0_.1, bf16[512,1024]{1,0:T(8,128)(2,1)} %collective-permute-done.refs_1_, ...), custom_call_target="tpu_custom_call" | custom-call | tf_op jit(solution)/shard_map/norm_project/pallas_call | solution.py:174
  98.8 8.4 %chunk_states.1 = (bf16[2,144,2048]{2,1,0:T(8,128)(2,1)}, bf16[2,4,128,2048]{3,2,1,0:T(8,128)(2,1)}, f32[512,128]{1,0:T(8,128)}, f32[512,128]{1,0:T(8,128)}, f32...) custom-call(s32[4]{0:T(128)} %starts_ref.3, s32[1]{0:T(128)} %bitcast.5.base_ref, ...), custom_call_target="tpu_custom_call" | custom-call | tf_op jit(solution)/shard_map/chunk_states/pallas_call | solution.py:311
  107.2 1.3 broadcast_select_fusion
  108.6 1.7 constant_dynamic-slice_fusion
  113.5 44.9 %collective-permute-done.11.refs_4_ = bf16[512,2048]{1,0:T(8,128)(2,1)S(1)} collective-permute-done((bf16[512,2048]{1,0:T(8,128)(2,1)S(1)}, bf16[512,2048]{1,0:T(8,128)(2,1)S(1)}, u32[]{:S(2)}, u32[]{:S(2)}) %collective-permute-start.11) | collective-permute-done | bytes 2097184 | tf_op jit(solution)/shard_map/ppermute | solution.py:617
  158.4 1.5 collective-permute-start.6
  159.9 11.1 %collective-permute-done.6 = bf16[144,2048]{1,0:T(8,128)(2,1)S(1)} collective-permute-done((bf16[144,2048]{1,0:T(8,128)(2,1)S(1)}, bf16[144,2048]{1,0:T(8,128)(2,1)S(1)}, u32[]{:S(2)}, u32[]{:S(2)}) %collective-permute-start.6) | collective-permute-done | bytes 589856 | tf_op jit(solution)/shard_map/ppermute | solution.py:557
  174.7 9.9 %within_chunk.1.near_ref = bf16[2,512,2048]{2,1,0:T(8,128)(2,1)} custom-call(s32[4]{0:T(128)} %starts_ref.3, s32[1]{0:T(128)} %bitcast.5.base_ref, bf16[512,384]{1,0:T(8,128)(2,1)} %get-tuple-element.19.control_ref, bf16[512,2048]{1,0:T(8,128)(2,1)} %get-tuple-element.20.values_ref, f32[1,2048]{1,0:T(1,128)} %broadcast_in_dim_reshape.3.skip_ref, ...), custom_call_target="tpu_custom_call" | custom-call | tf_op jit(solution)/shard_map/within_chunk/pallas_call | solution.py:399
  184.6 9.5 %activated_gates.1.active_ref = bf16[512,2048]{1,0:T(8,128)(2,1)} custom-call(bf16[512,2048]{1,0:T(8,128)(2,1)} %get-tuple-element.28.x_ref, bf16[2048,1024]{1,0:T(8,128)(2,1)} %wa_ref.1, bf16[2048,1024]{1,0:T(8,128)(2,1)} %all-gather.5.cloned.1.call-done.wb_ref), custom_call_target="tpu_custom_call" | custom-call | tf_op jit(solution)/shard_map/activated_gates/pallas_call | solution.py:158
  194.2 1.8 select_bitcast_fusion.2
  197.1 4.9 %carry_gate.2 = (bf16[2,256,2048]{2,1,0:T(8,128)(2,1)}, f32[8,256]{1,0:T(8,128)}) custom-call(bf16[512,384]{1,0:T(8,128)(2,1)} %get-tuple-element.19.control_ref, bf16[2,512,2048]{2,1,0:T(8,128)(2,1)} %within_chunk.1.near_ref, bf16[2,128,2048]{2,1,0:T(8,128)(2,1)} %pad_maximum_fusion.into_ref, f32[2,512,128]{2,1,0:T(8,128)} %get-tuple-element.27.reach_ref, ...), custom_call_target="tpu_custom_call" | custom-call | tf_op jit(solution)/shard_map/carry_gate/pallas_call | solution.py:441
  202.0 1.6 collective-permute-start.9
  204.2 2.6 collective-permute-done.9.refs_1_
  207.4 6.0 %output_project.4 = bf16[256,1024]{1,0:T(8,128)(2,1)} custom-call(s32[3]{0:T(128)} %add_add_fusion.place_ref, bf16[2,256,2048]{2,1,0:T(8,128)(2,1)} %get-tuple-element.29.gated_ref, f32[8,256]{1,0:T(8,128)} %get-tuple-element.30.refs_0_, f32[8,256]{1,0:T(8,128)} %copy-done.10, f32[1,2048]{1,0:T(1,128)} %bitcast.35, bf16[1024,2048]{1,0:T(8,128)(2,1)} %refs_3_.7, ...), custom_call_target="tpu_custom_call" | custom-call | tf_op jit(solution)/shard_map/output_project/pallas_call | solution.py:521
  213.4 1.6 collective-permute-start.13
  215.0 6.0 %output_project.5 = bf16[256,1024]{1,0:T(8,128)(2,1)} custom-call(s32[3]{0:T(128)} %add_add_fusion.1.place_ref, bf16[2,256,2048]{2,1,0:T(8,128)(2,1)} %get-tuple-element.29.gated_ref, f32[8,256]{1,0:T(8,128)} %get-tuple-element.30.refs_0_, f32[8,256]{1,0:T(8,128)} %copy-done.10, f32[1,2048]{1,0:T(1,128)} %bitcast.36, bf16[1024,2048]{1,0:T(8,128)(2,1)} %refs_3_.7, ...), custom_call_target="tpu_custom_call" | custom-call | tf_op jit(solution)/shard_map/output_project/pallas_call | solution.py:521
  221.0 4.4 %collective-permute-start.14 = (bf16[256,1024]{1,0:T(8,128)(2,1)}, bf16[256,1024]{1,0:T(8,128)(2,1)S(1)}, u32[]{:S(2)}, u32[]{:S(2)}) collective-permute-start(bf16[256,1024]{1,0:T(8,128)(2,1)} %output_project.5), channel_id=1, source_target_pairs={{1,2},{2,1},{5,6},{6,5},{9,10},{10,9},{13,14},{14,13},{17,18},{18,... | collective-permute-start | bytes 1572872 | tf_op jit(solution)/shard_map/ppermute | solution.py:681
  225.4 4.9 %carry_gate.3 = (bf16[2,256,2048]{2,1,0:T(8,128)(2,1)}, f32[8,256]{1,0:T(8,128)}) custom-call(bf16[512,384]{1,0:T(8,128)(2,1)} %get-tuple-element.19.control_ref, bf16[2,512,2048]{2,1,0:T(8,128)(2,1)} %within_chunk.1.near_ref, bf16[2,128,2048]{2,1,0:T(8,128)(2,1)} %pad_maximum_fusion.into_ref, f32[2,512,128]{2,1,0:T(8,128)} %get-tuple-element.27.reach_ref, ...), custom_call_target="tpu_custom_call" | custom-call | tf_op jit(solution)/shard_map/carry_gate/pallas_call | solution.py:441
  230.3 6.9 %collective-permute-done.15.refs_1_ = f32[8,256]{1,0:T(8,128)S(1)} collective-permute-done((f32[8,256]{1,0:T(8,128)}, f32[8,256]{1,0:T(8,128)S(1)}, u32[]{:S(2)}, u32[]{:S(2)}) %collective-permute-start.15) | collective-permute-done | bytes 8224 | tf_op jit(solution)/shard_map/ppermute | solution.py:568
  237.8 6.0 %output_project.6 = bf16[256,1024]{1,0:T(8,128)(2,1)} custom-call(s32[3]{0:T(128)} %add_add_fusion.place_ref, bf16[2,256,2048]{2,1,0:T(8,128)(2,1)} %get-tuple-element.31.gated_ref, f32[8,256]{1,0:T(8,128)} %get-tuple-element.32.refs_0_, f32[8,256]{1,0:T(8,128)} %copy-done.11, f32[1,2048]{1,0:T(1,128)} %bitcast.37, bf16[1024,2048]{1,0:T(8,128)(2,1)} %refs_3_.7, ...), custom_call_target="tpu_custom_call" | custom-call | tf_op jit(solution)/shard_map/output_project/pallas_call | solution.py:521
  243.8 3.4 %collective-permute-start.16 = (bf16[256,1024]{1,0:T(8,128)(2,1)}, bf16[256,1024]{1,0:T(8,128)(2,1)}, u32[]{:S(2)}, u32[]{:S(2)}) collective-permute-start(bf16[256,1024]{1,0:T(8,128)(2,1)} %output_project.6), channel_id=1, source_target_pairs={{0,1},{1,3},{2,0},{3,2},{4,5},{5,7},{6,4},{7,6},{8,9},{9,11},{10,8... | collective-permute-start | bytes 1572872 | tf_op jit(solution)/shard_map/ppermute | solution.py:681
  247.3 6.0 %output_project.7 = bf16[256,1024]{1,0:T(8,128)(2,1)} custom-call(s32[3]{0:T(128)} %add_add_fusion.1.place_ref, bf16[2,256,2048]{2,1,0:T(8,128)(2,1)} %get-tuple-element.31.gated_ref, f32[8,256]{1,0:T(8,128)} %get-tuple-element.32.refs_0_, f32[8,256]{1,0:T(8,128)} %copy-done.11, f32[1,2048]{1,0:T(1,128)} %bitcast.38, bf16[1024,2048]{1,0:T(8,128)(2,1)} %refs_3_.7, ...), custom_call_target="tpu_custom_call" | custom-call | tf_op jit(solution)/shard_map/output_project/pallas_call | solution.py:521
  253.3 4.9 %collective-permute-start.17 = (bf16[256,1024]{1,0:T(8,128)(2,1)}, bf16[256,1024]{1,0:T(8,128)(2,1)}, u32[]{:S(2)}, u32[]{:S(2)}) collective-permute-start(bf16[256,1024]{1,0:T(8,128)(2,1)} %output_project.7), channel_id=1, source_target_pairs={{1,2},{2,1},{5,6},{6,5},{9,10},{10,9},{13,14},{14,13},{17,18},{18,... | collective-permute-start | bytes 1572872 | tf_op jit(solution)/shard_map/ppermute | solution.py:681
  259.0 12.0 %collective-permute-done.17 = bf16[256,1024]{1,0:T(8,128)(2,1)} collective-permute-done((bf16[256,1024]{1,0:T(8,128)(2,1)}, bf16[256,1024]{1,0:T(8,128)(2,1)}, u32[]{:S(2)}, u32[]{:S(2)}) %collective-permute-start.17) | collective-permute-done | bytes 524320 | tf_op jit(solution)/shard_map/ppermute | solution.py:681
  271.0 1.6 add_convert_fusion
  (92 shorter events, 19.3 us)
Async XLA Ops:
  6.5 78.5 %all-gather.3.cloned.1.call-start = ((), (), s32[]{:S(2)}) async-start(), calls=%async_computation | async-start | bytes 4718592 | tf_op jit(solution)/shard_map/all_gather | solution.py:610
  7.6 13.7 %collective-permute-start.2 = (bf16[256,1024]{1,0:T(8,128)(2,1)S(1)}, bf16[256,1024]{1,0:T(8,128)(2,1)S(1)}, u32[]{:S(2)}, u32[]{:S(2)}) collective-permute-start(bf16[256,1024]{1,0:T(8,128)(2,1)S(1)} %constant_dynamic-slice_fusion.4), channel_id=1, source_target_pairs={{0,1},{1,0},{2,3},{3,2},{4,5},{5,4},{6,7},{7,6},{8,9},{9,8},{10,11... | collective-permute-start | bytes 1572872 | tf_op jit(solution)/shard_map/ppermute | solution.py:609
  22.2 18.2 %slice-start = ((bf16[2048,320]{0,1:T(8,128)(2,1)}), bf16[2048,64]{0,1:T(8,128)(2,1)S(1)}, s32[]{:S(2)}) async-start(bf16[2048,320]{0,1:T(8,128)(2,1)} %param.15), calls=%async_computation.2 | async-start | bytes 524288 | tf_op jit(solution)/shard_map/slice | solution.py:650
  22.2 162.5 %all-gather.5.cloned.1.call-start = ((), (), s32[]{:S(2)}) async-start(), calls=%async_computation.1 | async-start | bytes 4718592 | tf_op jit(solution)/shard_map/all_gather | solution.py:610
  23.3 12.9 %collective-permute-start.8 = (bf16[256,1024]{1,0:T(8,128)(2,1)S(1)}, bf16[256,1024]{1,0:T(8,128)(2,1)S(1)}, u32[]{:S(2)}, u32[]{:S(2)}) collective-permute-start(bf16[256,1024]{1,0:T(8,128)(2,1)S(1)} %constant_dynamic-slice_fusion.1), channel_id=1, source_target_pairs={{0,1},{1,0},{2,3},{3,2},{4,5},{5,4},{6,7},{7,6},{8,9},{9,8},{10,11... | collective-permute-start | bytes 1572872 | tf_op jit(solution)/shard_map/ppermute | solution.py:609
  36.2 4.5 %slice-start.1 = ((bf16[2048,320]{0,1:T(8,128)(2,1)}), bf16[2048,256]{0,1:T(8,128)(2,1)S(1)}, s32[]{:S(2)}) async-start(bf16[2048,320]{0,1:T(8,128)(2,1)} %param.15), calls=%async_computation.3 | async-start | bytes 2097152 | tf_op jit(solution)/shard_map/slice | solution.py:650
  37.1 48.0 %collective-permute-start = (bf16[512,1024]{1,0:T(8,128)(2,1)}, bf16[512,1024]{1,0:T(8,128)(2,1)}, u32[]{:S(2)}, u32[]{:S(2)}) collective-permute-start(bf16[512,1024]{1,0:T(8,128)(2,1)} %refs_0_.1), channel_id=1, source_target_pairs={{2,1},{1,2},{6,5},{5,6},{10,9},{9,10},{14,13},{13,14},{18,17},{17,... | collective-permute-start | bytes 3145736 | tf_op jit(solution)/shard_map/ppermute | solution.py:595
  39.4 45.6 %collective-permute-start.1 = (bf16[512,1024]{1,0:T(8,128)(2,1)}, bf16[512,1024]{1,0:T(8,128)(2,1)}, u32[]{:S(2)}, u32[]{:S(2)}) collective-permute-start(bf16[512,1024]{1,0:T(8,128)(2,1)} %refs_0_.1), channel_id=1, source_target_pairs={{1,0},{3,1},{0,2},{2,3},{5,4},{7,5},{4,6},{6,7},{9,8},{11,9},{8,10... | collective-permute-start | bytes 3145736 | tf_op jit(solution)/shard_map/ppermute | solution.py:595
  40.4 1.1 copy-start.15
  108.5 2.1 collective-permute-start.3
  110.3 48.1 %collective-permute-start.11 = (bf16[512,2048]{1,0:T(8,128)(2,1)S(1)}, bf16[512,2048]{1,0:T(8,128)(2,1)S(1)}, u32[]{:S(2)}, u32[]{:S(2)}) collective-permute-start(bf16[512,2048]{1,0:T(8,128)(2,1)S(1)} %constant_dynamic-slice_fusion), channel_id=1, source_target_pairs={{0,1},{1,0},{2,3},{3,2},{4,5},{5,4},{6,7},{7,6},{8,9},{9,8},{10,11... | collective-permute-start | bytes 6291464 | tf_op jit(solution)/shard_map/ppermute | solution.py:617
  110.6 61.6 %copy-start.5 = (bf16[144,2048]{1,0:T(8,128)(2,1)}, bf16[144,2048]{1,0:T(8,128)(2,1)S(1)}, u32[]{:S(2)}) copy-start(bf16[144,2048]{1,0:T(8,128)(2,1)S(1)} %collective-permute-done.3) | copy-start | bytes 1769476
  110.8 61.4 %copy-start.12 = (f32[1024]{0:T(1024)S(1)}, f32[1024]{0:T(1024)}, u32[]{:S(2)}) copy-start(f32[1024]{0:T(1024)} %param.19) | copy-start | bytes 12292
  110.9 49.0 %collective-permute-start.4 = (bf16[144,2048]{1,0:T(8,128)(2,1)S(1)}, bf16[144,2048]{1,0:T(8,128)(2,1)S(1)}, u32[]{:S(2)}, u32[]{:S(2)}) collective-permute-start(bf16[144,2048]{1,0:T(8,128)(2,1)S(1)} %pad_maximum_fusion.2), channel_id=1, source_target_pairs={{4,12},{12,20},{20,28},{8,0},{16,8},{24,16},{5,13},{13,21},{21,29}... | collective-permute-start | bytes 1769480 | tf_op jit(solution)/shard_map/ppermute | solution.py:557
  112.2 47.8 %collective-permute-start.5 = (bf16[144,2048]{1,0:T(8,128)(2,1)S(1)}, bf16[144,2048]{1,0:T(8,128)(2,1)S(1)}, u32[]{:S(2)}, u32[]{:S(2)}) collective-permute-start(bf16[144,2048]{1,0:T(8,128)(2,1)S(1)} %pad_maximum_fusion.2), channel_id=1, source_target_pairs={{4,20},{12,28},{16,0},{24,8},{5,21},{13,29},{17,1},{25,9},{6,22},{... | collective-permute-start | bytes 1769480 | tf_op jit(solution)/shard_map/ppermute | solution.py:557
  158.4 26.2 %copy-start = (bf16[512,2048]{1,0:T(8,128)(2,1)}, bf16[512,2048]{1,0:T(8,128)(2,1)S(1)}, u32[]{:S(2)}) copy-start(bf16[512,2048]{1,0:T(8,128)(2,1)S(1)} %collective-permute-done.11.refs_4_) | copy-start | bytes 6291460
  158.4 45.8 %collective-permute-start.12 = (bf16[512,2048]{1,0:T(8,128)(2,1)S(1)}, bf16[512,2048]{1,0:T(8,128)(2,1)}, u32[]{:S(2)}, u32[]{:S(2)}) collective-permute-start(bf16[512,2048]{1,0:T(8,128)(2,1)S(1)} %collective-permute-done.11.refs_4_), channel_id=1, source_target_pairs={{0,4},{4,0},{8,12},{12,8},{16,20},{20,16},{24,28},{28,24},{1,5},{5... | collective-permute-start | bytes 6291464 | tf_op jit(solution)/shard_map/ppermute | solution.py:618
  158.4 12.7 %collective-permute-start.6 = (bf16[144,2048]{1,0:T(8,128)(2,1)S(1)}, bf16[144,2048]{1,0:T(8,128)(2,1)S(1)}, u32[]{:S(2)}, u32[]{:S(2)}) collective-permute-start(bf16[144,2048]{1,0:T(8,128)(2,1)S(1)} %pad_maximum_fusion.2), channel_id=1, source_target_pairs={{4,28},{24,0},{5,29},{25,1},{6,30},{26,2},{7,31},{27,3}} | collective-permute-start | bytes 1769480 | tf_op jit(solution)/shard_map/ppermute | solution.py:557
  159.9 12.3 %copy-start.6 = (bf16[144,2048]{1,0:T(8,128)(2,1)}, bf16[144,2048]{1,0:T(8,128)(2,1)S(1)}, u32[]{:S(2)}) copy-start(bf16[144,2048]{1,0:T(8,128)(2,1)S(1)} %collective-permute-done.5) | copy-start | bytes 1769476
  171.1 1.1 copy-start.7
  172.2 22.0 %collective-permute-start.7 = (bf16[128,2048]{1,0:T(8,128)(2,1)}, bf16[128,2048]{1,0:T(8,128)(2,1)S(1)}, u32[]{:S(2)}, u32[]{:S(2)}) collective-permute-start(bf16[128,2048]{1,0:T(8,128)(2,1)} %fusion.5), channel_id=1, source_target_pairs={{0,4},{4,0},{8,12},{12,8},{16,20},{20,16},{24,28},{28,24},{1,5},{5... | collective-permute-start | bytes 1572872 | tf_op jit(solution)/shard_map/ppermute | solution.py:560
  172.2 31.4 %collective-permute-start.10 = (f32[1024]{0:T(1024)S(1)}, f32[1024]{0:T(1024)S(1)}, u32[]{:S(2)}, u32[]{:S(2)}) collective-permute-start(f32[1024]{0:T(1024)S(1)} %copy-done.12), channel_id=1, source_target_pairs={{0,1},{1,0},{2,3},{3,2},{4,5},{5,4},{6,7},{7,6},{8,9},{9,8},{10,11... | collective-permute-start | bytes 12296 | tf_op jit(solution)/shard_map/ppermute | solution.py:648
  202.0 4.8 %collective-permute-start.9 = (f32[8,256]{1,0:T(8,128)}, f32[8,256]{1,0:T(8,128)S(1)}, u32[]{:S(2)}, u32[]{:S(2)}) collective-permute-start(f32[8,256]{1,0:T(8,128)} %get-tuple-element.30.refs_0_), channel_id=1, source_target_pairs={{0,2},{1,3},{2,0},{3,1},{4,6},{5,7},{6,4},{7,5},{8,10},{9,11},{10,... | collective-permute-start | bytes 24584 | tf_op jit(solution)/shard_map/ppermute | solution.py:568
  213.4 44.8 %collective-permute-start.13 = (bf16[256,1024]{1,0:T(8,128)(2,1)}, bf16[256,1024]{1,0:T(8,128)(2,1)S(1)}, u32[]{:S(2)}, u32[]{:S(2)}) collective-permute-start(bf16[256,1024]{1,0:T(8,128)(2,1)} %output_project.4), channel_id=1, source_target_pairs={{0,1},{1,3},{2,0},{3,2},{4,5},{5,7},{6,4},{7,6},{8,9},{9,11},{10,8... | collective-permute-start | bytes 1572872 | tf_op jit(solution)/shard_map/ppermute | solution.py:681
  221.0 37.2 %collective-permute-start.14 = (bf16[256,1024]{1,0:T(8,128)(2,1)}, bf16[256,1024]{1,0:T(8,128)(2,1)S(1)}, u32[]{:S(2)}, u32[]{:S(2)}) collective-permute-start(bf16[256,1024]{1,0:T(8,128)(2,1)} %output_project.5), channel_id=1, source_target_pairs={{1,2},{2,1},{5,6},{6,5},{9,10},{10,9},{13,14},{14,13},{17,18},{18,... | collective-permute-start | bytes 1572872 | tf_op jit(solution)/shard_map/ppermute | solution.py:681
  230.3 6.9 %collective-permute-start.15 = (f32[8,256]{1,0:T(8,128)}, f32[8,256]{1,0:T(8,128)S(1)}, u32[]{:S(2)}, u32[]{:S(2)}) collective-permute-start(f32[8,256]{1,0:T(8,128)} %get-tuple-element.32.refs_0_), channel_id=1, source_target_pairs={{0,2},{1,3},{2,0},{3,1},{4,6},{5,7},{6,4},{7,5},{8,10},{9,11},{10,... | collective-permute-start | bytes 24584 | tf_op jit(solution)/shard_map/ppermute | solution.py:568
  243.8 14.4 %copy-start.1 = (bf16[256,1024]{1,0:T(8,128)(2,1)S(1)}, bf16[256,1024]{1,0:T(8,128)(2,1)}, u32[]{:S(2)}) copy-start(bf16[256,1024]{1,0:T(8,128)(2,1)} %output_project.4) | copy-start | bytes 1572868
  243.8 14.4 %copy-start.2 = (bf16[256,1024]{1,0:T(8,128)(2,1)S(1)}, bf16[256,1024]{1,0:T(8,128)(2,1)}, u32[]{:S(2)}) copy-start(bf16[256,1024]{1,0:T(8,128)(2,1)} %output_project.5) | copy-start | bytes 1572868
  243.8 15.1 %collective-permute-start.16 = (bf16[256,1024]{1,0:T(8,128)(2,1)}, bf16[256,1024]{1,0:T(8,128)(2,1)}, u32[]{:S(2)}, u32[]{:S(2)}) collective-permute-start(bf16[256,1024]{1,0:T(8,128)(2,1)} %output_project.6), channel_id=1, source_target_pairs={{0,1},{1,3},{2,0},{3,2},{4,5},{5,7},{6,4},{7,6},{8,9},{9,11},{10,8... | collective-permute-start | bytes 1572872 | tf_op jit(solution)/shard_map/ppermute | solution.py:681
  253.3 17.7 %copy-start.3 = (bf16[256,1024]{1,0:T(8,128)(2,1)S(1)}, bf16[256,1024]{1,0:T(8,128)(2,1)}, u32[]{:S(2)}) copy-start(bf16[256,1024]{1,0:T(8,128)(2,1)} %output_project.6) | copy-start | bytes 1572868
  253.3 17.7 %copy-start.4 = (bf16[256,1024]{1,0:T(8,128)(2,1)S(1)}, bf16[256,1024]{1,0:T(8,128)(2,1)}, u32[]{:S(2)}) copy-start(bf16[256,1024]{1,0:T(8,128)(2,1)} %output_project.7) | copy-start | bytes 1572868
  253.3 17.7 %collective-permute-start.17 = (bf16[256,1024]{1,0:T(8,128)(2,1)}, bf16[256,1024]{1,0:T(8,128)(2,1)}, u32[]{:S(2)}, u32[]{:S(2)}) collective-permute-start(bf16[256,1024]{1,0:T(8,128)(2,1)} %output_project.7), channel_id=1, source_target_pairs={{1,2},{2,1},{5,6},{6,5},{9,10},{10,9},{13,14},{14,13},{17,18},{18,... | collective-permute-start | bytes 1572872 | tf_op jit(solution)/shard_map/ppermute | solution.py:681
  (6 other events, 4.6 us)
Sparse Core Ops, SparseCore 0:
  22.3 37.6 all-gather.2
  61.9 36.5 all-gather.4

commit v3 on v2

--- a/solution.py
+++ b/solution.py
@@ -15,7 +15,7 @@
 REV = 256
 TILE = 512
 KEEP_ROWS = 16
-PIECES = 2
+PIECES = (1, 1)
 
 
 norm_eps = 1e-05
@@ -77,7 +77,7 @@
 def norm_project_kernel(routes, rank_ref, mirror_ref, *refs):
     slots, pieces = len(routes[0]), len(routes[0][0])
     xs = refs[: 1 + max(at for by_slot in routes for row in by_slot for at in row)]
-    gain_ref, wa_ref, wb_ref, wc_ref, normed_ref, values_ref, control_ref, scr, held, sems = refs[
+    gain_ref, wv_ref, wc_ref, normed_ref, values_ref, control_ref, scr, held, sems = refs[
         len(xs) :
     ]
     half = normed_ref.shape[1]
@@ -117,68 +117,56 @@
             normed_ref[:, cols] = (scr[q].astype(f32) * scale * gain_ref[:, cols]).astype(bf16)
         control_ref[...] = mm(normed_ref[...], wc_ref[...]).astype(bf16)
 
-    two_weights(normed_ref, wa_ref, wb_ref, values_ref)
-
-
-def two_weights(x_ref, wa_ref, wb_ref, out_ref):
-    first = pl.program_id(0) < pl.num_programs(0) // 2
-
-    @pl.when(first)
-    def _():
-        out_ref[...] = mm(x_ref[...], wa_ref[...]).astype(bf16)
-
-    @pl.when(jnp.logical_not(first))
-    def _():
-        out_ref[...] = mm(x_ref[...], wb_ref[...]).astype(bf16)
-
-
-def weight_specs(half, tile, steps):
-    return [
-        pl.BlockSpec((half, tile), lambda j: (0, jnp.minimum(j, steps - 1))),
-        pl.BlockSpec((half, tile), lambda j: (0, jnp.maximum(j - steps, 0))),
-    ]
-
-
-def gates_kernel(x_ref, wa_ref, wb_ref, out_ref):
-    first = pl.program_id(0) < pl.num_programs(0) // 2
-
-    def activate(w_ref):
-        gate = mm(x_ref[...], w_ref[...]).astype(bf16).astype(f32)
-        out_ref[...] = (gate * jax.nn.sigmoid(gate)).astype(bf16)
-
-    pl.when(first)(lambda: activate(wa_ref))
-    pl.when(jnp.logical_not(first))(lambda: activate(wb_ref))
-
-
-def activated_gates(x, weights):
-    tokens, half = x.shape
+    values_ref[...] = mm(normed_ref[...], wv_ref[...]).astype(bf16)
+
+
+def column_half(x, weights, filled=None, activate=False, parity=None):
+    tokens, _ = x.shape
     cols = weights[0].shape[1]
     tile = min(TILE, cols)
     steps = cols // tile
+    first = 0 if filled is None else steps
+    scalars = [] if parity is None else [parity]
+    given = [] if filled is None else [filled]
+
+    def kernel(*refs):
+        x_ref, *w_refs, out_ref = refs[len(scalars) + len(given) :]
+        if scalars:
+            product = split_mm(refs[0][0], x_ref, 0, *w_refs)
+        else:
+            product = mm(x_ref[...], w_refs[0][...])
+        product = product.astype(bf16)
+        if activate:
+            gate = product.astype(f32)
+            product = (gate * jax.nn.sigmoid(gate)).astype(bf16)
+        out_ref[...] = product
+
     return pl.pallas_call(
-        gates_kernel,
-        grid=(2 * steps,),
-        in_specs=[full(x.shape)] + weight_specs(half, tile, steps),
-        out_specs=pl.BlockSpec((tokens, tile), lambda j: (0, j)),
+        kernel,
+        grid=(steps,),
+        in_specs=[SMEM for _ in scalars]
+        + [pl.BlockSpec(memory_space=pl.ANY) for _ in given]
+        + [full(x.shape)]
+        + [pl.BlockSpec((w.shape[0], tile), lambda j: (0, j)) for w in weights],
+        out_specs=pl.BlockSpec((tokens, tile), lambda j: (0, j + first)),
         out_shape=jax.ShapeDtypeStruct((tokens, 2 * cols), bf16),
-        name="activated_gates",
-    )(x, *weights)
-
-
-def norm_project(routes, xs, rank, mirror, gain, weights, w_control):
+        input_output_aliases={len(scalars): 0} if given else {},
+        name="column_half",
+    )(*scalars, *given, x, *weights)
+
+
+def norm_project(routes, xs, rank, mirror, gain, w_values, w_control):
     slots, pieces = len(routes[0]), len(routes[0][0])
     tokens = xs[0].shape[0] * pieces
-    half, cols = weights[0].shape
+    half, cols = w_values.shape
     tile = min(TILE, cols)
     steps = cols // tile
     return pl.pallas_call(
         functools.partial(norm_project_kernel, routes),
-        grid=(2 * steps,),
+        grid=(steps,),
         in_specs=[SMEM, SMEM]
         + [pl.BlockSpec(memory_space=pl.ANY) for x in xs]
-        + [full(gain.shape)]
-        + weight_specs(half, tile, steps)
-        + [full(w_control.shape)],
+        + [full(gain.shape), pl.BlockSpec((half, tile), lambda j: (0, j)), full(w_control.shape)],
         out_specs=[
             full((tokens, half)),
             pl.BlockSpec((tokens, tile), lambda j: (0, j)),
@@ -195,12 +183,12 @@
             pltpu.SemaphoreType.DMA((slots, pieces)),
         ],
         name="norm_project",
-    )(rank, mirror, *xs, gain, *weights, w_control)
+    )(rank, mirror, *xs, gain, w_values, w_control)
 
 
 def states_kernel(
-    starts_ref, base_ref, control_ref, values_ref, par_ref,
-    total_ref, pre_ref, cola_ref, colb_ref, rowf_ref, rowb_ref, reach_ref,
+    starts_ref, base_ref, parity_ref, control_ref, values_ref, par_ref,
+    mine_ref, send_ref, pre_ref, cola_ref, colb_ref, rowf_ref, rowb_ref, reach_ref,
     weights_ref, keeps_ref,
 ):
     tokens, cols = values_ref.shape
@@ -220,6 +208,7 @@
         spread = expander(tile, j * cols + at)
         lifted = mm(keeps_ref[...], spread)
         wide = values_ref[:, lanes].astype(f32)
+        totals = []
         for d, order in enumerate((range(chunks), range(chunks - 1, -1, -1))):
             scaled = (wide * mm(weights_ref[d], spread)).astype(bf16)
             state = jnp.zeros((STATE, tile), f32)
@@ -230,11 +219,12 @@
                 state = lifted[line : line + 1] * state + mm_tn(
                     control_ref[rows, :STATE], scaled[rows]
                 )
-            total_ref[d, :STATE, lanes] = state.astype(bf16)
             line = d * (chunks + 1) + chunks
-            total_ref[d, STATE:, lanes] = jnp.broadcast_to(
-                lifted[line : line + 1], (KEEP_ROWS, tile)
-            ).astype(bf16)
+            keep = jnp.broadcast_to(lifted[line : line + 1], (KEEP_ROWS, tile))
+            totals.append(jnp.concatenate([state, keep], axis=0))
+        late = parity_ref[0] == 1
+        mine_ref[:, lanes] = jnp.where(late, totals[0], totals[1]).astype(bf16)
+        send_ref[:, lanes] = jnp.where(late, totals[1], totals[0]).astype(bf16)
 
 
 def step_terms(
@@ -290,11 +280,12 @@
         weights_ref[d] = halves(jnp.concatenate(weights[d], axis=0))
 
 
-def chunk_states(starts, base, control, values, par):
+def chunk_states(starts, base, parity, control, values, par):
     tokens, cols = values.shape
     chunks, heads = tokens // CHUNK, cols // HEAD_DIM
     shapes = [
-        ((2, STATE + KEEP_ROWS, cols), bf16),
+        ((STATE + KEEP_ROWS, cols), bf16),
+        ((STATE + KEEP_ROWS, cols), bf16),
         ((2, chunks, STATE, cols), bf16),
         ((tokens, LANES), f32),
         ((tokens, LANES), f32),
@@ -305,14 +296,16 @@
     steps = 2 if cols % 512 == 0 else 1
     width = cols // steps
     specs = [
-        pl.BlockSpec((2, STATE + KEEP_ROWS, width), lambda j: (0, 0, j)),
+        pl.BlockSpec((STATE + KEEP_ROWS, width), lambda j: (0, j)),
+        pl.BlockSpec((STATE + KEEP_ROWS, width), lambda j: (0, j)),
         pl.BlockSpec((2, chunks, STATE, width), lambda j: (0, 0, 0, j)),
-    ] + [full(shape) for shape, _ in shapes[2:]]
+    ] + [full(shape) for shape, _ in shapes[3:]]
     return pl.pallas_call(
         states_kernel,
         grid=(steps,),
         in_specs=[
-            SMEM, SMEM, full(control.shape), pl.BlockSpec((tokens, width), lambda j: (0, j)),
+            SMEM, SMEM, SMEM, full(control.shape),
+            pl.BlockSpec((tokens, width), lambda j: (0, j)),
             full(par.shape),
         ],
         out_specs=specs,
@@ -322,7 +315,7 @@
             pltpu.VMEM((-(-2 * (chunks + 1) // 16) * 16, 2 * LANES), bf16),
         ],
         name="chunk_states",
-    )(starts, base, control, values, par)
+    )(starts, base, parity, control, values, par)
 
 
 def within_kernel(
@@ -413,7 +406,10 @@
     )(starts, base, control, values, skip_row, pre, cola, colb, rowf, rowb)
 
 
-def gate_kernel(control_ref, near_ref, into_ref, reach_ref, active_ref, out_ref, squares_ref, acc):
+def gate_kernel(
+    parity_ref, control_ref, near_ref, through_ref, across_ref, reach_ref, active_ref,
+    out_ref, squares_ref, acc,
+):
     tile = active_ref.shape[1]
     rows = active_ref.shape[0]
     j = pl.program_id(0)
@@ -423,7 +419,8 @@
     lane = iota((rows, LANES), 1)
     total = jnp.where(j == 0, 0.0, acc[...])
     for d in range(2):
-        carry = mm(c_out, into_ref[d]) * expand(reach_ref[d], spread)
+        state = jnp.where(parity_ref[0] + d == 1, through_ref[...], across_ref[...])
+        carry = mm(c_out, state) * expand(reach_ref[d], spread)
         v = (near_ref[d].astype(f32) + carry) * active
         total = total + jnp.where(lane == d, jnp.sum(v * v, axis=1, keepdims=True), 0.0)
         out_ref[d] = v.astype(bf16)
@@ -434,17 +431,19 @@
         squares_ref[...] = jnp.transpose(acc[...])[:8]
 
 
-def carry_gate(control, near, into, reach, active, piece, pieces):
-    tokens, cols = active.shape
-    rows = tokens // pieces
+def carry_gate(parity, control, near, into, reach, active, first, rows):
+    cols = active.shape[1]
+    piece = first // rows
     tile = min(1024, cols)
     return pl.pallas_call(
         gate_kernel,
         grid=(cols // tile,),
         in_specs=[
+            SMEM,
             pl.BlockSpec((rows, STATE), lambda j: (piece, 1)),
             pl.BlockSpec((2, rows, tile), lambda j: (0, piece, j)),
-            pl.BlockSpec((2, STATE, tile), lambda j: (0, 0, j)),
+            pl.BlockSpec((STATE, tile), lambda j: (0, j)),
+            pl.BlockSpec((STATE, tile), lambda j: (0, j)),
             pl.BlockSpec((2, rows, LANES), lambda j: (0, piece, 0)),
             pl.BlockSpec((rows, tile), lambda j: (piece, j)),
         ],
@@ -458,7 +457,7 @@
         ],
         scratch_shapes=[pltpu.VMEM((rows, LANES), f32)],
         name="carry_gate",
-    )(control, near, into, reach, active)
+    )(parity, control, near, *into, reach, active)
 
 
 def split_mm(parity, x_ref, first, near_ref, far_ref):
@@ -535,18 +534,16 @@
     )(place, gated, *squares, gain_row, *weights)
 
 
-def incoming_states(total):
+def incoming_states(mine, send):
     count = lax.axis_size("seq")
-    late = lax.axis_index("seq") % 2 == 1
     state = lambda m: m[:STATE].astype(f32)
     keep = lambda m: m[STATE : STATE + 1].astype(f32)
     swap = [(i, i ^ 1) for i in range(count)]
-    mine = jnp.where(late, total[0], total[1])
-    near = lax.ppermute(jnp.where(late, total[1], total[0]), "seq", swap)
+    near = lax.ppermute(send, "seq", swap)
     pair = jnp.concatenate(
         [
             keep(mine) * state(near) + state(mine),
-            jnp.broadcast_to(keep(mine) * keep(near), (KEEP_ROWS, total.shape[2])),
+            jnp.broadcast_to(keep(mine) * keep(near), (KEEP_ROWS, mine.shape[1])),
         ],
         axis=0,
     ).astype(bf16)
@@ -559,7 +556,7 @@
         decay = decay * keep(got)
     across = lax.ppermute(into.astype(bf16), "seq", swap)
     through = (keep(near) * into + state(near)).astype(bf16)
-    return jnp.stack([jnp.where(late, through, across), jnp.where(late, across, through)])
+    return through, across
 
 
 def chan_parts(part):
@@ -592,7 +589,9 @@
 
 def gather_strand(hidden, count):
     slots = count // 2
-    xs = [hidden] + [lax.ppermute(hidden, "chan", pairs) for _, pairs in turns(count, False)]
+    xs = [hidden]
+    for turn, pairs in turns(count, False):
+        xs.append(lax.ppermute(hidden, "chan", pairs))
     routes = []
     for rank in range(count):
         by_slot = [None] * slots
@@ -603,11 +602,38 @@
     return routes, xs
 
 
+def placed_kernel(chip_ref, *refs):
+    *parts, out_ref = refs
+    rows = parts[0].shape[0]
+    for k, part in enumerate(parts):
+        at = pl.multiple_of((chip_ref[0] ^ k) * rows, rows)
+        out_ref[pl.ds(at, rows), :] = part[...]
+
+
+def placed(chip, parts):
+    rows, cols = parts[0].shape
+    return pl.pallas_call(
+        placed_kernel,
+        in_specs=[SMEM] + [full(part.shape) for part in parts],
+        out_specs=full((rows * len(parts), cols)),
+        out_shape=jax.ShapeDtypeStruct((rows * len(parts), cols), bf16),
+        name="placed",
+    )(chip, *parts)
+
+
 def partner_weights(w, count):
-    rows = w.shape[0] // lax.axis_size("seq")
-    part = lax.dynamic_slice_in_dim(w, lax.axis_index("seq") * rows, rows, 0)
+    seq = lax.axis_size("seq")
+    place = lax.axis_index("seq")
+    chips = seq // 2
+    rows = w.shape[0] // seq
+    part = lax.dynamic_slice_in_dim(w, (place % 2 * chips + place // 2) * rows, rows, 0)
     part = lax.ppermute(part, "chan", [(i, i ^ 1) for i in range(count)])
-    return lax.all_gather(part, "seq", axis=0, tiled=True)
+    parts = [part]
+    for k in range(1, chips):
+        parts.append(lax.ppermute(part, "seq", [(i, i ^ (2 * k)) for i in range(seq)]))
+    near = placed(jnp.reshape(place // 2, (1,)).astype(jnp.int32), parts)
+    far = lax.ppermute(near, "seq", [(i, i ^ 1) for i in range(seq)])
+    return near, far
 
 
 def partner_halves(w, count):
@@ -641,9 +667,9 @@
 
     lanes = lambda a: jnp.pad(a, ((0, 0), (0, LANES - 2 * heads)))
     routes, xs = gather_strand(hidden, chan_count)
-    values_w = (w_values, partner_weights(w_values, chan_count))
-    gates_w = (w_gates, partner_weights(w_gates, chan_count))
-    out_w = (w_out, *partner_halves(w_out, chan_count))
+    values_w = partner_weights(w_values, chan_count)
+    gates_w = partner_halves(w_gates, chan_count)
+    out_w = (w_out, *partner_weights(w_out, chan_count))
     swap = [(i, i ^ 1) for i in range(chan_count)]
     gate_row = jnp.concatenate([gate_gain, lax.ppermute(gate_gain, "chan", swap)])[None]
     w_small = jnp.concatenate(
@@ -655,26 +681,32 @@
     skip_row = jnp.repeat(mine(skip_gain, 0), HEAD_DIM)[None]
     scalar = lambda v: jnp.reshape(v, (1,)).astype(jnp.int32)
     base, mirror = scalar(seq_rank * tokens), scalar(chan_rank % 2)
+    parity = scalar(seq_rank % 2)
     normed, values, control = norm_project(
-        routes, xs, scalar(chan_rank), mirror, norm_gain[None], values_w, w_small
+        routes, xs, scalar(chan_rank), mirror, norm_gain[None], w_values, w_small
     )
-    total, pre, cola, colb, rowf, rowb, reach = chunk_states(doc_starts, base, control, values, par)
-    into = incoming_states(total)
-    active = activated_gates(normed, gates_w)
+    values = column_half(normed, values_w, values, False, parity)
+    kept, send, pre, cola, colb, rowf, rowb, reach = chunk_states(
+        doc_starts, base, parity, control, values, par
+    )
+    into = incoming_states(kept, send)
+    active = column_half(normed, (w_gates,), None, True)
+    active = column_half(normed, gates_w, active, True, parity)
     near = within(
         doc_starts, base, control, values, skip_row, pre, cola, colb, rowf, rowb
     )
     gated, sums = [], []
-    for p in range(PIECES):
-        v, squares = carry_gate(control, near, into, reach, active, p, PIECES)
+    rows = [tokens * share // sum(PIECES) for share in PIECES]
+    for p in range(len(rows)):
+        v, squares = carry_gate(parity, control, near, into, reach, active, sum(rows[:p]), rows[p])
         gated.append(v)
         sums.append(chan_parts(squares))
-    total = [0.0] * PIECES
+    total = [0.0] * len(rows)
     for turn, pairs in reversed(list(turns(chan_count, True))):
         place = [chan_rank % 2, (chan_rank // 2 + turn) % slots, seq_rank % 2]
         place = jnp.stack(place).astype(jnp.int32)
         kept = shard_of(chan_rank, turn, chan_count) == chan_rank
-        for p in range(PIECES):
+        for p in range(len(rows)):
             part = output_project(
                 cols * chan_count, place, gated[p], sums[p], gate_row, out_w, slots
             )

time: 281 us -> 293 us (1.043)
  between operations: 13.8 us -> 0.32 us
  Pallas kernels: 76.7 us -> 86.2 us
  starting transfers between devices: 27 us -> 36.3 us
  local copies, waits for them, and re-layouts: 9.12 us -> 12.3 us
    ppermute x3 -> x11, waiting for transfers between devices: 40.4 us -> 86.5 us  [the longest x6 49.3 us: partner_weights(): lax.ppermute(part, 'seq', [(i, i ^ 2 * k) for i in range(seq)])]
    ppermute x1, waiting for transfers between devices: 44.9 us -> 0.01 us  [partner_halves(): near = lax.ppermute(part, 'chan', [(i, i ^ 1) for i in range(count)])]
    pallas_call x5 -> x9, Pallas kernels: 41.5 us -> 50.8 us  [the longest x3 17.1 us: column_half(): pl.pallas_call(kernel, grid=(steps,), in_specs=[SMEM for _ in scalars] +...]
    ppermute x3 -> x11, starting transfers between devices: 3.34 us -> 11.9 us  [the longest x6 8.7 us: partner_weights(): lax.ppermute(part, 'seq', [(i, i ^ 2 * k) for i in range(seq)])]
    ppermute x2, waiting for transfers between devices: 23.3 us -> 26.4 us  [partner_weights(): part = lax.ppermute(part, 'chan', [(i, i ^ 1) for i in range(count)])]
  transfers between devices with their start and end apart: 20 -> 26, of which waited for: 10 -> 12; matrix products, arithmetic and copies ran while one was open for 5% -> 6% of each run, Pallas kernels for 25% -> 26%
where the time goes in v3:
time: 293 us; the launch traced here: 292 us
  waiting for transfers between devices  144 us (49%)
  Pallas kernels  86.2 us (29%)
  starting transfers between devices  36.3 us (12%)
  other arithmetic  12.4 us (4%)
  local copies, waits for them, and re-layouts  12.3 us (4%)
    ppermute x6, waiting for transfers between devices, partner_weights(): lax.ppermute(part, 'seq', [(i, i ^ 2 * k) for i in range(seq)])  49.3 us
    ppermute x2, waiting for transfers between devices, gather_strand(): xs.append(lax.ppermute(hidden, 'chan', pairs))  37.1 us
    ppermute x2, waiting for transfers between devices, partner_weights(): part = lax.ppermute(part, 'chan', [(i, i ^ 1) for i in range(count)])  26.4 us
    pallas_call x4, Pallas kernels, output_project(): pl.pallas_call(functools.partial(output_kernel, inner, len(squares)), gri...  24.1 us
    pallas_call x3, Pallas kernels, column_half(): pl.pallas_call(kernel, grid=(steps,), in_specs=[SMEM for _ in scalars] +...  17.1 us
    ppermute x4, starting transfers between devices, local(): got = lax.ppermute(part, 'chan', pairs)  14.4 us
    ppermute x4, waiting for transfers between devices, local(): got = lax.ppermute(part, 'chan', pairs)  12.4 us
    pallas_call x1, Pallas kernels, within(): pl.pallas_call(within_kernel, grid=(chunks // n,), in_specs=[SMEM, SMEM,...  9.98 us
  transfers between devices with their start and end apart: 26, of which 12 were waited for; matrix products, arithmetic and copies ran while one was open for 6% of the time, Pallas kernels for 26%

profile of v3, /device:TPU:16, one launch (start us, length us, event | category | flops | bytes accessed | tf_op | source)
XLA Modules:
  0.0 291.7 jit_solution(9901332163769965451)
XLA Ops:
  2.7 12.1 %collective-permute-done.2.refs_0_ = bf16[256,1024]{1,0:T(8,128)(2,1)S(1)} collective-permute-done((bf16[256,1024]{1,0:T(8,128)(2,1)S(1)}, bf16[256,1024]{1,0:T(8,128)(2,1)S(1)}, u32[]{:S(2)}, u32[]{:S(2)}) %collective-permute-start.2) | collective-permute-done | bytes 524320 | tf_op jit(solution)/shard_map/ppermute | solution.py:630
  18.3 11.3 %collective-permute-done.3.refs_1_ = bf16[256,1024]{1,0:T(8,128)(2,1)S(1)} collective-permute-done((bf16[256,1024]{1,0:T(8,128)(2,1)S(1)}, bf16[256,1024]{1,0:T(8,128)(2,1)S(1)}, u32[]{:S(2)}, u32[]{:S(2)}) %collective-permute-start.3) | collective-permute-done | bytes 524320 | tf_op jit(solution)/shard_map/ppermute | solution.py:633
  29.6 10.5 %collective-permute-done.4.refs_2_ = bf16[256,1024]{1,0:T(8,128)(2,1)S(1)} collective-permute-done((bf16[256,1024]{1,0:T(8,128)(2,1)S(1)}, bf16[256,1024]{1,0:T(8,128)(2,1)S(1)}, u32[]{:S(2)}, u32[]{:S(2)}) %collective-permute-start.4) | collective-permute-done | bytes 524320 | tf_op jit(solution)/shard_map/ppermute | solution.py:633
  41.0 3.0 %placed.2.refs_3_ = bf16[1024,1024]{1,0:T(8,128)(2,1)} custom-call(s32[1]{0:T(128)} %bitcast.6.chip_ref, bf16[256,1024]{1,0:T(8,128)(2,1)} %copy-done.9, bf16[256,1024]{1,0:T(8,128)(2,1)} %copy-done.11, bf16[256,1024]{1,0:T(8,128)(2,1)} %copy-done.12, bf16[256,1024]{1,0:T(8,128)(2,1)} %copy-done.13), custom_call_target="tpu_custom_call" | custom-call | tf_op jit(solution)/shard_map/placed/pallas_call | solution.py:615
  44.0 2.3 collective-permute-start
  47.3 3.2 %constant_dynamic-slice_fusion.1 = bf16[1024,1024]{1,0:T(8,128)(2,1)} fusion(bf16[2048,1024]{1,0:T(8,128)(2,1)} %refs_1_.1, s32[]{:T(128)S(6)} %select_n.106), kind=kLoop, calls=%fused_computation.23 | loop fusion | bytes 4194308 | tf_op jit(solution)/shard_map/dynamic_slice | solution.py:642
  57.1 37.1 %collective-permute-done.refs_1_ = bf16[512,1024]{1,0:T(8,128)(2,1)} collective-permute-done((bf16[512,1024]{1,0:T(8,128)(2,1)}, bf16[512,1024]{1,0:T(8,128)(2,1)}, u32[]{:S(2)}, u32[]{:S(2)}) %collective-permute-start) | collective-permute-done | bytes 1048608 | tf_op jit(solution)/shard_map/ppermute | solution.py:594
  94.3 9.4 %norm_project.1 = (bf16[512,2048]{1,0:T(8,128)(2,1)}, bf16[512,2048]{1,0:T(8,128)(2,1)}, bf16[512,384]{1,0:T(8,128)(2,1)}) custom-call(s32[1]{0:T(128)} %bitcast.3.rank_ref, s32[1]{0:T(128)} %bitcast.mirror_ref, bf16[512,1024]{1,0:T(8,128)(2,1)} %refs_0_.1, bf16[512,1024]{1,0:T(8,128)(2,1)} %collective-permute-done.refs_1_, ...), custom_call_target="tpu_custom_call" | custom-call | tf_op jit(solution)/shard_map/norm_project/pallas_call | solution.py:164
  103.7 5.6 %column_half.3.values_ref = bf16[512,2048]{1,0:T(8,128)(2,1)} custom-call(s32[1]{0:T(128)} %bitcast.2.refs_0_.parity_ref, bf16[512,2048]{1,0:T(8,128)(2,1)} %get-tuple-element.21.refs_1_, bf16[512,2048]{1,0:T(8,128)(2,1)} %get-tuple-element.22.refs_2_.refs_0_, bf16[1024,1024]{1,0:T(8,128)(2,1)} %placed.2.refs_3_, ...), custom_call_target="tpu_custom_call", output_to_operand_aliasing={{}: (1, {})} | custom-call | tf_op jit(solution)/shard_map/column_half/pallas_call | solution.py:144
  109.3 8.5 %chunk_states.1 = (bf16[144,2048]{1,0:T(8,128)(2,1)}, bf16[144,2048]{1,0:T(8,128)(2,1)}, bf16[2,4,128,2048]{3,2,1,0:T(8,128)(2,1)}, f32[512,128]{1,0:T(8,128)}, ...) custom-call(s32[4]{0:T(128)} %starts_ref.3, s32[1]{0:T(128)} %bitcast.5.base_ref, ...), custom_call_target="tpu_custom_call" | custom-call | tf_op jit(solution)/shard_map/chunk_states/pallas_call | solution.py:303
  119.0 14.3 %collective-permute-done.16.refs_0_ = bf16[128,2048]{1,0:T(8,128)(2,1)S(1)} collective-permute-done((bf16[128,2048]{1,0:T(8,128)(2,1)S(1)}, bf16[128,2048]{1,0:T(8,128)(2,1)S(1)}, u32[]{:S(2)}, u32[]{:S(2)}) %collective-permute-start.16) | collective-permute-done | bytes 524320 | tf_op jit(solution)/shard_map/ppermute | solution.py:630
  137.7 3.1 %collective-permute-start.18 = (bf16[128,2048]{1,0:T(8,128)(2,1)S(1)}, bf16[128,2048]{1,0:T(8,128)(2,1)S(1)}, u32[]{:S(2)}, u32[]{:S(2)}) collective-permute-start(bf16[128,2048]{1,0:T(8,128)(2,1)S(1)} %collective-permute-done.16.refs_0_), channel_id=1, source_target_pairs={{0,16},{4,20},{8,24},{12,28},{16,0},{20,4},{24,8},{28,12},{1,17},{... | collective-permute-start | bytes 1572872 | tf_op jit(solution)/shard_map/ppermute | solution.py:633
  141.9 6.2 %collective-permute-done.17.refs_1_ = bf16[128,2048]{1,0:T(8,128)(2,1)S(1)} collective-permute-done((bf16[128,2048]{1,0:T(8,128)(2,1)S(1)}, bf16[128,2048]{1,0:T(8,128)(2,1)S(1)}, u32[]{:S(2)}, u32[]{:S(2)}) %collective-permute-start.17) | collective-permute-done | bytes 524320 | tf_op jit(solution)/shard_map/ppermute | solution.py:633
  149.4 21.3 %collective-permute-done.18.refs_2_ = bf16[128,2048]{1,0:T(8,128)(2,1)S(1)} collective-permute-done((bf16[128,2048]{1,0:T(8,128)(2,1)S(1)}, bf16[128,2048]{1,0:T(8,128)(2,1)S(1)}, u32[]{:S(2)}, u32[]{:S(2)}) %collective-permute-start.18) | collective-permute-done | bytes 524320 | tf_op jit(solution)/shard_map/ppermute | solution.py:633
  172.3 3.1 %placed.3.refs_4_ = bf16[512,2048]{1,0:T(8,128)(2,1)} custom-call(s32[1]{0:T(128)} %bitcast.6.chip_ref, bf16[128,2048]{1,0:T(8,128)(2,1)} %copy-done.6, bf16[128,2048]{1,0:T(8,128)(2,1)} %copy-done.7, bf16[128,2048]{1,0:T(8,128)(2,1)} %copy-done.8, bf16[128,2048]{1,0:T(8,128)(2,1)} %copy-done.10), custom_call_target="tpu_custom_call" | custom-call | tf_op jit(solution)/shard_map/placed/pallas_call | solution.py:615
  178.6 9.6 %collective-permute-done.10 = bf16[144,2048]{1,0:T(8,128)(2,1)S(1)} collective-permute-done((bf16[144,2048]{1,0:T(8,128)(2,1)S(1)}, bf16[144,2048]{1,0:T(8,128)(2,1)S(1)}, u32[]{:S(2)}, u32[]{:S(2)}) %collective-permute-start.10) | collective-permute-done | bytes 589856 | tf_op jit(solution)/shard_map/ppermute | solution.py:554
  188.2 2.4 fusion.5
  192.8 5.7 %column_half.4.refs_1_ = bf16[512,2048]{1,0:T(8,128)(2,1)} custom-call(bf16[512,2048]{1,0:T(8,128)(2,1)} %get-tuple-element.22.refs_2_.refs_0_, bf16[2048,1024]{1,0:T(8,128)(2,1)} %refs_1_.1), custom_call_target="tpu_custom_call" | custom-call | tf_op jit(solution)/shard_map/column_half/pallas_call | solution.py:144
  198.5 10.0 %within_chunk.1.near_ref = bf16[2,512,2048]{2,1,0:T(8,128)(2,1)} custom-call(s32[4]{0:T(128)} %starts_ref.3, s32[1]{0:T(128)} %bitcast.5.base_ref, bf16[512,384]{1,0:T(8,128)(2,1)} %get-tuple-element.20.control_ref, bf16[512,2048]{1,0:T(8,128)(2,1)} %column_half.3.values_ref, f32[1,2048]{1,0:T(1,128)} %broadcast_in_dim_reshape.3.skip_ref, ...), custom_call_target="tpu_custom_call" | custom-call | tf_op jit(solution)/shard_map/within_chunk/pallas_call | solution.py:392
  208.5 5.8 %column_half.5.active_ref = bf16[512,2048]{1,0:T(8,128)(2,1)} custom-call(s32[1]{0:T(128)} %bitcast.2.refs_0_.parity_ref, bf16[512,2048]{1,0:T(8,128)(2,1)} %column_half.4.refs_1_, bf16[512,2048]{1,0:T(8,128)(2,1)} %get-tuple-element.22.refs_2_.refs_0_, bf16[1024,1024]{1,0:T(8,128)(2,1)} %collective-permute-done.12.refs_3_, ...), custom_call_target="tpu_custom_call", output_to_operand_aliasing={{}: (1, {})} | custom-call | tf_op jit(solution)/shard_map/column_half/pallas_call | solution.py:144
  215.1 4.9 %carry_gate.2 = (bf16[2,256,2048]{2,1,0:T(8,128)(2,1)}, f32[8,256]{1,0:T(8,128)}) custom-call(s32[1]{0:T(128)} %bitcast.2.refs_0_.parity_ref, bf16[512,384]{1,0:T(8,128)(2,1)} %get-tuple-element.20.control_ref, bf16[2,512,2048]{2,1,0:T(8,128)(2,1)} %within_chunk.1.near_ref, bf16[128,2048]{1,0:T(8,128)(2,1)} %get-tuple-element.36.through_ref, ...), custom_call_target="tpu_custom_call" | custom-call | tf_op jit(solution)/shard_map/carry_gate/pallas_call | solution.py:438
  222.3 2.4 collective-permute-done.14.refs_1_
  225.3 6.0 %output_project.4 = bf16[256,1024]{1,0:T(8,128)(2,1)} custom-call(s32[3]{0:T(128)} %add_add_fusion.place_ref, bf16[2,256,2048]{2,1,0:T(8,128)(2,1)} %get-tuple-element.31.gated_ref, f32[8,256]{1,0:T(8,128)} %get-tuple-element.32.refs_0_, f32[8,256]{1,0:T(8,128)} %copy-done.14, f32[1,2048]{1,0:T(1,128)} %bitcast.19, bf16[1024,2048]{1,0:T(8,128)(2,1)} %refs_3_.7, ...), custom_call_target="tpu_custom_call" | custom-call | tf_op jit(solution)/shard_map/output_project/pallas_call | solution.py:520
  233.1 6.0 %output_project.5 = bf16[256,1024]{1,0:T(8,128)(2,1)} custom-call(s32[3]{0:T(128)} %add_add_fusion.1.place_ref, bf16[2,256,2048]{2,1,0:T(8,128)(2,1)} %get-tuple-element.31.gated_ref, f32[8,256]{1,0:T(8,128)} %get-tuple-element.32.refs_0_, f32[8,256]{1,0:T(8,128)} %copy-done.14, f32[1,2048]{1,0:T(1,128)} %bitcast.20, bf16[1024,2048]{1,0:T(8,128)(2,1)} %refs_3_.7, ...), custom_call_target="tpu_custom_call" | custom-call | tf_op jit(solution)/shard_map/output_project/pallas_call | solution.py:520
  239.1 4.3 %collective-permute-start.22 = (bf16[256,1024]{1,0:T(8,128)(2,1)}, bf16[256,1024]{1,0:T(8,128)(2,1)S(1)}, u32[]{:S(2)}, u32[]{:S(2)}) collective-permute-start(bf16[256,1024]{1,0:T(8,128)(2,1)} %output_project.5), channel_id=1, source_target_pairs={{1,2},{2,1},{5,6},{6,5},{9,10},{10,9},{13,14},{14,13},{17,18},{18,... | collective-permute-start | bytes 1572872 | tf_op jit(solution)/shard_map/ppermute | solution.py:713
  243.4 4.9 %carry_gate.3 = (bf16[2,256,2048]{2,1,0:T(8,128)(2,1)}, f32[8,256]{1,0:T(8,128)}) custom-call(s32[1]{0:T(128)} %bitcast.2.refs_0_.parity_ref, bf16[512,384]{1,0:T(8,128)(2,1)} %get-tuple-element.20.control_ref, bf16[2,512,2048]{2,1,0:T(8,128)(2,1)} %within_chunk.1.near_ref, bf16[128,2048]{1,0:T(8,128)(2,1)} %get-tuple-element.36.through_ref, ...), custom_call_target="tpu_custom_call" | custom-call | tf_op jit(solution)/shard_map/carry_gate/pallas_call | solution.py:438
  248.4 7.0 %collective-permute-done.23.refs_1_ = f32[8,256]{1,0:T(8,128)S(1)} collective-permute-done((f32[8,256]{1,0:T(8,128)}, f32[8,256]{1,0:T(8,128)S(1)}, u32[]{:S(2)}, u32[]{:S(2)}) %collective-permute-start.23) | collective-permute-done | bytes 8224 | tf_op jit(solution)/shard_map/ppermute | solution.py:565
  255.9 6.0 %output_project.6 = bf16[256,1024]{1,0:T(8,128)(2,1)} custom-call(s32[3]{0:T(128)} %add_add_fusion.place_ref, bf16[2,256,2048]{2,1,0:T(8,128)(2,1)} %get-tuple-element.33.gated_ref, f32[8,256]{1,0:T(8,128)} %get-tuple-element.34.refs_0_, f32[8,256]{1,0:T(8,128)} %copy-done.15, f32[1,2048]{1,0:T(1,128)} %bitcast.21, bf16[1024,2048]{1,0:T(8,128)(2,1)} %refs_3_.7, ...), custom_call_target="tpu_custom_call" | custom-call | tf_op jit(solution)/shard_map/output_project/pallas_call | solution.py:520
  262.0 3.4 %collective-permute-start.24 = (bf16[256,1024]{1,0:T(8,128)(2,1)}, bf16[256,1024]{1,0:T(8,128)(2,1)}, u32[]{:S(2)}, u32[]{:S(2)}) collective-permute-start(bf16[256,1024]{1,0:T(8,128)(2,1)} %output_project.6), channel_id=1, source_target_pairs={{0,1},{1,3},{2,0},{3,2},{4,5},{5,7},{6,4},{7,6},{8,9},{9,11},{10,8... | collective-permute-start | bytes 1572872 | tf_op jit(solution)/shard_map/ppermute | solution.py:713
  265.4 6.0 %output_project.7 = bf16[256,1024]{1,0:T(8,128)(2,1)} custom-call(s32[3]{0:T(128)} %add_add_fusion.1.place_ref, bf16[2,256,2048]{2,1,0:T(8,128)(2,1)} %get-tuple-element.33.gated_ref, f32[8,256]{1,0:T(8,128)} %get-tuple-element.34.refs_0_, f32[8,256]{1,0:T(8,128)} %copy-done.15, f32[1,2048]{1,0:T(1,128)} %bitcast.22, bf16[1024,2048]{1,0:T(8,128)(2,1)} %refs_3_.7, ...), custom_call_target="tpu_custom_call" | custom-call | tf_op jit(solution)/shard_map/output_project/pallas_call | solution.py:520
  271.4 4.9 %collective-permute-start.25 = (bf16[256,1024]{1,0:T(8,128)(2,1)}, bf16[256,1024]{1,0:T(8,128)(2,1)}, u32[]{:S(2)}, u32[]{:S(2)}) collective-permute-start(bf16[256,1024]{1,0:T(8,128)(2,1)} %output_project.7), channel_id=1, source_target_pairs={{1,2},{2,1},{5,6},{6,5},{9,10},{10,9},{13,14},{14,13},{17,18},{18,... | collective-permute-start | bytes 1572872 | tf_op jit(solution)/shard_map/ppermute | solution.py:713
  277.0 12.1 %collective-permute-done.25 = bf16[256,1024]{1,0:T(8,128)(2,1)} collective-permute-done((bf16[256,1024]{1,0:T(8,128)(2,1)}, bf16[256,1024]{1,0:T(8,128)(2,1)}, u32[]{:S(2)}, u32[]{:S(2)}) %collective-permute-start.25) | collective-permute-done | bytes 524320 | tf_op jit(solution)/shard_map/ppermute | solution.py:713
  (109 shorter events, 38.9 us)
Async XLA Ops:
  1.1 13.7 %collective-permute-start.2 = (bf16[256,1024]{1,0:T(8,128)(2,1)S(1)}, bf16[256,1024]{1,0:T(8,128)(2,1)S(1)}, u32[]{:S(2)}, u32[]{:S(2)}) collective-permute-start(bf16[256,1024]{1,0:T(8,128)(2,1)S(1)} %constant_dynamic-slice_fusion.2), channel_id=1, source_target_pairs={{0,1},{1,0},{2,3},{3,2},{4,5},{5,4},{6,7},{7,6},{8,9},{9,8},{10,11... | collective-permute-start | bytes 1572872 | tf_op jit(solution)/shard_map/ppermute | solution.py:630
  14.8 25.3 %copy-start.9 = (bf16[256,1024]{1,0:T(8,128)(2,1)}, bf16[256,1024]{1,0:T(8,128)(2,1)S(1)}, u32[]{:S(2)}) copy-start(bf16[256,1024]{1,0:T(8,128)(2,1)S(1)} %collective-permute-done.2.refs_0_) | copy-start | bytes 1572868
  14.8 14.8 %collective-permute-start.3 = (bf16[256,1024]{1,0:T(8,128)(2,1)S(1)}, bf16[256,1024]{1,0:T(8,128)(2,1)S(1)}, u32[]{:S(2)}, u32[]{:S(2)}) collective-permute-start(bf16[256,1024]{1,0:T(8,128)(2,1)S(1)} %collective-permute-done.2.refs_0_), channel_id=1, source_target_pairs={{0,8},{4,12},{8,0},{12,4},{16,24},{20,28},{24,16},{28,20},{1,9},{5... | collective-permute-start | bytes 1572872 | tf_op jit(solution)/shard_map/ppermute | solution.py:633
  16.3 23.8 %collective-permute-start.4 = (bf16[256,1024]{1,0:T(8,128)(2,1)S(1)}, bf16[256,1024]{1,0:T(8,128)(2,1)S(1)}, u32[]{:S(2)}, u32[]{:S(2)}) collective-permute-start(bf16[256,1024]{1,0:T(8,128)(2,1)S(1)} %collective-permute-done.2.refs_0_), channel_id=1, source_target_pairs={{0,16},{4,20},{8,24},{12,28},{16,0},{20,4},{24,8},{28,12},{1,17},{... | collective-permute-start | bytes 1572872 | tf_op jit(solution)/shard_map/ppermute | solution.py:633
  17.8 22.2 %collective-permute-start.5 = (bf16[256,1024]{1,0:T(8,128)(2,1)S(1)}, bf16[256,1024]{1,0:T(8,128)(2,1)S(1)}, u32[]{:S(2)}, u32[]{:S(2)}) collective-permute-start(bf16[256,1024]{1,0:T(8,128)(2,1)S(1)} %collective-permute-done.2.refs_0_), channel_id=1, source_target_pairs={{0,24},{4,28},{8,16},{12,20},{16,8},{20,12},{24,0},{28,4},{1,25},{... | collective-permute-start | bytes 1572872 | tf_op jit(solution)/shard_map/ppermute | solution.py:633
  44.0 59.6 %collective-permute-start.6 = (bf16[1024,1024]{1,0:T(8,128)(2,1)}, bf16[1024,1024]{1,0:T(8,128)(2,1)}, u32[]{:S(2)}, u32[]{:S(2)}) collective-permute-start(bf16[1024,1024]{1,0:T(8,128)(2,1)} %placed.2.refs_3_), channel_id=1, source_target_pairs={{0,4},{4,0},{8,12},{12,8},{16,20},{20,16},{24,28},{28,24},{1,5},{5... | collective-permute-start | bytes 6291464 | tf_op jit(solution)/shard_map/ppermute | solution.py:635
  44.0 50.2 %collective-permute-start = (bf16[512,1024]{1,0:T(8,128)(2,1)}, bf16[512,1024]{1,0:T(8,128)(2,1)}, u32[]{:S(2)}, u32[]{:S(2)}) collective-permute-start(bf16[512,1024]{1,0:T(8,128)(2,1)} %refs_0_.1), channel_id=1, source_target_pairs={{2,1},{1,2},{6,5},{5,6},{10,9},{9,10},{14,13},{13,14},{18,17},{17,... | collective-permute-start | bytes 3145736 | tf_op jit(solution)/shard_map/ppermute | solution.py:594
  46.4 47.9 %collective-permute-start.1 = (bf16[512,1024]{1,0:T(8,128)(2,1)}, bf16[512,1024]{1,0:T(8,128)(2,1)}, u32[]{:S(2)}, u32[]{:S(2)}) collective-permute-start(bf16[512,1024]{1,0:T(8,128)(2,1)} %refs_0_.1), channel_id=1, source_target_pairs={{1,0},{3,1},{0,2},{2,3},{5,4},{7,5},{4,6},{6,7},{9,8},{11,9},{8,10... | collective-permute-start | bytes 3145736 | tf_op jit(solution)/shard_map/ppermute | solution.py:594
  50.4 91.4 %collective-permute-start.12 = (bf16[1024,1024]{1,0:T(8,128)(2,1)}, bf16[1024,1024]{1,0:T(8,128)(2,1)}, u32[]{:S(2)}, u32[]{:S(2)}) collective-permute-start(bf16[1024,1024]{1,0:T(8,128)(2,1)} %constant_dynamic-slice_fusion.1), channel_id=1, source_target_pairs={{0,1},{1,0},{2,3},{3,2},{4,5},{5,4},{6,7},{7,6},{8,9},{9,8},{10,11... | collective-permute-start | bytes 6291464 | tf_op jit(solution)/shard_map/ppermute | solution.py:643
  117.8 16.5 %collective-permute-start.7 = (bf16[144,2048]{1,0:T(8,128)(2,1)}, bf16[144,2048]{1,0:T(8,128)(2,1)S(1)}, u32[]{:S(2)}, u32[]{:S(2)}) collective-permute-start(bf16[144,2048]{1,0:T(8,128)(2,1)} %get-tuple-element.28), channel_id=1, source_target_pairs={{0,4},{4,0},{8,12},{12,8},{16,20},{20,16},{24,28},{28,24},{1,5},{5... | collective-permute-start | bytes 1769480 | tf_op jit(solution)/shard_map/ppermute | solution.py:542
  118.9 14.4 %collective-permute-start.16 = (bf16[128,2048]{1,0:T(8,128)(2,1)S(1)}, bf16[128,2048]{1,0:T(8,128)(2,1)S(1)}, u32[]{:S(2)}, u32[]{:S(2)}) collective-permute-start(bf16[128,2048]{1,0:T(8,128)(2,1)S(1)} %constant_dynamic-slice_fusion), channel_id=1, source_target_pairs={{0,1},{1,0},{2,3},{3,2},{4,5},{5,4},{6,7},{7,6},{8,9},{9,8},{10,11... | collective-permute-start | bytes 1572872 | tf_op jit(solution)/shard_map/ppermute | solution.py:630
  133.3 37.4 %copy-start.6 = (bf16[128,2048]{1,0:T(8,128)(2,1)}, bf16[128,2048]{1,0:T(8,128)(2,1)S(1)}, u32[]{:S(2)}) copy-start(bf16[128,2048]{1,0:T(8,128)(2,1)S(1)} %collective-permute-done.16.refs_0_) | copy-start | bytes 1572868
  133.3 14.8 %collective-permute-start.17 = (bf16[128,2048]{1,0:T(8,128)(2,1)S(1)}, bf16[128,2048]{1,0:T(8,128)(2,1)S(1)}, u32[]{:S(2)}, u32[]{:S(2)}) collective-permute-start(bf16[128,2048]{1,0:T(8,128)(2,1)S(1)} %collective-permute-done.16.refs_0_), channel_id=1, source_target_pairs={{0,8},{4,12},{8,0},{12,4},{16,24},{20,28},{24,16},{28,20},{1,9},{5... | collective-permute-start | bytes 1572872 | tf_op jit(solution)/shard_map/ppermute | solution.py:633
  136.4 40.6 %collective-permute-start.8 = (bf16[144,2048]{1,0:T(8,128)(2,1)S(1)}, bf16[144,2048]{1,0:T(8,128)(2,1)}, u32[]{:S(2)}, u32[]{:S(2)}) collective-permute-start(bf16[144,2048]{1,0:T(8,128)(2,1)S(1)} %pad_maximum_fusion.1), channel_id=1, source_target_pairs={{4,12},{12,20},{20,28},{8,0},{16,8},{24,16},{5,13},{13,21},{21,29}... | collective-permute-start | bytes 1769480 | tf_op jit(solution)/shard_map/ppermute | solution.py:554
  137.7 33.0 %collective-permute-start.18 = (bf16[128,2048]{1,0:T(8,128)(2,1)S(1)}, bf16[128,2048]{1,0:T(8,128)(2,1)S(1)}, u32[]{:S(2)}, u32[]{:S(2)}) collective-permute-start(bf16[128,2048]{1,0:T(8,128)(2,1)S(1)} %collective-permute-done.16.refs_0_), channel_id=1, source_target_pairs={{0,16},{4,20},{8,24},{12,28},{16,0},{20,4},{24,8},{28,12},{1,17},{... | collective-permute-start | bytes 1572872 | tf_op jit(solution)/shard_map/ppermute | solution.py:633
  140.8 29.9 %collective-permute-start.19 = (bf16[128,2048]{1,0:T(8,128)(2,1)S(1)}, bf16[128,2048]{1,0:T(8,128)(2,1)S(1)}, u32[]{:S(2)}, u32[]{:S(2)}) collective-permute-start(bf16[128,2048]{1,0:T(8,128)(2,1)S(1)} %collective-permute-done.16.refs_0_), channel_id=1, source_target_pairs={{0,24},{4,28},{8,16},{12,20},{16,8},{20,12},{24,0},{28,4},{1,25},{... | collective-permute-start | bytes 1572872 | tf_op jit(solution)/shard_map/ppermute | solution.py:633
  141.9 66.6 %collective-permute-start.13 = (bf16[1024,1024]{1,0:T(8,128)(2,1)}, bf16[1024,1024]{1,0:T(8,128)(2,1)}, u32[]{:S(2)}, u32[]{:S(2)}) collective-permute-start(bf16[1024,1024]{1,0:T(8,128)(2,1)} %collective-permute-done.12.refs_3_), channel_id=1, source_target_pairs={{0,4},{4,0},{8,12},{12,8},{16,20},{20,16},{24,28},{28,24},{1,5},{5... | collective-permute-start | bytes 6291464 | tf_op jit(solution)/shard_map/ppermute | solution.py:644
  148.1 22.6 %copy-start.7 = (bf16[128,2048]{1,0:T(8,128)(2,1)}, bf16[128,2048]{1,0:T(8,128)(2,1)S(1)}, u32[]{:S(2)}) copy-start(bf16[128,2048]{1,0:T(8,128)(2,1)S(1)} %collective-permute-done.17.refs_1_) | copy-start | bytes 1572868
  148.1 29.7 %collective-permute-start.9 = (bf16[144,2048]{1,0:T(8,128)(2,1)S(1)}, bf16[144,2048]{1,0:T(8,128)(2,1)}, u32[]{:S(2)}, u32[]{:S(2)}) collective-permute-start(bf16[144,2048]{1,0:T(8,128)(2,1)S(1)} %pad_maximum_fusion.1), channel_id=1, source_target_pairs={{4,20},{12,28},{16,0},{24,8},{5,21},{13,29},{17,1},{25,9},{6,22},{... | collective-permute-start | bytes 1769480 | tf_op jit(solution)/shard_map/ppermute | solution.py:554
  175.4 15.2 %copy-start.16 = (f32[1024]{0:T(1024)S(1)}, f32[1024]{0:T(1024)}, u32[]{:S(2)}) copy-start(f32[1024]{0:T(1024)} %param.19) | copy-start | bytes 12292
  175.4 46.9 %collective-permute-start.20 = (bf16[512,2048]{1,0:T(8,128)(2,1)}, bf16[512,2048]{1,0:T(8,128)(2,1)S(1)}, u32[]{:S(2)}, u32[]{:S(2)}) collective-permute-start(bf16[512,2048]{1,0:T(8,128)(2,1)} %placed.3.refs_4_), channel_id=1, source_target_pairs={{0,4},{4,0},{8,12},{12,8},{16,20},{20,16},{24,28},{28,24},{1,5},{5... | collective-permute-start | bytes 6291464 | tf_op jit(solution)/shard_map/ppermute | solution.py:635
  175.4 12.8 %collective-permute-start.10 = (bf16[144,2048]{1,0:T(8,128)(2,1)S(1)}, bf16[144,2048]{1,0:T(8,128)(2,1)S(1)}, u32[]{:S(2)}, u32[]{:S(2)}) collective-permute-start(bf16[144,2048]{1,0:T(8,128)(2,1)S(1)} %pad_maximum_fusion.1), channel_id=1, source_target_pairs={{4,28},{24,0},{5,29},{25,1},{6,30},{26,2},{7,31},{27,3}} | collective-permute-start | bytes 1769480 | tf_op jit(solution)/shard_map/ppermute | solution.py:554
  190.6 23.7 %collective-permute-start.11 = (bf16[128,2048]{1,0:T(8,128)(2,1)S(1)}, bf16[128,2048]{1,0:T(8,128)(2,1)S(1)}, u32[]{:S(2)}, u32[]{:S(2)}) collective-permute-start(bf16[128,2048]{1,0:T(8,128)(2,1)S(1)} %get-tuple-element.35), channel_id=1, source_target_pairs={{0,4},{4,0},{8,12},{12,8},{16,20},{20,16},{24,28},{28,24},{1,5},{5... | collective-permute-start | bytes 1572872 | tf_op jit(solution)/shard_map/ppermute | solution.py:557
  190.6 31.1 %collective-permute-start.15 = (f32[1024]{0:T(1024)S(1)}, f32[1024]{0:T(1024)S(1)}, u32[]{:S(2)}, u32[]{:S(2)}) collective-permute-start(f32[1024]{0:T(1024)S(1)} %copy-done.16), channel_id=1, source_target_pairs={{0,1},{1,0},{2,3},{3,2},{4,5},{5,4},{6,7},{7,6},{8,9},{9,8},{10,11... | collective-permute-start | bytes 12296 | tf_op jit(solution)/shard_map/ppermute | solution.py:674
  220.0 4.8 %collective-permute-start.14 = (f32[8,256]{1,0:T(8,128)}, f32[8,256]{1,0:T(8,128)S(1)}, u32[]{:S(2)}, u32[]{:S(2)}) collective-permute-start(f32[8,256]{1,0:T(8,128)} %get-tuple-element.32.refs_0_), channel_id=1, source_target_pairs={{0,2},{1,3},{2,0},{3,1},{4,6},{5,7},{6,4},{7,5},{8,10},{9,11},{10,... | collective-permute-start | bytes 24584 | tf_op jit(solution)/shard_map/ppermute | solution.py:565
  231.3 44.9 %collective-permute-start.21 = (bf16[256,1024]{1,0:T(8,128)(2,1)}, bf16[256,1024]{1,0:T(8,128)(2,1)S(1)}, u32[]{:S(2)}, u32[]{:S(2)}) collective-permute-start(bf16[256,1024]{1,0:T(8,128)(2,1)} %output_project.4), channel_id=1, source_target_pairs={{0,1},{1,3},{2,0},{3,2},{4,5},{5,7},{6,4},{7,6},{8,9},{9,11},{10,8... | collective-permute-start | bytes 1572872 | tf_op jit(solution)/shard_map/ppermute | solution.py:713
  239.1 37.2 %collective-permute-start.22 = (bf16[256,1024]{1,0:T(8,128)(2,1)}, bf16[256,1024]{1,0:T(8,128)(2,1)S(1)}, u32[]{:S(2)}, u32[]{:S(2)}) collective-permute-start(bf16[256,1024]{1,0:T(8,128)(2,1)} %output_project.5), channel_id=1, source_target_pairs={{1,2},{2,1},{5,6},{6,5},{9,10},{10,9},{13,14},{14,13},{17,18},{18,... | collective-permute-start | bytes 1572872 | tf_op jit(solution)/shard_map/ppermute | solution.py:713
  248.4 7.0 %collective-permute-start.23 = (f32[8,256]{1,0:T(8,128)}, f32[8,256]{1,0:T(8,128)S(1)}, u32[]{:S(2)}, u32[]{:S(2)}) collective-permute-start(f32[8,256]{1,0:T(8,128)} %get-tuple-element.34.refs_0_), channel_id=1, source_target_pairs={{0,2},{1,3},{2,0},{3,1},{4,6},{5,7},{6,4},{7,5},{8,10},{9,11},{10,... | collective-permute-start | bytes 24584 | tf_op jit(solution)/shard_map/ppermute | solution.py:565
  262.0 15.0 %collective-permute-start.24 = (bf16[256,1024]{1,0:T(8,128)(2,1)}, bf16[256,1024]{1,0:T(8,128)(2,1)}, u32[]{:S(2)}, u32[]{:S(2)}) collective-permute-start(bf16[256,1024]{1,0:T(8,128)(2,1)} %output_project.6), channel_id=1, source_target_pairs={{0,1},{1,3},{2,0},{3,2},{4,5},{5,7},{6,4},{7,6},{8,9},{9,11},{10,8... | collective-permute-start | bytes 1572872 | tf_op jit(solution)/shard_map/ppermute | solution.py:713
  271.4 17.7 %copy-start.4 = (bf16[256,1024]{1,0:T(8,128)(2,1)S(1)}, bf16[256,1024]{1,0:T(8,128)(2,1)}, u32[]{:S(2)}) copy-start(bf16[256,1024]{1,0:T(8,128)(2,1)} %output_project.6) | copy-start | bytes 1572868
  271.4 17.7 %copy-start.5 = (bf16[256,1024]{1,0:T(8,128)(2,1)S(1)}, bf16[256,1024]{1,0:T(8,128)(2,1)}, u32[]{:S(2)}) copy-start(bf16[256,1024]{1,0:T(8,128)(2,1)} %output_project.7) | copy-start | bytes 1572868
  271.4 17.7 %collective-permute-start.25 = (bf16[256,1024]{1,0:T(8,128)(2,1)}, bf16[256,1024]{1,0:T(8,128)(2,1)}, u32[]{:S(2)}, u32[]{:S(2)}) collective-permute-start(bf16[256,1024]{1,0:T(8,128)(2,1)} %output_project.7), channel_id=1, source_target_pairs={{1,2},{2,1},{5,6},{6,5},{9,10},{10,9},{13,14},{14,13},{17,18},{18,... | collective-permute-start | bytes 1572872 | tf_op jit(solution)/shard_map/ppermute | solution.py:713
  (16 other events, 54.6 us)
